TPU v7x, 32 devices: a whole 2x2x4 slice. The times are simulated.
32 devices in a mesh: ctx: 8 (over y, x, core), fsdp: 4 (over z).
Axes of the slice: x: 2, y: 2, z: 4, core: 2. Of those that a mesh axis runs over, the one named last changes fastest.
Arguments:
- tokens: bfloat16 [2, 4, 1536, 768], P(None, 'fsdp', 'ctx'), may hold values from -6 to 6
- doc_ids: int32 [2, 4, 1536], P(None, 'fsdp', 'ctx'), may hold values from 0 to 4, as said below
- keep_mask: int32 [2, 4, 4], P(None, 'fsdp'), may hold values 0 or 1
- qkv_weight: bfloat16 [768, 2304], P('fsdp'), may hold values from -0.3125 to 0.3125
- query_bias: bfloat16 [768], P('fsdp'), may hold values from -3 to 3
- value_bias: bfloat16 [768], P('fsdp'), may hold values from -0.29882812 to 0.29882812
- proj_weight: bfloat16 [768, 768], P('fsdp'), may hold values from -1.25 to 1.25
- proj_bias: bfloat16 [768], P('fsdp'), may hold values from -2 to 2
- norm1_gain: bfloat16 [768], P('fsdp'), may hold values from 0.5 to 1.5
- norm1_bias: bfloat16 [768], P('fsdp'), may hold values from -3 to 3
- up_weight: bfloat16 [768, 3072], P('fsdp'), may hold values from -0.21875 to 0.21875
- up_bias: bfloat16 [3072], P('fsdp'), may hold values from -3 to 3
- down_weight: bfloat16 [3072, 768], P('fsdp'), may hold values from -0.109375 to 0.109375
- down_bias: bfloat16 [768], P('fsdp'), may hold values from -3 to 3
- norm2_gain: bfloat16 [768], P('fsdp'), may hold values from 0.5 to 1.5
- norm2_bias: bfloat16 [768], P('fsdp'), may hold values from -3 to 3
- cotangent: bfloat16 [2, 4, 1536, 768], P(None, 'fsdp', 'ctx'), may hold values from -6 to 6
Outputs:
- block_out: bfloat16 [2, 4, 1536, 768], P(None, 'fsdp', 'ctx')
- grad_tokens: float32 [2, 4, 1536, 768], P(None, 'fsdp', 'ctx')
- grad_qkv: float32 [768, 2304], P(('ctx', 'fsdp'))
- grad_query_bias: float32 [768], P(('ctx', 'fsdp'))
- grad_value_bias: float32 [768], P(('ctx', 'fsdp'))
- grad_proj: float32 [768, 768], P(('ctx', 'fsdp'))
- grad_proj_bias: float32 [768], P(('ctx', 'fsdp'))
- grad_gain1: float32 [768], P(('ctx', 'fsdp'))
- grad_bias1: float32 [768], P(('ctx', 'fsdp'))
- grad_up: float32 [768, 3072], P(('ctx', 'fsdp'))
- grad_up_bias: float32 [3072], P(('ctx', 'fsdp'))
- grad_down: float32 [3072, 768], P(('ctx', 'fsdp'))
- grad_down_bias: float32 [768], P(('ctx', 'fsdp'))
- grad_gain2: float32 [768], P(('ctx', 'fsdp'))
- grad_bias2: float32 [768], P(('ctx', 'fsdp'))
Inputs may be any that keep to these rules, and one draw needn't show every extreme that they name: `doc_ids`: within a pool, ids 0 to 3 name documents and id 4 marks empty slots; one document has exactly 1024 slots, every other at least one, 1344 slots hold documents. The pool's slots are made of blocks of 48 consecutive slots, each holding consecutive positions of the packed documents, in an order drawn from the seed.
All inputs are finite; a program needn't handle non-finite values. No bound on the sum of `keep_mask` on one device may be relied on, other than what follows from the above.
Results may differ from a plain program's by a relative error of at most 0.025.
Values may be sent and summed in bfloat16 or wider, within the bound.
No kernel may reach another device: no remote copies, remote signals or barrier semaphores. Data moves between devices by JAX's collectives and lax.ppermute only.
A program may use at most 192 MiB of HBM per device.

v0:
```python
import math

import jax
import jax.numpy as jnp
from jax import lax
from jax.sharding import PartitionSpec as P

H = 12
NDOC = 4


epsilon = 1e-05
score_scale = 0.125
masked_score = -1e30


def layer_norm(values, gain_vec, offset_vec):
    centre = jnp.mean(values, axis=-1, keepdims=True)
    centred = values - centre
    spread = jnp.mean(centred * centred, axis=-1, keepdims=True)
    return centred * lax.rsqrt(spread + epsilon) * gain_vec + offset_vec


def exact_gelu(values):
    return jax.nn.gelu(values, approximate=False)


def in_blocks(stepper, carried, portion, shard_rows):
    total_rows = portion[0].shape[0]
    shard_count = total_rows // shard_rows
    limit_rows = max(1, 1024 // shard_rows)
    grouped = math.gcd(shard_count, 1 << limit_rows.bit_length() - 1)
    block_rows = grouped * shard_rows
    turn_count = total_rows // block_rows
    stacked = tuple(
        (member.reshape((turn_count, block_rows) + member.shape[1:]) for member in portion)
    )
    offsets = block_rows * jnp.arange(turn_count, dtype=jnp.int32)

    def one_turn(inner_state, element):
        return (stepper(inner_state, element[0], element[1]), None)

    carried, ignored = lax.scan(one_turn, carried, (stacked, offsets))
    return carried


def micro_step(token_rows, slot_ids, keep_flags, weights_full, grad_rows):
    (
        qkv_weight,
        query_bias,
        value_bias,
        proj_weight,
        proj_bias,
        norm1_gain,
        norm1_bias,
        up_weight,
        up_bias,
        down_weight,
        down_bias,
        norm2_gain,
        norm2_bias,
    ) = weights_full
    local_rows, features = token_rows.shape
    num_heads = H
    head_size = features // num_heads
    documents = jnp.arange(NDOC, dtype=jnp.int32)
    keep_rows = jnp.sum(
        jnp.where(slot_ids[:, None] == documents[None, :], keep_flags[None, :], 0), axis=1
    ).astype(jnp.float32)[:, None]
    token_float = token_rows.astype(jnp.float32)
    slot_labels = slot_ids.astype(jnp.float32).astype(jnp.bfloat16)
    projected = jnp.dot(token_rows, qkv_weight, preferred_element_type=jnp.float32)
    query_rows = (projected[:, :features] + query_bias.astype(jnp.float32)).astype(jnp.bfloat16)
    key_rows = projected[:, features : 2 * features].astype(jnp.bfloat16)
    value_rows = (projected[:, 2 * features :] + value_bias.astype(jnp.float32)).astype(
        jnp.bfloat16
    )
    query_heads = query_rows.reshape(local_rows, num_heads, head_size)
    key_heads_local = key_rows.reshape(local_rows, num_heads, head_size)
    value_heads_local = value_rows.reshape(local_rows, num_heads, head_size)

    def forward_step(carried, portion, offset):
        key_part, value_part, id_part = portion
        running_max, running_sum, running_out = carried
        scores = (
            jnp.einsum(
                "qhd,khd->hqk",
                query_heads,
                key_part.reshape(-1, num_heads, head_size),
                preferred_element_type=jnp.float32,
            )
            * score_scale
        )
        same_doc = (slot_labels[:, None] == id_part[None, :])[None]
        scores = jnp.where(same_doc, scores, masked_score)
        new_max = jnp.maximum(running_max, jnp.max(scores, axis=-1))
        factor = jnp.exp(running_max - new_max)
        weights = jnp.where(same_doc, jnp.exp(scores - new_max[..., None]), 0.0)
        running_sum = running_sum * factor + jnp.sum(weights, axis=-1)
        running_out = running_out * factor[..., None] + jnp.einsum(
            "hqk,khd->hqd",
            weights.astype(jnp.bfloat16),
            value_part.reshape(-1, num_heads, head_size),
            preferred_element_type=jnp.float32,
        )
        return (new_max, running_sum, running_out)

    start_state = (
        jnp.full((num_heads, local_rows), masked_score, jnp.float32),
        jnp.zeros((num_heads, local_rows), jnp.float32),
        jnp.zeros((num_heads, local_rows, head_size), jnp.float32),
    )
    running_max, running_sum, running_out = in_blocks(
        forward_step,
        start_state,
        (
            lax.all_gather(key_rows, "ctx", axis=0, tiled=True),
            lax.all_gather(value_rows, "ctx", axis=0, tiled=True),
            lax.all_gather(slot_labels, "ctx", axis=0, tiled=True),
        ),
        local_rows,
    )
    attended = jnp.transpose(running_out / running_sum[..., None], (1, 0, 2))
    log_total = running_max + jnp.log(running_sum)
    attended_low = attended.reshape(local_rows, features).astype(jnp.bfloat16)
    projection = jnp.dot(
        attended_low, proj_weight, preferred_element_type=jnp.float32
    ) + proj_bias.astype(jnp.float32)
    hidden, norm1_back = jax.vjp(
        layer_norm,
        token_float + projection,
        norm1_gain.astype(jnp.float32),
        norm1_bias.astype(jnp.float32),
    )
    hidden_low = hidden.astype(jnp.bfloat16)
    inner_rows = jnp.dot(
        hidden_low, up_weight, preferred_element_type=jnp.float32
    ) + up_bias.astype(jnp.float32)
    active, gelu_back = jax.vjp(exact_gelu, inner_rows)
    active_low = active.astype(jnp.bfloat16)
    branch = jnp.dot(
        active_low, down_weight, preferred_element_type=jnp.float32
    ) + down_bias.astype(jnp.float32)
    result, norm2_back = jax.vjp(
        layer_norm, hidden + branch, norm2_gain.astype(jnp.float32), norm2_bias.astype(jnp.float32)
    )
    block_rows = (keep_rows * result + (1.0 - keep_rows) * token_float).astype(jnp.bfloat16)
    grad_float = grad_rows.astype(jnp.float32)
    grad_sum, grad_gain2, grad_bias2 = norm2_back(keep_rows * grad_float)
    grad_branch = grad_sum.astype(jnp.bfloat16)
    grad_down = jnp.einsum("rf,rd->fd", active_low, grad_branch, preferred_element_type=jnp.float32)
    grad_down_bias = jnp.sum(grad_branch.astype(jnp.float32), axis=0)
    (grad_inner,) = gelu_back(
        jnp.einsum("rd,fd->rf", grad_branch, down_weight, preferred_element_type=jnp.float32)
    )
    grad_inner_low = grad_inner.astype(jnp.bfloat16)
    grad_up = jnp.einsum(
        "rd,rf->df", hidden_low, grad_inner_low, preferred_element_type=jnp.float32
    )
    grad_up_bias = jnp.sum(grad_inner_low.astype(jnp.float32), axis=0)
    grad_hidden = grad_sum + jnp.einsum(
        "rf,df->rd", grad_inner_low, up_weight, preferred_element_type=jnp.float32
    )
    grad_mixed, grad_gain1, grad_bias1 = norm1_back(grad_hidden)
    grad_proj_low = grad_mixed.astype(jnp.bfloat16)
    grad_proj = jnp.einsum(
        "re,rd->ed", attended_low, grad_proj_low, preferred_element_type=jnp.float32
    )
    grad_proj_bias = jnp.sum(grad_proj_low.astype(jnp.float32), axis=0)
    grad_attended = jnp.einsum(
        "rd,ed->re", grad_proj_low, proj_weight, preferred_element_type=jnp.float32
    ).astype(jnp.bfloat16)
    grad_heads = grad_attended.reshape(local_rows, num_heads, head_size)
    row_delta = jnp.transpose(jnp.sum(grad_heads.astype(jnp.float32) * attended, axis=-1))

    def query_step(carried, portion, offset):
        key_part, value_part, id_part = portion
        key_heads = key_part.reshape(-1, num_heads, head_size)
        scores = (
            jnp.einsum("qhd,khd->hqk", query_heads, key_heads, preferred_element_type=jnp.float32)
            * score_scale
        )
        same_doc = (slot_labels[:, None] == id_part[None, :])[None]
        scores = jnp.where(same_doc, scores, masked_score)
        probs = jnp.where(same_doc, jnp.exp(scores - log_total[..., None]), 0.0)
        grad_probs = jnp.einsum(
            "qhd,khd->hqk",
            grad_heads,
            value_part.reshape(-1, num_heads, head_size),
            preferred_element_type=jnp.float32,
        )
        grad_scores = (probs * (grad_probs - row_delta[..., None])).astype(jnp.bfloat16)
        return carried + jnp.einsum(
            "hqk,khd->qhd", grad_scores, key_heads, preferred_element_type=jnp.float32
        )

    grad_query_sum = in_blocks(
        query_step,
        jnp.zeros((local_rows, num_heads, head_size), jnp.float32),
        (
            lax.all_gather(key_rows, "ctx", axis=0, tiled=True),
            lax.all_gather(value_rows, "ctx", axis=0, tiled=True),
            lax.all_gather(slot_labels, "ctx", axis=0, tiled=True),
        ),
        local_rows,
    )
    log_rows, delta_rows = (
        lax.all_gather(jnp.transpose(log_total), "ctx", axis=0, tiled=True),
        lax.all_gather(jnp.transpose(row_delta), "ctx", axis=0, tiled=True),
    )

    def key_step(carried, portion, offset):
        query_part, grad_part, id_part = portion
        grad_key_sum, grad_value_sum = carried
        span_rows = query_part.shape[0]
        log_part = lax.dynamic_slice_in_dim(log_rows, offset, span_rows, 0)
        delta_part = lax.dynamic_slice_in_dim(delta_rows, offset, span_rows, 0)
        query_part_heads = query_part.reshape(-1, num_heads, head_size)
        grad_part_heads = grad_part.reshape(-1, num_heads, head_size)
        scores = (
            jnp.einsum(
                "qhd,khd->hqk",
                query_part_heads,
                key_heads_local,
                preferred_element_type=jnp.float32,
            )
            * score_scale
        )
        same_doc = (id_part[:, None] == slot_labels[None, :])[None]
        scores = jnp.where(same_doc, scores, masked_score)
        probs = jnp.where(same_doc, jnp.exp(scores - jnp.transpose(log_part)[..., None]), 0.0)
        grad_value_sum = grad_value_sum + jnp.einsum(
            "hqk,qhd->khd",
            probs.astype(jnp.bfloat16),
            grad_part_heads,
            preferred_element_type=jnp.float32,
        )
        grad_probs = jnp.einsum(
            "qhd,khd->hqk", grad_part_heads, value_heads_local, preferred_element_type=jnp.float32
        )
        grad_scores = (probs * (grad_probs - jnp.transpose(delta_part)[..., None])).astype(
            jnp.bfloat16
        )
        grad_key_sum = grad_key_sum + jnp.einsum(
            "hqk,qhd->khd", grad_scores, query_part_heads, preferred_element_type=jnp.float32
        )
        return (grad_key_sum, grad_value_sum)

    zero_heads = jnp.zeros((local_rows, num_heads, head_size), jnp.float32)
    grad_key_sum, grad_value_sum = in_blocks(
        key_step,
        (zero_heads, zero_heads),
        (
            lax.all_gather(query_rows, "ctx", axis=0, tiled=True),
            lax.all_gather(grad_attended, "ctx", axis=0, tiled=True),
            lax.all_gather(slot_labels, "ctx", axis=0, tiled=True),
        ),
        local_rows,
    )
    grad_query = (grad_query_sum * score_scale).reshape(local_rows, features).astype(jnp.bfloat16)
    grad_key = (grad_key_sum * score_scale).reshape(local_rows, features).astype(jnp.bfloat16)
    grad_value = grad_value_sum.reshape(local_rows, features).astype(jnp.bfloat16)
    grad_projected = jnp.concatenate([grad_query, grad_key, grad_value], axis=1)
    grad_qkv = jnp.einsum(
        "rd,re->de", token_rows, grad_projected, preferred_element_type=jnp.float32
    )
    grad_query_bias = jnp.sum(grad_query.astype(jnp.float32), axis=0)
    grad_value_bias = jnp.sum(grad_value.astype(jnp.float32), axis=0)
    grad_input = grad_mixed + jnp.einsum(
        "re,de->rd", grad_projected, qkv_weight, preferred_element_type=jnp.float32
    )
    grad_tokens = keep_rows * grad_input + (1.0 - keep_rows) * grad_float
    terms = (
        grad_qkv,
        grad_query_bias,
        grad_value_bias,
        grad_proj,
        grad_proj_bias,
        grad_gain1,
        grad_bias1,
        grad_up,
        grad_up_bias,
        grad_down,
        grad_down_bias,
        grad_gain2,
        grad_bias2,
    )
    return (block_rows, grad_tokens, terms)


def on_device(
    tokens,
    doc_ids,
    keep_mask,
    qkv_weight,
    query_bias,
    value_bias,
    proj_weight,
    proj_bias,
    norm1_gain,
    norm1_bias,
    up_weight,
    up_bias,
    down_weight,
    down_bias,
    norm2_gain,
    norm2_bias,
    cotangent,
):
    block_list = []
    grad_list = []
    summed = None
    for micro_index in range(tokens.shape[0]):
        weights_full = (
            lax.all_gather(qkv_weight, "fsdp", axis=0, tiled=True),
            lax.all_gather(query_bias, "fsdp", axis=0, tiled=True),
            lax.all_gather(value_bias, "fsdp", axis=0, tiled=True),
            lax.all_gather(proj_weight, "fsdp", axis=0, tiled=True),
            lax.all_gather(proj_bias, "fsdp", axis=0, tiled=True),
            lax.all_gather(norm1_gain, "fsdp", axis=0, tiled=True),
            lax.all_gather(norm1_bias, "fsdp", axis=0, tiled=True),
            lax.all_gather(up_weight, "fsdp", axis=0, tiled=True),
            lax.all_gather(up_bias, "fsdp", axis=0, tiled=True),
            lax.all_gather(down_weight, "fsdp", axis=0, tiled=True),
            lax.all_gather(down_bias, "fsdp", axis=0, tiled=True),
            lax.all_gather(norm2_gain, "fsdp", axis=0, tiled=True),
            lax.all_gather(norm2_bias, "fsdp", axis=0, tiled=True),
        )
        block_rows, grad_tokens, terms = micro_step(
            tokens[micro_index, 0],
            doc_ids[micro_index, 0],
            keep_mask[micro_index, 0],
            weights_full,
            cotangent[micro_index, 0],
        )
        block_list.append(block_rows)
        grad_list.append(grad_tokens)
        if summed is None:
            summed = terms
        else:
            summed = tuple((earlier + later for earlier, later in zip(summed, terms)))
    reduced = (
        lax.psum_scatter(summed[0], ("ctx", "fsdp"), scatter_dimension=0, tiled=True),
        lax.psum_scatter(summed[1], ("ctx", "fsdp"), scatter_dimension=0, tiled=True),
        lax.psum_scatter(summed[2], ("ctx", "fsdp"), scatter_dimension=0, tiled=True),
        lax.psum_scatter(summed[3], ("ctx", "fsdp"), scatter_dimension=0, tiled=True),
        lax.psum_scatter(summed[4], ("ctx", "fsdp"), scatter_dimension=0, tiled=True),
        lax.psum_scatter(summed[5], ("ctx", "fsdp"), scatter_dimension=0, tiled=True),
        lax.psum_scatter(summed[6], ("ctx", "fsdp"), scatter_dimension=0, tiled=True),
        lax.psum_scatter(summed[7], ("ctx", "fsdp"), scatter_dimension=0, tiled=True),
        lax.psum_scatter(summed[8], ("ctx", "fsdp"), scatter_dimension=0, tiled=True),
        lax.psum_scatter(summed[9], ("ctx", "fsdp"), scatter_dimension=0, tiled=True),
        lax.psum_scatter(summed[10], ("ctx", "fsdp"), scatter_dimension=0, tiled=True),
        lax.psum_scatter(summed[11], ("ctx", "fsdp"), scatter_dimension=0, tiled=True),
        lax.psum_scatter(summed[12], ("ctx", "fsdp"), scatter_dimension=0, tiled=True),
    )
    block_out = jnp.stack(block_list)[:, None]
    grad_tokens_all = jnp.stack(grad_list)[:, None]
    return (
        block_out,
        grad_tokens_all,
        reduced[0],
        reduced[1],
        reduced[2],
        reduced[3],
        reduced[4],
        reduced[5],
        reduced[6],
        reduced[7],
        reduced[8],
        reduced[9],
        reduced[10],
        reduced[11],
        reduced[12],
    )


def solution(mesh):
    in_specs = (
        P(None, "fsdp", "ctx", None),
        P(None, "fsdp", "ctx"),
        P(None, "fsdp", None),
        P("fsdp", None),
        P("fsdp"),
        P("fsdp"),
        P("fsdp", None),
        P("fsdp"),
        P("fsdp"),
        P("fsdp"),
        P("fsdp", None),
        P("fsdp"),
        P("fsdp", None),
        P("fsdp"),
        P("fsdp"),
        P("fsdp"),
        P(None, "fsdp", "ctx", None),
    )
    out_specs = (
        P(None, "fsdp", "ctx", None),
        P(None, "fsdp", "ctx", None),
        P(("ctx", "fsdp"), None),
        P(("ctx", "fsdp")),
        P(("ctx", "fsdp")),
        P(("ctx", "fsdp"), None),
        P(("ctx", "fsdp")),
        P(("ctx", "fsdp")),
        P(("ctx", "fsdp")),
        P(("ctx", "fsdp"), None),
        P(("ctx", "fsdp")),
        P(("ctx", "fsdp"), None),
        P(("ctx", "fsdp")),
        P(("ctx", "fsdp")),
        P(("ctx", "fsdp")),
    )
    return jax.shard_map(
        on_device, mesh=mesh, in_specs=in_specs, out_specs=out_specs, check_vma=False
    )
```

profile of v0, /device:TPU:0, one launch (start us, length us, event | category | flops | bytes accessed | tf_op | source)
XLA Modules:
  0.0 1104.0 jit_solution(3093867166511820813)
XLA Ops:
  8.0 74.3 %all-gather.18.cloned.1.call-done = bf16[768,2304]{1,0:T(8,128)(2,1)} async-done(((bf16[192,2304]{1,0:T(8,128)(2,1)}), bf16[768,2304]{1,0:T(8,128)(2,1)}) %all-gather.18.cloned.1.call-update) | async-done | bytes 3538960 | tf_op jit(solution)/shard_map/all_gather | solution.py:315
  97.5 17.3 %all-reduce.21 = (bf16[768]{0:T(1024)(128)(2,1)}, bf16[768]{0:T(1024)(128)(2,1)}, bf16[768]{0:T(1024)(128)(2,1)}, bf16[768]{0:T(1024)(128)(2,1)}, bf16[768]{0:T(...) all-reduce(bf16[768]{0:T(1024)(128)(2,1)S(1)} %dynamic-update-slice, ...), channel_id=1, replica_groups=mesh['ctx'=8,'fsdp'=4] {'fsdp'}, use_global_device_ids=true, to_apply=%add.1 | all-reduce | flops 6144 | bytes 24576
  124.8 13.0 %all-gather = bf16[4,1,768]{2,1,0:T(2,128)(2,1)S(1)} all-gather(bf16[1,1,768]{2,1,0:T(2,128)(2,1)S(1)} %reshape.549), channel_id=1, replica_groups=mesh['ctx'=8,'fsdp'=4] {'fsdp'}, dimensions={0}, use_global_device_ids=true | all-gather | bytes 7680 | tf_op jit(solution)/shard_map/all_gather | solution.py:323
  141.9 12.0 %all-reduce.20 = (bf16[1536]{0:T(1024)(128)(2,1)S(1)}, bf16[1536]{0:T(1024)(128)(2,1)S(1)}) all-reduce(bf16[1536]{0:T(1024)(128)(2,1)S(1)} %dynamic-update-slice.9, bf16[1536]{0:T(1024)(128)(2,1)S(1)} %dynamic-update-slice), channel_id=1, replica_groups=mesh['ctx'=8,'fsdp'=4] {'ctx'}, use_global_device_ids=true, to_apply=%add.9 | all-reduce | flops 3072 | bytes 12288
  167.9 34.1 %while.78 = (s32[]{:T(128)}, f32[12,192]{1,0:T(8,128)S(1)}, f32[12,192]{1,0:T(8,128)S(1)}, f32[12,192,64]{1,2,0:T(8,128)}, bf16[192]{0:T(256)(128)(2,1)}, /*inde...) while((s32[]{:T(128)}, f32[12,192]{1,0:T(8,128)S(1)}, ...), condition=%wide.region_4.5_spmd.clone, body=%wide.region_1.4_spmd.clone.sunk | while | flops 476589312 | bytes 58864732 | solution.py:43
  207.6 61.7 %all-gather.26.cloned.1.call-done = bf16[768,3072]{1,0:T(8,128)(2,1)} async-done(((bf16[192,3072]{1,0:T(8,128)(2,1)}), bf16[768,3072]{1,0:T(8,128)(2,1)}) %all-gather.26.cloned.1.call-update) | async-done | bytes 4718608 | tf_op jit(solution)/shard_map/all_gather | solution.py:322
  269.3 9.4 multiply_convert_fusion.13
  278.8 79.8 %all-gather.28.cloned.1.call-done = bf16[3072,768]{1,0:T(8,128)(2,1)} async-done(((bf16[768,768]{1,0:T(8,128)(2,1)}), bf16[3072,768]{1,0:T(8,128)(2,1)}) %all-gather.28.cloned.1.call-update) | async-done | bytes 4718608 | tf_op jit(solution)/shard_map/all_gather | solution.py:324
  363.3 24.7 %all-gather.30.cloned.1.call-done = bf16[1536,768]{1,0:T(8,128)(2,1)} async-done(((bf16[192,768]{1,0:T(8,128)(2,1)}), bf16[1536,768]{1,0:T(8,128)(2,1)}) %all-gather.30.cloned.1.call-update) | async-done | bytes 2359312 | tf_op jit(solution)/shard_map/all_gather | solution.py:117
  390.9 28.1 %all-gather.32.cloned.1.call-done = bf16[1536,768]{1,0:T(8,128)(2,1)} async-done(((bf16[192,768]{1,0:T(8,128)(2,1)}), bf16[1536,768]{1,0:T(8,128)(2,1)}) %all-gather.32.cloned.1.call-update) | async-done | bytes 2359312 | tf_op jit(solution)/shard_map/all_gather | solution.py:118
  423.3 34.8 %while.79 = (s32[]{:T(128)}, f32[12,192]{1,0:T(8,128)S(1)}, f32[12,192]{1,0:T(8,128)S(1)}, f32[12,192,64]{1,2,0:T(8,128)}, bf16[192]{0:T(256)(128)(2,1)S(1)}, /*...) while((s32[]{:T(128)}, f32[12,192]{1,0:T(8,128)S(1)}, ...), condition=%wide.region_13.14_spmd.clone, body=%wide.region_10.13_spmd.clone.sunk | while | flops 476589312 | bytes 58840100 | solution.py:43
  527.0 33.1 %while.82 = (s32[]{:T(128)}, f32[192,12,64]{0,2,1:T(8,128)}, bf16[2,768,768]{1,2,0:T(8,128)(2,1)S(1)}, bf16[192]{0:T(256)(128)(2,1)}, bf16[2,768]{1,0:T(2,128)(2...) while((s32[]{:T(128)}, f32[192,12,64]{0,2,1:T(8,128)}, ...), condition=%wide.region_33.34_spmd.clone, body=%wide.region_32.33_spmd.clone.sunk | while | flops 692305920 | bytes 24515144 | solution.py:43
  551.8 8.3 fusion.354
  570.7 32.7 %while.80 = (s32[]{:T(128)}, f32[192,12,64]{0,2,1:T(8,128)}, bf16[2,768,768]{1,2,0:T(8,128)(2,1)S(1)}, bf16[192]{0:T(256)(128)(2,1)}, bf16[2,768]{1,0:T(2,128)(2...) while((s32[]{:T(128)}, f32[192,12,64]{0,2,1:T(8,128)}, ...), condition=%wide.region_24.25_spmd.clone, body=%wide.region_23.24_spmd.clone.sunk | while | flops 692305920 | bytes 25680940 | solution.py:43
  578.9 8.2 fusion.336
  595.0 8.4 fusion.336
  604.1 9.2 all-gather.3
  623.1 9.2 all-gather.1
  633.1 8.2 all-gather.2
  643.6 52.0 %while.83 = (s32[]{:T(128)}, f32[192,12,64]{0,2,1:T(8,128)}, f32[192,12,64]{0,2,1:T(8,128)}, bf16[2,768,768]{2,1,0:T(8,128)(2,1)}, bf16[2,768]{1,0:T(2,128)(2,1)...) while((s32[]{:T(128)}, f32[192,12,64]{0,2,1:T(8,128)}, ...), condition=%wide.region_35.36_spmd.clone, body=%wide.region_34.35_spmd.clone.sunk | while | flops 927940608 | bytes 45090048 | solution.py:43
  700.0 53.5 %while.81 = (s32[]{:T(128)}, f32[192,12,64]{0,2,1:T(8,128)}, f32[192,12,64]{0,2,1:T(8,128)}, bf16[2,768,768]{2,1,0:T(8,128)(2,1)}, bf16[2,768]{1,0:T(2,128)(2,1)...) while((s32[]{:T(128)}, f32[192,12,64]{0,2,1:T(8,128)}, ...), condition=%wide.region_26.27_spmd.clone, body=%wide.region_25.26_spmd.clone.sunk | while | flops 927940608 | bytes 45090048 | solution.py:43
  785.5 42.8 %all-reduce.19 = (f32[768]{0:T(1024)}, f32[768]{0:T(1024)}, f32[768]{0:T(1024)}, f32[768]{0:T(1024)}, f32[768]{0:T(1024)}, /*index=5*/f32[3072]{0:T(1024)}, f32[768]{0:T(1024)}, f32[768]{0:T(1024)}, f32[768]{0:T(1024)}) all-reduce(f32[768]{0:T(1024)S(1)} %add.352, ...), channel_id=3, replica_groups=mesh['ctx'=8,'fsdp'=4] {'ctx','fsdp'}, use_global_device_ids=true, to_apply=%region_39.40.clone | all-reduce | flops 9216 | bytes 73728
  845.2 126.7 %reduce-scatter.11.cloned.1.call-done = f32[96,768]{1,0:T(8,128)} async-done(((f32[3072,768]{1,0:T(8,128)}), f32[96,768]{1,0:T(8,128)}) %reduce-scatter.11.cloned.1.call-update) | async-done | bytes 294928 | tf_op jit(solution)/shard_map/reduce_scatter | solution.py:352
  971.9 125.4 %reduce-scatter.13.cloned.1.call-done = f32[24,2304]{1,0:T(8,128)} async-done(((f32[768,2304]{1,0:T(8,128)}), f32[24,2304]{1,0:T(8,128)}) %reduce-scatter.13.cloned.1.call-update) | async-done | bytes 221200
  (620 shorter events, 410.8 us)
Async XLA Ops:
  7.2 75.1 %all-gather.18.cloned.1.call-start = ((), (), s32[]{:S(2)}) async-start(), calls=%async_computation.4 | async-start | bytes 4423680 | tf_op jit(solution)/shard_map/all_gather | solution.py:315
  7.9 79.6 %copy-start.134 = (u32[32]{0:T(128)S(1)}, u32[32]{0:T(128)}, u32[]{:S(2)}) copy-start(u32[32]{0:T(128)} %constant.204) | copy-start | bytes 388
  7.9 80.8 %copy-start.130 = (bf16[192]{0:T(256)(128)(2,1)S(1)}, bf16[192]{0:T(256)(128)(2,1)}, u32[]{:S(2)}) copy-start(bf16[192]{0:T(256)(128)(2,1)} %param.33) | copy-start | bytes 1156
  7.9 81.1 %copy-start.131 = (bf16[192]{0:T(256)(128)(2,1)S(1)}, bf16[192]{0:T(256)(128)(2,1)}, u32[]{:S(2)}) copy-start(bf16[192]{0:T(256)(128)(2,1)} %param.34) | copy-start | bytes 1156
  7.9 152.7 %all-gather.20.cloned.1.call-start = ((), (), s32[]{:S(2)}) async-start(), calls=%async_computation.5 | async-start | bytes 2654208 | tf_op jit(solution)/shard_map/all_gather | solution.py:117
  87.4 76.1 %all-gather.22.cloned.1.call-start = ((), (), s32[]{:S(2)}) async-start(), calls=%async_computation.6 | async-start | bytes 2654208 | tf_op jit(solution)/shard_map/all_gather | solution.py:118
  119.7 85.0 %all-gather.24.cloned.1.call-start = ((), (), s32[]{:S(2)}) async-start(), calls=%async_computation.7 | async-start | bytes 1474560 | tf_op jit(solution)/shard_map/all_gather | solution.py:318
  120.3 149.0 %all-gather.26.cloned.1.call-start = ((), (), s32[]{:S(2)}) async-start(), calls=%async_computation.8 | async-start | bytes 5898240 | tf_op jit(solution)/shard_map/all_gather | solution.py:322
  120.9 237.8 %all-gather.28.cloned.1.call-start = ((), (), s32[]{:S(2)}) async-start(), calls=%async_computation.9 | async-start | bytes 5898240 | tf_op jit(solution)/shard_map/all_gather | solution.py:324
  121.4 266.6 %all-gather.30.cloned.1.call-start = ((), (), s32[]{:S(2)}) async-start(), calls=%async_computation.10 | async-start | bytes 2654208 | tf_op jit(solution)/shard_map/all_gather | solution.py:117
  123.3 295.6 %all-gather.32.cloned.1.call-start = ((), (), s32[]{:S(2)}) async-start(), calls=%async_computation.11 | async-start | bytes 2654208 | tf_op jit(solution)/shard_map/all_gather | solution.py:118
  124.1 519.5 %all-gather.38.cloned.1.call-start = ((), (), s32[]{:S(2)}) async-start(), calls=%async_computation.14 | async-start | bytes 2654208 | tf_op jit(solution)/shard_map/all_gather | solution.py:254
  160.4 483.1 %all-gather.40.cloned.1.call-start = ((), (), s32[]{:S(2)}) async-start(), calls=%async_computation.15 | async-start | bytes 2654208 | tf_op jit(solution)/shard_map/all_gather | solution.py:255
  202.0 76.7 %copy-start.37 = (f32[12,192]{1,0:T(8,128)}, f32[12,192]{1,0:T(8,128)S(1)}, u32[]{:S(2)}) copy-start(f32[12,192]{1,0:T(8,128)S(1)} %get-tuple-element.347) | copy-start | bytes 27652
  206.6 152.1 %copy-start.97 = (f32[192]{0:T(256)}, f32[192]{0:T(256)S(1)}, u32[]{:S(2)}) copy-start(f32[192]{0:T(256)S(1)} %broadcast_multiply_fusion.3) | copy-start | bytes 2308
  207.6 151.1 %copy-start.102 = (f32[192]{0:T(256)}, f32[192]{0:T(256)S(1)}, u32[]{:S(2)}) copy-start(f32[192]{0:T(256)S(1)} %fusion.167) | copy-start | bytes 2308
  269.3 89.3 %copy-start.15 = (f32[192,768]{1,0:T(8,128)S(1)}, f32[192,768]{1,0:T(8,128)}, u32[]{:S(2)}) copy-start(f32[192,768]{1,0:T(8,128)} %copy-done.14) | copy-start | bytes 1769476
  269.3 89.3 %copy-start.116 = (f32[768]{0:T(1024)S(1)}, f32[768]{0:T(1024)}, u32[]{:S(2)}) copy-start(f32[768]{0:T(1024)} %convert_element_type.274) | copy-start | bytes 9220
  492.3 207.7 %all-gather.34.cloned.1.call-start = ((), (), s32[]{:S(2)}) async-start(), calls=%async_computation.12 | async-start | bytes 2654208 | tf_op jit(solution)/shard_map/all_gather | solution.py:254
  493.0 207.0 %all-gather.36.cloned.1.call-start = ((), (), s32[]{:S(2)}) async-start(), calls=%async_computation.13 | async-start | bytes 2654208 | tf_op jit(solution)/shard_map/all_gather | solution.py:255
  498.1 347.1 %reduce-scatter.7.cloned.1.call-start = ((), (), s32[]{:S(2)}) async-start(), calls=%async_computation.16 | async-start | bytes 2433024 | tf_op jit(solution)/shard_map/reduce_scatter | solution.py:346
  501.8 343.5 %reduce-scatter.9.cloned.1.call-start = ((), (), s32[]{:S(2)}) async-start(), calls=%async_computation.17 | async-start | bytes 9732096 | tf_op jit(solution)/shard_map/reduce_scatter | solution.py:350
  511.0 460.9 %reduce-scatter.11.cloned.1.call-start = ((), (), s32[]{:S(2)}) async-start(), calls=%async_computation.18 | async-start | bytes 9732096 | tf_op jit(solution)/shard_map/reduce_scatter | solution.py:352
  603.5 493.8 %reduce-scatter.13.cloned.1.call-start = ((), (), s32[]{:S(2)}) async-start(), calls=%async_computation.19 | async-start | bytes 7299072
  (152 other events, 1847.9 us)
Sparse Core Ops, SparseCore 0:
  9.6 72.6 all-gather.17
  87.6 27.6 all-gather.19
  119.8 27.3 all-gather.21
  148.7 30.6 all-gather.23
  180.8 88.5 all-gather.25
  270.7 87.8 all-gather.27
  360.5 27.4 all-gather.29
  389.9 29.0 all-gather.31
  420.8 29.0 all-gather.37
  492.4 29.0 all-gather.39
  523.4 29.0 all-gather.33
  554.1 29.0 all-gather.35
  589.1 99.2 reduce-scatter.6
  695.7 135.3 reduce-scatter.8
  837.5 134.3 reduce-scatter.10
  978.9 118.2 reduce-scatter.12
where the time goes:
time: 1110 us; the launch traced here: 1100 us
  waiting for transfers between devices  525 us (47%)
  matrix products  231 us (21%)
  blocking collectives  120 us (11%)
  local copies, waits for them, and re-layouts  116 us (10%)
  other arithmetic  85.2 us (8%)
  between operations  17 us (2%)
    unnamed x17, waiting for transfers between devices  129 us
    reduce_scatter x1, waiting for transfers between devices, on_device(): lax.psum_scatter(summed[9], ('ctx', 'fsdp'), scatter_dimension=0, tiled=T...  127 us
    all_gather x1, waiting for transfers between devices, on_device(): lax.all_gather(down_weight, 'fsdp', axis=0, tiled=True)  79.8 us
    all_gather x1, waiting for transfers between devices, on_device(): lax.all_gather(qkv_weight, 'fsdp', axis=0, tiled=True)  74.3 us
    unnamed x3, blocking collectives  72.1 us
    all_gather x1, waiting for transfers between devices, on_device(): lax.all_gather(up_weight, 'fsdp', axis=0, tiled=True)  61.7 us
    unnamed x285, local copies, waits for them, and re-layouts  56.7 us
    dynamic_slice x36, local copies, waits for them, and re-layouts, in_blocks(): carried, ignored = lax.scan(one_turn, carried, (stacked, offsets))  35 us
  transfers between devices with their start and end apart: 16, of which 7 were waited for; matrix products, arithmetic and copies ran while one was open for 38% of the time, Pallas kernels for 0%

commit v1 on v0

--- a/solution.py
+++ b/solution.py
@@ -1,8 +1,11 @@
+import functools
 import math
 
 import jax
 import jax.numpy as jnp
 from jax import lax
+from jax.experimental import pallas as pl
+from jax.experimental.pallas import tpu as pltpu
 from jax.sharding import PartitionSpec as P
 
 H = 12
@@ -375,6 +378,801 @@
     )
 
 
+MASKED = -1e30
+LOWEST = -3e38
+ARRIVAL = (0, 4, 2, 6, 1, 5, 3, 7)
+GROUP = 192
+HEAD = 64
+HEADS_EACH = 3
+PAIR = 384
+SLOTS = 1536
+ID_ROWS = 8
+
+
+def fits(mesh):
+    return mesh.shape["ctx"] == 8 and mesh.shape["fsdp"] == 4
+
+
+def dot(a, b):
+    return lax.dot_general(a, b, (((1,), (0,)), ((), ())), preferred_element_type=jnp.float32)
+
+
+def dot_nt(a, b):
+    return lax.dot_general(a, b, (((1,), (1,)), ((), ())), preferred_element_type=jnp.float32)
+
+
+def flip(value):
+    return jnp.transpose(value.astype(jnp.float32)).astype(jnp.bfloat16)
+
+
+def split3(value):
+    high = value.astype(jnp.bfloat16).astype(jnp.float32)
+    mid = (value - high).astype(jnp.bfloat16).astype(jnp.float32)
+    return high, mid, value - high - mid
+
+
+def call(kernel, name, ins, outs, scratch=(), scalars=1, any_ins=0, flops=5 * 10**9, aliases=None):
+    vmem = pl.BlockSpec(memory_space=pltpu.VMEM)
+    return pl.pallas_call(
+        kernel,
+        name=name,
+        out_shape=[jax.ShapeDtypeStruct(shape, kind) for shape, kind in outs],
+        grid_spec=pltpu.PrefetchScalarGridSpec(
+            num_scalar_prefetch=scalars,
+            in_specs=[vmem] * (len(ins) - scalars - any_ins)
+            + [pl.BlockSpec(memory_space=pl.ANY)] * any_ins,
+            out_specs=[vmem] * len(outs),
+            scratch_shapes=list(scratch),
+        ),
+        cost_estimate=pl.CostEstimate(flops=flops, bytes_accessed=10**7, transcendentals=10**6),
+        compiler_params=pltpu.CompilerParams(vmem_limit_bytes=56 * 2**20),
+    )(*ins)
+
+
+QUAD = 768
+TILE = 256
+TILES = SLOTS // TILE
+
+
+def project_kernel(place, *refs):
+    x_refs = refs[:2]
+    own_ref, near_ref, mid_ref, far_ref = refs[2:6]
+    qt_refs, ka_refs = refs[6:9], refs[9:12]
+    vt_ref, w_ref, vec_ref, turned = refs[12:]
+    me, depth = place[0], place[1]
+    for m, ref in enumerate((own_ref, near_ref, mid_ref, far_ref)):
+        owner = depth ^ m
+        rows = pl.ds(pl.multiple_of(owner * GROUP, GROUP), GROUP)
+        w_ref[rows, :] = ref[0:GROUP, :]
+        vec_ref[owner] = ref[GROUP : GROUP + 8, :].astype(jnp.float32)
+    mine = vec_ref[me & 3]
+    turned[0:GROUP] = flip(w_ref[:, 0:GROUP])
+    turned[GROUP:] = flip(w_ref[:, 2 * GROUP :])
+    bias = jnp.concatenate([mine[:, 0:GROUP], mine[:, GROUP : 2 * GROUP]], axis=1)
+    bias = jnp.transpose(bias)[:, 0:1]
+    lane = lax.broadcasted_iota(jnp.int32, (QUAD, HEAD), 1)
+    row = lax.broadcasted_iota(jnp.int32, (HEAD, QUAD), 0)
+    for t in range(2):
+        span = slice(t * QUAD, (t + 1) * QUAD)
+        x = jnp.concatenate([x_refs[t][i, 0:GROUP] for i in range(4)], axis=0)
+        ids = jnp.concatenate(
+            [x_refs[t][i, GROUP : GROUP + 8, 0:GROUP] for i in range(4)], axis=1
+        ).astype(jnp.float32)
+        id_row = ids[0:1, :]
+        id_col = jnp.transpose(ids)[:, 0:1]
+        k_side = jnp.where(
+            lane < 5,
+            jnp.where(id_col == lane.astype(jnp.float32), 0.0, MASKED),
+            jnp.where(lane < 8, -1.0, 0.0),
+        ).astype(jnp.bfloat16)
+        q_side = jnp.where((row < 5) & (id_row == row.astype(jnp.float32)), 1.0, 0.0).astype(
+            jnp.bfloat16
+        )
+        k = dot(x, w_ref[:, GROUP : 2 * GROUP]).astype(jnp.bfloat16)
+        qv = (dot_nt(turned[...], x) + bias).astype(jnp.bfloat16)
+        vt_ref[:, span] = qv[GROUP:]
+        q = (qv[:GROUP] * 0.125).astype(jnp.bfloat16)
+        for h in range(HEADS_EACH):
+            heads = slice(h * HEAD, (h + 1) * HEAD)
+            ka_refs[h][span, :] = jnp.concatenate([k[:, heads], k_side], axis=1)
+            qt_refs[h][0:HEAD, span] = q[heads]
+            qt_refs[h][HEAD : 2 * HEAD, span] = q_side
+
+
+def turn_kernel(*refs):
+    x_refs, qt_refs, ka_refs = refs[:2], refs[2:5], refs[5:8]
+    vt_ref, w_ref = refs[8:10]
+    xt_ref, qn_ref, kt_ref, va_refs, by_head = refs[10], refs[11], refs[12], refs[13:16], refs[16]
+    lane = lax.broadcasted_iota(jnp.int32, (PAIR, HEAD), 1)
+    v_side = jnp.where(lane < 3, -1.0, 0.0).astype(jnp.bfloat16)
+    for t in range(4):
+        span = slice(t * PAIR, (t + 1) * PAIR)
+        x = jnp.concatenate([x_refs[t // 2][2 * (t % 2) + i, 0:GROUP] for i in (0, 1)], axis=0)
+        xt_ref[:, span] = flip(x)
+        for h in range(HEADS_EACH):
+            heads = slice(h * HEAD, (h + 1) * HEAD)
+            qn_ref[span, heads] = flip(qt_refs[h][0:HEAD, span])
+            kt_ref[heads, span] = flip(ka_refs[h][span, 0:HEAD])
+            va_refs[h][span, :] = jnp.concatenate([flip(vt_ref[heads, span]), v_side], axis=1)
+    for h in range(HEADS_EACH):
+        for i in range(3):
+            by_head[:, (3 * h + i) * HEAD : (3 * h + i + 1) * HEAD] = w_ref[
+                :, i * GROUP + h * HEAD : i * GROUP + (h + 1) * HEAD
+            ]
+
+
+def attend_kernel(heads, place, *refs):
+    n = len(heads)
+    qt_refs, ka_refs, vt_ref = refs[:n], refs[n : 2 * n], refs[2 * n]
+    last = heads[-1] == HEADS_EACH - 1
+    earlier = refs[2 * n + 1 : 3 * n + 1] if not last else refs[2 * n + 1 : 2 * n + 3]
+    refs = refs[2 * n + 1 + (len(earlier) if last else 0) :]
+    out_qt, out_ot = refs[:n], refs[n : 2 * n]
+    o_ref = refs[2 * n] if last else None
+    held = refs[-1]
+    me = place[0]
+    at_row = lax.broadcasted_iota(jnp.int32, (16, TILE), 0)
+
+    def one_tile(t, unused):
+        here = pl.ds(pl.multiple_of(t * TILE, TILE), TILE)
+        tops = []
+        for i in range(n):
+            q_tile = qt_refs[i][:, here]
+            top = jnp.full((8, TILE), LOWEST, jnp.float32)
+            for j in range(TILES):
+                span = slice(j * TILE, (j + 1) * TILE)
+                scores = dot(ka_refs[i][span, :], q_tile)
+                held[i, span, :] = scores
+                top = jnp.maximum(top, jnp.max(scores.reshape(TILE // 8, 8, TILE), axis=0))
+            tops.append(jnp.max(top, axis=0, keepdims=True))
+        for i, h in enumerate(heads):
+            rows = slice(h * HEAD, (h + 1) * HEAD)
+            total = jnp.zeros((8, TILE), jnp.float32)
+            out = jnp.zeros((HEAD, TILE), jnp.float32)
+            for j in range(TILES):
+                span = slice(j * TILE, (j + 1) * TILE)
+                probs = jnp.exp(held[i, span, :] - tops[i])
+                total = total + jnp.sum(probs.reshape(TILE // 8, 8, TILE), axis=0)
+                out = out + dot(vt_ref[rows, span], probs.astype(jnp.bfloat16))
+            total = jnp.sum(total, axis=0, keepdims=True)
+            out_ot[i][:, here] = (out / total).astype(jnp.bfloat16)
+            high, mid, low = split3(tops[i] + jnp.log(total))
+            side = qt_refs[i][HEAD : HEAD + 16, here].astype(jnp.float32)
+            side = jnp.where(at_row == 5, high, side)
+            side = jnp.where(at_row == 6, mid, side)
+            side = jnp.where(at_row == 7, low, side)
+            out_qt[i][0:HEAD, here] = qt_refs[i][0:HEAD, here]
+            out_qt[i][HEAD : HEAD + 16, here] = side.astype(jnp.bfloat16)
+            out_qt[i][HEAD + 16 :, here] = qt_refs[i][HEAD + 16 :, here]
+        return unused
+
+    lax.fori_loop(0, TILES, one_tile, 0)
+    if last:
+        for t in range(4):
+            span = slice(t * PAIR, (t + 1) * PAIR)
+            whole = jnp.concatenate(
+                [ref[:, span] for ref in (*earlier, *out_ot)], axis=0
+            )
+            rows = flip(whole)
+            for half in range(2):
+                o_ref[me ^ ARRIVAL[2 * t + half]] = rows[half * GROUP : (half + 1) * GROUP, :]
+
+
+def attend_back_kernel(heads, place, *refs):
+    n = len(heads)
+    do_ref, kt_ref, qn_ref, xt_ref = refs[:4]
+    refs = refs[4:]
+    ot_refs, qt_refs, ka_refs, va_refs = [refs[i * n : (i + 1) * n] for i in range(4)]
+    refs = refs[4 * n :]
+    last = heads[-1] == HEADS_EACH - 1
+    if last:
+        earlier_ref, w_ref = refs[:2]
+        refs = refs[2:]
+        sent_ref, keep_ref, give_ref, g_ref = refs[:4]
+        refs = refs[4:]
+    else:
+        sent_ref, g_ref = refs[0], refs[1]
+        refs = refs[2:]
+    dot_t, don, dqt = refs
+    me = place[0]
+    row = lax.broadcasted_iota(jnp.int32, (HEAD, PAIR), 0)
+    for t in range(4):
+        here = slice(t * PAIR, (t + 1) * PAIR)
+        a, b = me ^ ARRIVAL[2 * t], me ^ ARRIVAL[2 * t + 1]
+        for i, h in enumerate(heads):
+            cols = slice(h * HEAD, (h + 1) * HEAD)
+            grad = jnp.concatenate([do_ref[a][:, cols], do_ref[b][:, cols]], axis=0)
+            don[i, here, :] = grad
+            grad_t = jnp.transpose(grad.astype(jnp.float32))
+            delta = jnp.sum(grad_t * ot_refs[i][:, here].astype(jnp.float32), axis=0, keepdims=True)
+            high, mid, low = split3(delta)
+            side = jnp.where(
+                row == 0, high, jnp.where(row == 1, mid, jnp.where(row == 2, low, 0.0))
+            )
+            dot_t[i, 0:HEAD, here] = grad_t.astype(jnp.bfloat16)
+            dot_t[i, HEAD : 2 * HEAD, here] = side.astype(jnp.bfloat16)
+    dqt[...] = jnp.zeros_like(dqt)
+
+    def keys(j, unused):
+        here = pl.ds(pl.multiple_of(j * TILE, TILE), TILE)
+        for i, h in enumerate(heads):
+            rows = slice(h * HEAD, (h + 1) * HEAD)
+            key = ka_refs[i][here, :]
+            val = va_refs[i][here, :]
+            key_t = kt_ref[rows, here]
+            dk = jnp.zeros((TILE, HEAD), jnp.float32)
+            dv = jnp.zeros((TILE, HEAD), jnp.float32)
+            for t in range(TILES):
+                span = slice(t * TILE, (t + 1) * TILE)
+                probs = jnp.exp(dot(key, qt_refs[i][:, span]))
+                grad_probs = dot(val, dot_t[i, :, span])
+                grad_scores = (probs * grad_probs).astype(jnp.bfloat16)
+                dv = dv + dot(probs.astype(jnp.bfloat16), don[i, span, :])
+                dk = dk + dot(grad_scores, qn_ref[span, rows])
+                dqt[i, :, span] = dqt[i, :, span] + dot(key_t, grad_scores)
+            at = i * GROUP
+            g_ref[here, at + HEAD : at + 2 * HEAD] = dk.astype(jnp.bfloat16)
+            g_ref[here, at + 2 * HEAD : at + GROUP] = dv.astype(jnp.bfloat16)
+        return unused
+
+    lax.fori_loop(0, TILES, keys, 0)
+    bias = jnp.zeros((1, n * GROUP), jnp.float32)
+    for t in range(4):
+        span = slice(t * PAIR, (t + 1) * PAIR)
+        for i in range(n):
+            g_ref[span, i * GROUP : i * GROUP + HEAD] = (
+                jnp.transpose(dqt[i, :, span]) * 0.125
+            ).astype(jnp.bfloat16)
+        bias = bias + jnp.sum(g_ref[span, :].astype(jnp.float32), axis=0, keepdims=True)
+    high = bias.astype(jnp.bfloat16).astype(jnp.float32)
+    at_row = lax.broadcasted_iota(jnp.int32, (8, n * GROUP), 0)
+    fixed = jnp.where(at_row == 0, high, jnp.where(at_row == 1, bias - high, 0.0))
+
+    def weights_back(t, unused):
+        x_rows = xt_ref[pl.ds(pl.multiple_of(t * GROUP, GROUP), GROUP), :]
+        part = dot(x_rows, g_ref[...]).astype(jnp.bfloat16)
+        for i in range(8):
+            sent_ref[8 * t + i, 0:24, :] = part[24 * i : 24 * (i + 1)]
+            sent_ref[8 * t + i, 24:32, :] = fixed.astype(jnp.bfloat16)
+        return unused
+
+    lax.fori_loop(0, 4, weights_back, 0)
+    if last:
+        split = earlier_ref.shape[1]
+
+        for t in range(4):
+            here = slice(t * PAIR, (t + 1) * PAIR)
+            back_ref, at = (keep_ref, 2 * t) if t < 2 else (give_ref, 2 * t - 4)
+            part = dot_nt(earlier_ref[here, :], w_ref[:, :split])
+            part = (part + dot_nt(g_ref[here, :], w_ref[:, split:])).astype(jnp.bfloat16)
+            back_ref[at] = part[:GROUP]
+            back_ref[at + 1] = part[GROUP:]
+
+
+LOW, WIDE = jnp.bfloat16, jnp.float32
+
+
+def project(*ins):
+    outs = [((2 * HEAD, SLOTS), LOW)] * 3 + [((SLOTS, 2 * HEAD), LOW)] * 3
+    outs += [((GROUP, SLOTS), LOW), ((4 * GROUP, 3 * GROUP), LOW), ((4, 8, 3 * GROUP), WIDE)]
+    scratch = [pltpu.VMEM((2 * GROUP, 4 * GROUP), LOW)]
+    return call(project_kernel, "project", ins, outs, scratch)
+
+
+def turn(*ins):
+    outs = [((4 * GROUP, SLOTS), LOW), ((SLOTS, GROUP), LOW), ((GROUP, SLOTS), LOW)]
+    outs += [((SLOTS, 2 * HEAD), LOW)] * 3 + [((4 * GROUP, 3 * GROUP), LOW)]
+    return call(turn_kernel, "turn", ins, outs, scalars=0)
+
+
+def attend(heads, *ins):
+    n = len(heads)
+    outs = [((2 * HEAD, SLOTS), LOW)] * n + [((HEAD, SLOTS), LOW)] * n
+    if heads[-1] == HEADS_EACH - 1:
+        outs.append(((8, GROUP, GROUP), LOW))
+    scratch = [pltpu.VMEM((n, SLOTS, TILE), WIDE)]
+    kernel = functools.partial(attend_kernel, heads)
+    return call(kernel, f"attend{heads[0]}", ins, outs, scratch)
+
+
+def attend_back(heads, *ins):
+    n = len(heads)
+    scratch = [
+        pltpu.VMEM((n, 2 * HEAD, SLOTS), LOW),
+        pltpu.VMEM((n, SLOTS, HEAD), LOW),
+        pltpu.VMEM((n, HEAD, SLOTS), WIDE),
+    ]
+    outs = [((32, 32, n * GROUP), LOW)]
+    if heads[-1] == HEADS_EACH - 1:
+        outs += [((4, GROUP, 4 * GROUP), LOW)] * 2
+    outs.append(((SLOTS, n * GROUP), LOW))
+    kernel = functools.partial(attend_back_kernel, heads)
+    return call(kernel, f"attend_back{heads[0]}", ins, outs, scratch, flops=10**10)
+
+
+def from_ctx(value, bits):
+    return lax.ppermute(value, "ctx", [(i, i ^ bits) for i in range(8)])
+
+
+def from_fsdp(value, bits):
+    return lax.ppermute(value, "fsdp", [(i, i ^ bits) for i in range(4)])
+
+
+FF_CUT = 384
+PROJ_ROWS = 48
+DOWN_ROWS = 96
+PIECE = 240
+FIRST = 368
+SECOND = 3 * PIECE - FIRST
+COLUMNS = 3968
+LEFT = 2048
+
+
+def norm(value):
+    centred = value - jnp.mean(value, axis=1, keepdims=True)
+    scale = lax.rsqrt(jnp.mean(centred * centred, axis=1, keepdims=True) + epsilon)
+    return centred * scale, scale
+
+
+def norm_back(grad, normal, scale):
+    return scale * (
+        grad
+        - jnp.mean(grad, axis=1, keepdims=True)
+        - normal * jnp.mean(grad * normal, axis=1, keepdims=True)
+    )
+
+
+TAIL_AT = 0.35
+TAIL = (
+    0.19746588,
+    0.197487361,
+    0.184996341,
+    0.164759887,
+    0.106787389,
+    0.160058898,
+    -0.11534264,
+    0.24699889,
+    -0.186710954,
+    0.0434989602,
+)
+
+
+def gelu_parts(value):
+    bell = jnp.exp(-0.5 * value * value)
+    t = 1.0 / (1.0 + (TAIL_AT * 2.0**-0.5) * jnp.abs(value))
+    tail = jnp.full_like(t, 0.5 * TAIL[-1])
+    for term in TAIL[-2::-1]:
+        tail = tail * t + 0.5 * term
+    tail = tail * t * bell
+    return jnp.where(value < 0.0, tail, 1.0 - tail), bell
+
+
+FF_STEP = 512
+
+
+def dense_kernel(place, *refs):
+    a_ref, tok_ref, cot_ref, keep_ref, vec_ref = refs[:5]
+    proj_own, up_own, down_all = refs[5:8]
+    shared = refs[8:10]
+    block_ref, base_ref, ga_ref, rows_ref, keep_cols, give_cols = refs[10:16]
+    up, down, proj, slope, act_ref, att_ref, hid_ref, hid_t, gb_ref = refs[16:25]
+    sums_ref, upb_ref, turned, proj_sem, up_sem, down_sem = refs[25:]
+    me, depth = place[0], place[1]
+    width = 4 * GROUP
+    proj_copies, up_copies, down_copies = [], [], []
+
+    def copy(into, source, target, sem):
+        made = pltpu.make_async_copy(source, target, sem.at[len(into)])
+        made.start()
+        into.append(made)
+
+    def spot(k, m, up_row=0):
+        owner = me ^ k
+        return (
+            pl.ds(pl.multiple_of((depth ^ m) * GROUP + up_row, 64), GROUP - up_row),
+            pl.ds(pl.multiple_of(owner * FF_CUT, FF_CUT), FF_CUT),
+        )
+
+    def proj_spot(k, m):
+        owner = me ^ k
+        at = (depth ^ m) * GROUP + (owner >> 1) * PROJ_ROWS
+        return (
+            pl.ds(pl.multiple_of(at, PROJ_ROWS), PROJ_ROWS),
+            pl.ds(pl.multiple_of((owner & 1) * FF_CUT, FF_CUT), FF_CUT),
+        )
+
+    own_rows = pl.ds(pl.multiple_of(depth * GROUP, GROUP), GROUP)
+    starts = []
+    for core in range(2):
+        for i in range(4):
+            starts.append((core, core ^ (0, 2, 4, 6)[i], i * FIRST, core ^ (0, 4, 2, 6)[i], 4 * FIRST + i * SECOND))
+    copy(proj_copies, proj_own, proj.at[own_rows], proj_sem)
+    for core, k_first, first, k_second, second in starts:
+        source = shared[core]
+        for k, m, at in (
+            (k_first, 1, first + GROUP),
+            (k_second, 2, second + 64),
+            (k_second, 3, second + 64 + PROJ_ROWS + GROUP),
+        ):
+            copy(proj_copies, source.at[pl.ds(at, PROJ_ROWS)], proj.at[proj_spot(k, m)], proj_sem)
+    copy(up_copies, up_own, up.at[own_rows], up_sem)
+    for core, k_first, first, k_second, second in starts:
+        source = shared[core]
+        copy(up_copies, source.at[pl.ds(first, GROUP)], up.at[spot(k_first, 1)], up_sem)
+        rows, cols = spot(k_first, 2)
+        rows = pl.ds(pl.multiple_of((depth ^ 2) * GROUP, GROUP), 128)
+        copy(up_copies, source.at[pl.ds(first + PIECE, 128)], up.at[rows, cols], up_sem)
+        copy(up_copies, source.at[pl.ds(second, 64)], up.at[spot(k_second, 2, 128)], up_sem)
+        at = second + 64 + PROJ_ROWS
+        copy(up_copies, source.at[pl.ds(at, GROUP)], up.at[spot(k_second, 3)], up_sem)
+    for i in range(8):
+        for j in range(4):
+            copy(
+                down_copies,
+                down_all.at[i, j],
+                down.at[pl.ds(j * width + i * DOWN_ROWS, DOWN_ROWS)],
+                down_sem,
+            )
+
+    def vector(i):
+        row, at = i // 3, (i % 3) * GROUP
+        return jnp.concatenate(
+            [vec_ref[j, row : row + 1, at : at + GROUP] for j in range(4)], axis=1
+        )
+
+    up_bias = jnp.concatenate(
+        [
+            part
+            for j in range(4)
+            for part in (vec_ref[j, 2:3, 2 * GROUP : 3 * GROUP], vec_ref[j, 3:4, :])
+        ],
+        axis=1,
+    )
+    proj_bias, gain1, bias1, down_bias, gain2, bias2 = [vector(i) for i in range(2, 8)]
+    upb_ref[...] = up_bias
+    for mb in range(2):
+        att_ref[mb * GROUP : (mb + 1) * GROUP, :] = jnp.concatenate(
+            [a_ref[4 * mb + j] for j in range(4)], axis=1
+        )
+    tokens = jnp.concatenate([tok_ref[0], tok_ref[1]], axis=0).astype(jnp.float32)
+    cot = jnp.concatenate([cot_ref[0], cot_ref[1]], axis=0).astype(jnp.float32)
+    keep = keep_ref[...]
+
+    for made in proj_copies:
+        made.wait()
+    mixed = tokens + dot(att_ref[...], proj[...]) + proj_bias
+    normal1, scale1 = norm(mixed)
+    hidden = normal1 * gain1 + bias1
+    hid_ref[...] = hidden.astype(jnp.bfloat16)
+
+    def by_core(value):
+        for i in range(8):
+            at = 4 * ((i & 1) ^ (me & 1)) + (i >> 1)
+            hid_t[pl.ds(pl.multiple_of(at * 96, 96), 96), :] = value[i * 96 : (i + 1) * 96]
+
+    def out_columns(cols, grad):
+        keep_cols[:, cols] = dot(hid_t[0:FF_CUT], grad).astype(jnp.bfloat16)
+        give_cols[:, cols] = dot(hid_t[FF_CUT:], grad).astype(jnp.bfloat16)
+
+    by_core(flip(hid_ref[...]))
+    for made in up_copies:
+        made.wait()
+    for made in down_copies:
+        made.wait()
+
+    def forward(j, branch):
+        cols = pl.ds(pl.multiple_of(j * FF_STEP, FF_STEP), FF_STEP)
+        inner = dot(hid_ref[...], up[:, cols]) + upb_ref[:, cols]
+        share, bell = gelu_parts(inner)
+        slope[:, cols] = share + inner * bell * (1.0 / math.sqrt(2.0 * math.pi))
+        active = (inner * share).astype(jnp.bfloat16)
+        act_ref[:, cols] = active
+        return branch + dot(active, down[cols, :])
+
+    branch = lax.fori_loop(0, 6, forward, jnp.zeros((2 * GROUP, width), jnp.float32))
+    normal2, scale2 = norm(hidden + branch + down_bias)
+    result = normal2 * gain2 + bias2
+    block = (keep * result + (1.0 - keep) * tokens).astype(jnp.bfloat16)
+    block_ref[0] = block[:GROUP]
+    block_ref[1] = block[GROUP:]
+    grad = keep * cot
+    grad_sum = norm_back(grad * gain2, normal2, scale2)
+    grad_branch = grad_sum.astype(jnp.bfloat16)
+    gb_ref[...] = grad_branch
+
+    def add_up(value):
+        return jnp.sum(value, axis=0, keepdims=True)
+
+    sums_ref[3:4, :] = add_up(grad_branch.astype(jnp.float32))
+    sums_ref[4:5, :] = add_up(grad * normal2)
+    sums_ref[5:6, :] = add_up(grad)
+
+    def backward(j, total):
+        cols = pl.ds(pl.multiple_of(j * FF_STEP, FF_STEP), FF_STEP)
+        grad_inner = (dot_nt(gb_ref[...], down[cols, :]) * slope[:, cols]).astype(jnp.bfloat16)
+        out_columns(cols, grad_inner)
+        rows_ref[cols, :] = dot(flip(act_ref[:, cols]), gb_ref[...]).astype(
+            jnp.bfloat16
+        )
+        upb_ref[:, cols] = add_up(grad_inner.astype(jnp.float32))
+        return total + dot_nt(grad_inner, up[:, cols])
+
+    grad_hidden = lax.fori_loop(0, 6, backward, grad_sum)
+    sums_ref[1:2, :] = add_up(grad_hidden * normal1)
+    sums_ref[2:3, :] = add_up(grad_hidden)
+    grad_mixed = norm_back(grad_hidden * gain1, normal1, scale1)
+    base_ref[...] = keep * grad_mixed + (1.0 - keep) * cot
+    grad_proj = grad_mixed.astype(jnp.bfloat16)
+    by_core(flip(att_ref[...]))
+    out_columns(slice(4 * width, 5 * width), grad_proj)
+    sums_ref[0:1, :] = add_up(grad_proj.astype(jnp.float32))
+    sums_ref[6:8, :] = jnp.zeros((2, width), jnp.float32)
+    lane = lax.broadcasted_iota(jnp.int32, (width, 128), 1)
+    vectors = jnp.concatenate(
+        [jnp.transpose(sums_ref[...]), jnp.zeros((width, 120), jnp.float32)], axis=1
+    )
+    column = jnp.transpose(jnp.broadcast_to(upb_ref[...], (8, 4 * width)))[:, 0:1]
+    for j in range(4):
+        part = jnp.concatenate(
+            [column[i * 96 + j * 24 : i * 96 + (j + 1) * 24] for i in range(32)], axis=0
+        )
+        vectors = jnp.where(lane == 6 + j, part, vectors)
+    for i in range(8):
+        at = 4 * ((i & 1) ^ (me & 1)) + (i >> 1)
+        turned[pl.ds(pl.multiple_of(at * 96, 96), 96), :] = vectors[i * 96 : (i + 1) * 96].astype(
+            jnp.bfloat16
+        )
+    keep_cols[:, 5 * width :] = turned[0:FF_CUT]
+    give_cols[:, 5 * width :] = turned[FF_CUT:]
+    grad_att = dot_nt(grad_proj, proj[...]).astype(jnp.bfloat16)
+    for mb in range(2):
+        for j in range(4):
+            ga_ref[4 * mb + j] = grad_att[
+                mb * GROUP : (mb + 1) * GROUP, j * GROUP : (j + 1) * GROUP
+            ]
+
+
+def dense(*ins):
+    rows, width, hidden = 2 * GROUP, 4 * GROUP, 16 * GROUP
+    outs = [
+        ((2, GROUP, width), LOW),
+        ((rows, width), WIDE),
+        ((8, GROUP, GROUP), LOW),
+        ((hidden, width), LOW),
+        ((FF_CUT, COLUMNS), LOW),
+        ((FF_CUT, COLUMNS), LOW),
+    ]
+    scratch = [
+        pltpu.VMEM((width, hidden), LOW),
+        pltpu.VMEM((hidden, width), LOW),
+        pltpu.VMEM((width, width), LOW),
+        pltpu.VMEM((rows, hidden), WIDE),
+        pltpu.VMEM((rows, hidden), LOW),
+        pltpu.VMEM((rows, width), LOW),
+        pltpu.VMEM((rows, width), LOW),
+        pltpu.VMEM((width, rows), LOW),
+        pltpu.VMEM((rows, width), LOW),
+        pltpu.VMEM((8, width), WIDE),
+        pltpu.VMEM((1, hidden), WIDE),
+        pltpu.VMEM((width, 128), LOW),
+        pltpu.SemaphoreType.DMA((25,)),
+        pltpu.SemaphoreType.DMA((33,)),
+        pltpu.SemaphoreType.DMA((32,)),
+    ]
+    return call(dense_kernel, "dense", ins, outs, scratch, any_ins=5, flops=2 * 10**10)
+
+
+def take(value, at, axis):
+    return lax.dynamic_index_in_dim(value, at, axis, keepdims=False)
+
+
+def halve(value, at, axis, send):
+    kept = take(value, at, axis).astype(jnp.float32)
+    return (kept + send(take(value, 1 - at, axis)).astype(jnp.float32)).astype(jnp.bfloat16)
+
+
+def scatter_plane(value, me):
+    across, along = (me >> 1) & 1, me >> 2
+    value = value.reshape(2, 2, 96, COLUMNS)
+    left = halve(value[..., :LEFT], across, 1, lambda v: from_ctx(v, 2))
+    right = halve(value[..., LEFT:], along, 0, lambda v: from_ctx(v, 4))
+    return left, right
+
+
+def scatter_plane_end(left, right, me):
+    across, along = (me >> 1) & 1, me >> 2
+    left = halve(left, along, 0, lambda v: from_ctx(v, 4))
+    right = halve(right, across, 0, lambda v: from_ctx(v, 2))
+    return jnp.concatenate([left, right], axis=1)
+
+
+def scatter_depth(value, depth):
+    return halve(value.reshape(2, 2, 24, value.shape[1]), depth & 1, 1, lambda v: from_fsdp(v, 1))
+
+
+def scatter_depth_end(value, depth):
+    kept = take(value, depth >> 1, 0).astype(jnp.float32)
+    return kept + from_fsdp(take(value, 1 - (depth >> 1), 0), 2).astype(jnp.float32)
+
+
+def fast_on_device(
+    tokens,
+    doc_ids,
+    keep_mask,
+    qkv_weight,
+    query_bias,
+    value_bias,
+    proj_weight,
+    proj_bias,
+    norm1_gain,
+    norm1_bias,
+    up_weight,
+    up_bias,
+    down_weight,
+    down_bias,
+    norm2_gain,
+    norm2_bias,
+    cotangent,
+):
+    low = jnp.bfloat16
+    me = lax.axis_index("ctx")
+    height = me >> 2
+    group = me & 3
+    depth = lax.axis_index("fsdp")
+    place = jnp.stack([me, depth] + [jnp.int32(k) for k in ARRIVAL])
+    rows = tokens[:, 0]
+    ids = doc_ids[:, 0]
+    features = rows.shape[2]
+
+    id_rows = jnp.pad(ids.astype(low)[:, None, :], ((0, 0), (0, ID_ROWS - 1), (0, features - GROUP)))
+    marked = jnp.concatenate([rows, id_rows], axis=1)
+    own = take(marked, height, 0)
+    at = group * GROUP
+    columns = jnp.concatenate(
+        [lax.dynamic_slice_in_dim(qkv_weight, part * features + at, GROUP, 1) for part in range(3)],
+        axis=1,
+    )
+    vectors = jnp.concatenate(
+        [
+            query_bias,
+            value_bias,
+            proj_bias,
+            norm1_gain,
+            norm1_bias,
+            down_bias,
+            norm2_gain,
+            norm2_bias,
+            up_bias,
+        ]
+    ).reshape(4, 3 * GROUP)
+    columns = jnp.concatenate([columns, vectors, jnp.zeros((4, 3 * GROUP), low)], axis=0)
+    came = from_ctx(take(marked, 1 - height, 0), 4)
+    across = from_ctx(own, 2)
+    near, mid = from_fsdp(columns, 1), from_fsdp(columns, 2)
+    own, came, across, near, mid = lax.optimization_barrier((own, came, across, near, mid))
+    far = from_fsdp(columns, 3)
+    four = jnp.stack([own, came, across, from_ctx(came, 2)])
+    four, far = lax.optimization_barrier((four, far))
+    eight = from_ctx(four, 1)
+
+    down_cut = lax.dynamic_slice_in_dim(down_weight, me * DOWN_ROWS, DOWN_ROWS, 0)
+    down_all = lax.all_gather(down_cut, ("ctx", "fsdp"), axis=0).reshape(8, 4, DOWN_ROWS, features)
+    up_cut = lax.dynamic_slice_in_dim(up_weight, me * FF_CUT, FF_CUT, 1)
+    proj_cut = lax.dynamic_slice(
+        proj_weight, ((me >> 1) * PROJ_ROWS, (me & 1) * FF_CUT), (PROJ_ROWS, FF_CUT)
+    )
+    cut = jnp.concatenate([up_cut, proj_cut], axis=0)
+
+    documents = jnp.arange(NDOC, dtype=jnp.int32)
+    keep_rows = jnp.sum(
+        jnp.where(ids[:, :, None] == documents, keep_mask[:, 0][:, None, :], 0), axis=2
+    ).astype(jnp.float32).reshape(2 * GROUP, 1)
+
+    cut, four = lax.optimization_barrier((cut, four))
+    cuts = [from_fsdp(cut, m) for m in (1, 2, 3)]
+    made = project(place, four, eight, columns, near, mid, far)
+    qt, ka = list(made[:3]), made[3:6]
+    vt, qkv_mine, vec = made[6:]
+    ot = [None] * 3
+    turned = qt
+    qt = [None] * 3
+    qt[0], qt[1], ot[0], ot[1] = attend((0, 1), place, *turned[:2], *ka[:2], vt)
+    last, ot[1], *cuts = lax.optimization_barrier((turned[2], ot[1], *cuts))
+    cuts = jnp.concatenate(cuts, axis=0)
+    first, second = cuts[:FIRST], cuts[FIRST:]
+    both = [first, from_ctx(first, 2), second, from_ctx(second, 4)]
+    qt[2], ot[2], o = attend((2,), place, last, ka[2], vt, ot[0], ot[1])
+    o, *both = lax.optimization_barrier((o, *both))
+    first = jnp.concatenate(both[:2], axis=0)
+    second = jnp.concatenate(both[2:], axis=0)
+    first_far, second_far = from_ctx(first, 4), from_ctx(second, 2)
+    held = jnp.concatenate([first, first_far, second, second_far], axis=0)
+    held_too = from_ctx(held, 1)
+    xt, qn, kt, *va, by_head = turn(four, eight, *turned[:2], last, *ka, vt, qkv_mine)
+    heads = lax.all_to_all(o, "ctx", 0, 0, tiled=True)
+    heads, xt, qn, kt, *va, by_head = lax.optimization_barrier((heads, xt, qn, kt, *va, by_head))
+    block_rows, base, grad_heads, grad_down, kept, given = dense(
+        place,
+        heads,
+        rows,
+        cotangent[:, 0],
+        keep_rows,
+        vec,
+        proj_weight,
+        up_weight,
+        down_all,
+        held,
+        held_too,
+    )
+    grad_o = lax.all_to_all(grad_heads, "ctx", 0, 0, tiled=True)
+    down_part = lax.psum_scatter(grad_down, "ctx", scatter_dimension=0, tiled=True)
+    each = features // 32
+    both = (kept.astype(jnp.float32) + from_ctx(given, 1).astype(jnp.float32)).astype(low)
+    grad_o, both = lax.optimization_barrier((grad_o, both))
+    left, right = scatter_plane(both, me)
+    shared = (place, grad_o, kt, qn, xt)
+    sent, grads = attend_back((0, 1), *shared, *ot[:2], *qt[:2], *ka[:2], *va[:2])
+    last, left, right, grads = lax.optimization_barrier((qt[2], left, right, grads))
+    both = scatter_plane_end(left, right, me)
+    came_first = lax.all_to_all(sent, ("ctx", "fsdp"), 0, 0, tiled=True)
+    sent, kept, given, _ = attend_back(
+        (2,), *shared, ot[2], last, ka[2], va[2], grads, by_head
+    )
+    given, both, came_first, down_part = lax.optimization_barrier(
+        (given, both, came_first, down_part)
+    )
+    both = scatter_depth(both, depth)
+    out_down = lax.psum_scatter(down_part, "fsdp", scatter_dimension=0, tiled=True).astype(
+        jnp.float32
+    )
+
+    half = (kept.astype(jnp.float32) + from_ctx(given, 1).astype(jnp.float32)).astype(low)
+    half, sent = lax.optimization_barrier((half, sent))
+    quarter = half[:2].astype(jnp.float32) + from_ctx(half[2:], 2).astype(jnp.float32)
+    quarter, both, out_down = lax.optimization_barrier((quarter, both, out_down))
+    both = scatter_depth_end(both, depth)
+    out_up, out_proj = both[:, : 4 * features], both[:, 4 * features : 5 * features]
+    vectors = both[:, 5 * features :]
+    mine = quarter[0]
+    swapped = from_ctx(quarter[1].astype(low), 4).astype(jnp.float32)
+    first = height == 0
+    back = jnp.concatenate(
+        [jnp.where(first, mine, swapped), jnp.where(first, swapped, mine)], axis=0
+    )
+    grad_tokens = base + keep_rows * back
+
+    came_last = lax.all_to_all(sent, ("ctx", "fsdp"), 0, 0, tiled=True)
+    came = []
+    for value in (came_first, came_last):
+        value = value.reshape(2, 4, 4, 32, -1).astype(jnp.float32)
+        came.append(jnp.sum(value, axis=(0, 2)))
+    came = jnp.concatenate(came, axis=2)
+    out_qkv = came[:, :each].reshape(4, each, HEADS_EACH, 3, HEAD).transpose(1, 3, 0, 2, 4)
+    out_qkv = out_qkv.reshape(each, 3 * features)
+    head_bias = (came[:, each] + came[:, each + 1]).reshape(4, HEADS_EACH, 3, HEAD)
+    at = (4 * me + depth) * each
+    out_query_bias = lax.dynamic_slice_in_dim(head_bias[:, :, 0].reshape(features), at, each)
+    out_value_bias = lax.dynamic_slice_in_dim(head_bias[:, :, 2].reshape(features), at, each)
+
+    return (
+        block_rows.reshape(2, 1, GROUP, features),
+        grad_tokens.reshape(2, 1, GROUP, features),
+        out_qkv,
+        out_query_bias,
+        out_value_bias,
+        out_proj,
+        vectors[:, 0],
+        vectors[:, 1],
+        vectors[:, 2],
+        out_up,
+        vectors[:, 6:10].T.reshape(4 * each),
+        out_down,
+        vectors[:, 3],
+        vectors[:, 4],
+        vectors[:, 5],
+    )
+
+
 def solution(mesh):
     in_specs = (
         P(None, "fsdp", "ctx", None),
@@ -412,6 +1210,7 @@
         P(("ctx", "fsdp")),
         P(("ctx", "fsdp")),
     )
+    work = fast_on_device if fits(mesh) else on_device
     return jax.shard_map(
-        on_device, mesh=mesh, in_specs=in_specs, out_specs=out_specs, check_vma=False
-    )
+        work, mesh=mesh, in_specs=in_specs, out_specs=out_specs, check_vma=False
+    )

time: 1110 us -> 298 us (0.27)
  waiting for transfers between devices: 525 us -> 69 us
  matrix products: 231 us -> 0 us
  blocking collectives: 120 us -> 0 us
  Pallas kernels: 0 us -> 114 us
  local copies, waits for them, and re-layouts: 116 us -> 20 us
  other arithmetic: 85.2 us -> 18.4 us
  starting transfers between devices: 0.99 us -> 61.1 us
    all_gather x12 -> x1, waiting for transfers between devices: 269 us -> 0.01 us  [fast_on_device(): lax.all_gather(down_cut, ('ctx', 'fsdp'), axis=0)]
    dot_general x52 -> x0, matrix products: 231 us -> none  [the longest x4 32.9 us: query_step(): jnp.einsum('hqk,khd->qhd', grad_scores, key_heads, preferred_element_type...]
    unnamed x17 -> x3, waiting for transfers between devices: 129 us -> 0.05 us
    reduce_scatter x3 -> x2, waiting for transfers between devices: 127 us -> 3.82 us  [the longest x1 3.8 us: fast_on_device(): lax.psum_scatter(down_part, 'fsdp', scatter_dimension=0, tiled=True)]
    pallas_call x0 -> x7, Pallas kernels: none -> 114 us  [call(): pl.pallas_call(kernel, name=name, out_shape=[jax.ShapeDtypeStruct(shape,...]
    unnamed x3 -> x0, blocking collectives: 72.1 us -> none
    unnamed x285 -> x58, local copies, waits for them, and re-layouts: 56.7 us -> 3.89 us
    all_gather x5 -> x0, blocking collectives: 47.9 us -> none  [the longest x2 18.4 us: micro_step(): lax.all_gather(jnp.transpose(log_total), 'ctx', axis=0, tiled=True)]
  transfers between devices with their start and end apart: 16 -> 32, of which waited for: 7 -> 15; matrix products, arithmetic and copies ran while one was open for 38% -> 11% of each run, Pallas kernels for 0% -> 26%
where the time goes in v1:
time: 298 us; the launch traced here: 297 us
  Pallas kernels  114 us (38%)
  waiting for transfers between devices  69 us (23%)
  starting transfers between devices  61.1 us (21%)
  local copies, waits for them, and re-layouts  20 us (7%)
  other arithmetic  18.4 us (6%)
  between operations  14.4 us (5%)
    pallas_call x7, Pallas kernels, call(): pl.pallas_call(kernel, name=name, out_shape=[jax.ShapeDtypeStruct(shape,...  114 us
    ppermute x8, waiting for transfers between devices, from_fsdp(): return lax.ppermute(value, 'fsdp', [(i, i ^ bits) for i in range(4)])  29.3 us
    ppermute x8, starting transfers between devices, from_fsdp(): return lax.ppermute(value, 'fsdp', [(i, i ^ bits) for i in range(4)])  18.4 us
    ppermute x17, starting transfers between devices, from_ctx(): return lax.ppermute(value, 'ctx', [(i, i ^ bits) for i in range(8)])  17.1 us
    ppermute x17, waiting for transfers between devices, from_ctx(): return lax.ppermute(value, 'ctx', [(i, i ^ bits) for i in range(8)])  15.9 us
    all_to_all x1, starting transfers between devices, fast_on_device(): came_first = lax.all_to_all(sent, ('ctx', 'fsdp'), 0, 0, tiled=True)  11.2 us
    all_to_all x1, waiting for transfers between devices, fast_on_device(): came_last = lax.all_to_all(sent, ('ctx', 'fsdp'), 0, 0, tiled=True)  8.14 us
    all_to_all x1, waiting for transfers between devices, fast_on_device(): grad_o = lax.all_to_all(grad_heads, 'ctx', 0, 0, tiled=True)  7.56 us
  transfers between devices with their start and end apart: 32, of which 15 were waited for; matrix products, arithmetic and copies ran while one was open for 11% of the time, Pallas kernels for 26%

profile of v1, /device:TPU:0, one launch (start us, length us, event | category | flops | bytes accessed | tf_op | source)
XLA Modules:
  0.0 296.7 jit_solution(957011839423197276)
XLA Ops:
  11.0 3.0 %collective-permute-start.1 = (bf16[200,768]{1,0:T(8,128)(2,1)S(1)}, bf16[200,768]{1,0:T(8,128)(2,1)S(1)}, u32[]{:S(2)}, u32[]{:S(2)}) collective-permute-start(bf16[200,768]{1,0:T(8,128)(2,1)S(1)} %get-tuple-element.91), channel_id=1, source_target_pairs={{0,8},{4,12},{8,0},{12,4},{16,24},{20,28},{24,16},{28,20},{1,9},{5... | collective-permute-start | bytes 921608 | tf_op jit(solution)/shard_map/ppermute | solution.py:694
  18.9 2.6 collective-permute-start.3
  21.5 10.6 %collective-permute-done.2.refs_3_ = bf16[200,576]{1,0:T(8,128)(2,1)S(1)} collective-permute-done((bf16[200,576]{1,0:T(8,128)(2,1)S(1)}, bf16[200,576]{1,0:T(8,128)(2,1)S(1)}, u32[]{:S(2)}, u32[]{:S(2)}) %collective-permute-start.2) | collective-permute-done | bytes 230432 | tf_op jit(solution)/shard_map/ppermute | solution.py:698
  32.1 2.8 collective-permute-done.3.refs_4_
  35.0 6.8 %collective-permute-start.5 = (bf16[200,576]{1,0:T(8,128)(2,1)S(1)}, bf16[200,576]{1,0:T(8,128)(2,1)S(1)}, u32[]{:S(2)}, u32[]{:S(2)}) collective-permute-start(bf16[200,576]{1,0:T(8,128)(2,1)S(1)} %maximum_maximum_fusion.refs_2_), channel_id=1, source_target_pairs={{0,3},{1,2},{2,1},{3,0},{4,7},{5,6},{6,5},{7,4},{8,11},{9,10},{10,... | collective-permute-start | bytes 691208 | tf_op jit(solution)/shard_map/ppermute | solution.py:698
  42.0 5.6 %collective-permute-done.5.refs_5_ = bf16[200,576]{1,0:T(8,128)(2,1)S(1)} collective-permute-done((bf16[200,576]{1,0:T(8,128)(2,1)S(1)}, bf16[200,576]{1,0:T(8,128)(2,1)S(1)}, u32[]{:S(2)}, u32[]{:S(2)}) %collective-permute-start.5) | collective-permute-done | bytes 230432 | tf_op jit(solution)/shard_map/ppermute | solution.py:698
  55.0 6.1 %project.1 = (bf16[128,1536]{1,0:T(8,128)(2,1)}, bf16[128,1536]{1,0:T(8,128)(2,1)}, bf16[128,1536]{1,0:T(8,128)(2,1)}, bf16[1536,128]{1,0:T(8,128)(2,1)}, bf16[1...) custom-call(s32[10]{0:T(128)} %stack.26.place, ...), custom_call_target="tpu_custom_call" | custom-call | flops 5000000000 | bytes 10000000 | tf_op jit(solution)/shard_map/project/pallas_call | solution.py:416
  61.1 11.1 %attend0.1 = (bf16[128,1536]{1,0:T(8,128)(2,1)}, bf16[128,1536]{1,0:T(8,128)(2,1)}, bf16[64,1536]{1,0:T(8,128)(2,1)}, bf16[64,1536]{1,0:T(8,128)(2,1)}) custom-call(s32[10]{0:T(128)} %stack.26.place, bf16[128,1536]{1,0:T(8,128)(2,1)} %get-tuple-element.100.refs_0_.refs_2_, bf16[128,1536]{1,0:T(8,128)(2,1)} %get-tuple-element.101.refs_1_.refs_3_, ...), custom_call_target="tpu_custom_call" | custom-call | flops 5000000000 | bytes 10000000 | tf_op jit(solution)/shard_map/attend0/pallas_call | solution.py:416
  75.7 9.1 %attend2.1 = (bf16[128,1536]{1,0:T(8,128)(2,1)}, bf16[64,1536]{1,0:T(8,128)(2,1)}, bf16[8,192,192]{2,1,0:T(8,128)(2,1)}) custom-call(s32[10]{0:T(128)} %stack.26.place, bf16[128,1536]{1,0:T(8,128)(2,1)} %get-tuple-element.107.refs_0_.refs_4_, bf16[1536,128]{1,0:T(8,128)(2,1)} %get-tuple-element.108.refs_1_.refs_7_.refs_6_, ...), custom_call_target="tpu_custom_call" | custom-call | flops 5000000000 | bytes 10000000 | tf_op jit(solution)/shard_map/attend2/pallas_call | solution.py:416
  87.1 11.8 %collective-permute-done.12 = bf16[736,384]{1,0:T(8,128)(2,1)S(1)} collective-permute-done((bf16[736,384]{1,0:T(8,128)(2,1)S(1)}, bf16[736,384]{1,0:T(8,128)(2,1)S(1)}, u32[]{:S(2)}, u32[]{:S(2)}) %collective-permute-start.12) | collective-permute-done | bytes 565280 | tf_op jit(solution)/shard_map/ppermute | solution.py:694
  100.2 3.6 %all-to-all-start = ((bf16[8,192,192]{2,1,0:T(8,128)(2,1)}), bf16[8,192,192]{2,1,0:T(8,128)(2,1)S(1)}, u32[]{:S(2)}, u32[]{:S(2)}) async-start(bf16[8,192,192]{2,1,0:T(8,128)(2,1)} %get-tuple-element.115), calls=%async_computation | async-start | bytes 1572864 | tf_op jit(solution)/shard_map/all_to_all | solution.py:1092
  105.0 7.0 %turn.1 = (bf16[768,1536]{1,0:T(8,128)(2,1)}, bf16[1536,192]{1,0:T(8,128)(2,1)}, bf16[192,1536]{1,0:T(8,128)(2,1)}, bf16[1536,128]{1,0:T(8,128)(2,1)}, bf16[1536...) custom-call(bf16[4,200,768]{2,1,0:T(8,128)(2,1)} %copy-done.6, ...), custom_call_target="tpu_custom_call" | custom-call | flops 5000000000 | bytes 10000000 | tf_op jit(solution)/shard_map/turn/pallas_call | solution.py:416
  112.0 4.3 %all-to-all-done.refs_0_ = bf16[8,192,192]{2,1,0:T(8,128)(2,1)S(1)} async-done(((bf16[8,192,192]{2,1,0:T(8,128)(2,1)}), bf16[8,192,192]{2,1,0:T(8,128)(2,1)S(1)}, u32[]{:S(2)}, u32[]{:S(2)}) %all-to-all-start) | async-done | bytes 589856 | tf_op jit(solution)/shard_map/all_to_all | solution.py:1092
  117.3 37.1 %dense.1 = (bf16[2,192,768]{2,1,0:T(8,128)(2,1)}, f32[384,768]{1,0:T(8,128)}, bf16[8,192,192]{2,1,0:T(8,128)(2,1)}, bf16[3072,768]{1,0:T(8,128)(2,1)}, bf16[384,...) custom-call(s32[10]{0:T(128)} %stack.26.place, bf16[8,192,192]{2,1,0:T(8,128)(2,1)} %copy-done.8, ...), custom_call_target="tpu_custom_call" | custom-call | flops 20000000000 | bytes 10000000 | tf_op jit(solution)/shard_map/dense/pallas_call | solution.py:416
  154.5 4.5 %all-to-all-start.1 = ((bf16[8,192,192]{2,1,0:T(8,128)(2,1)}), bf16[8,192,192]{2,1,0:T(8,128)(2,1)}, u32[]{:S(2)}, u32[]{:S(2)}) async-start(bf16[8,192,192]{2,1,0:T(8,128)(2,1)} %get-tuple-element.132), calls=%async_computation.1 | async-start | bytes 1572864 | tf_op jit(solution)/shard_map/all_to_all | solution.py:1107
  160.3 3.5 %add_convert_fusion = bf16[384,3968]{1,0:T(8,128)(2,1)S(1)} fusion(bf16[384,3968]{1,0:T(8,128)(2,1)} %collective-permute-done.15, bf16[384,3968]{1,0:T(8,128)(2,1)} %get-tuple-element.133), kind=kLoop, calls=%fused_computation | loop fusion | flops 6094848 | bytes 9142272 | tf_op jit(solution)/shard_map/convert_element_type | solution.py:1110
  163.8 7.6 %all-to-all-done.1.refs_0_ = bf16[8,192,192]{2,1,0:T(8,128)(2,1)} async-done(((bf16[8,192,192]{2,1,0:T(8,128)(2,1)}), bf16[8,192,192]{2,1,0:T(8,128)(2,1)}, u32[]{:S(2)}, u32[]{:S(2)}) %all-to-all-start.1) | async-done | bytes 589856 | tf_op jit(solution)/shard_map/all_to_all | solution.py:1107
  175.7 25.3 %attend_back0.1 = (bf16[32,32,384]{2,1,0:T(8,128)(2,1)}, bf16[1536,384]{1,0:T(8,128)(2,1)}) custom-call(s32[10]{0:T(128)} %stack.26.place, bf16[8,192,192]{2,1,0:T(8,128)(2,1)} %all-to-all-done.1.refs_0_, bf16[192,1536]{1,0:T(8,128)(2,1)} %get-tuple-element.136.refs_1_, bf16[1536,192]{1,0:T(8,128)(2,1)} %get-tuple-element.137.refs_2_, ...), custom_call_target="tpu_custom_call" | custom-call | flops 10000000000 | bytes 10000000 | tf_op jit(solution)/shard_map/attend_back0/pallas_call | solution.py:416
  201.1 11.2 %all-to-all-start.2 = ((bf16[32,32,384]{2,1,0:T(8,128)(2,1)}), bf16[32,32,384]{2,1,0:T(8,128)(2,1)}, u32[]{:S(2)}, u32[]{:S(2)}) async-start(bf16[32,32,384]{2,1,0:T(8,128)(2,1)} %get-tuple-element.155), calls=%async_computation.2 | async-start | bytes 1572864 | tf_op jit(solution)/shard_map/all_to_all | solution.py:1117
  218.7 18.1 %attend_back2.1 = (bf16[32,32,192]{2,1,0:T(8,128)(2,1)}, bf16[4,192,768]{2,1,0:T(8,128)(2,1)}, bf16[4,192,768]{2,1,0:T(8,128)(2,1)}, bf16[1536,192]{1,0:T(8,128)(2,1)}) custom-call(s32[10]{0:T(128)} %stack.26.place, bf16[8,192,192]{2,1,0:T(8,128)(2,1)} %all-to-all-done.1.refs_0_, bf16[192,1536]{1,0:T(8,128)(2,1)} %get-tuple-element.136.refs_1_, ...), custom_call_target="tpu_custom_call" | custom-call | flops 10000000000 | bytes 10000000 | tf_op jit(solution)/shard_map/attend_back2/pallas_call | solution.py:416
  245.7 8.6 %collective-permute-done.22 = bf16[2,24,3968]{2,1,0:T(8,128)(2,1)S(1)} collective-permute-done((bf16[2,24,3968]{2,1,0:T(8,128)(2,1)S(1)}, bf16[2,24,3968]{2,1,0:T(8,128)(2,1)S(1)}, u32[]{:S(2)}, u32[]{:S(2)}) %collective-permute-start.22) | collective-permute-done | bytes 380960 | tf_op jit(solution)/shard_map/ppermute | solution.py:698
  254.3 6.2 %all-to-all-start.3 = ((bf16[32,32,192]{2,1,0:T(8,128)(2,1)}), bf16[32,32,192]{2,1,0:T(8,128)(2,1)S(1)}, u32[]{:S(2)}, u32[]{:S(2)}) async-start(bf16[32,32,192]{2,1,0:T(8,128)(2,1)} %get-tuple-element.164), calls=%async_computation.5 | async-start | bytes 1048576 | tf_op jit(solution)/shard_map/all_to_all | solution.py:1144
  260.5 3.8 %reduce-scatter.5.cloned.1.call-done = bf16[96,768]{1,0:T(8,128)(2,1)} async-done(((bf16[384,768]{1,0:T(8,128)(2,1)}), bf16[96,768]{1,0:T(8,128)(2,1)}) %reduce-scatter.5.cloned.1.call-update) | async-done | bytes 147472 | tf_op jit(solution)/shard_map/reduce_scatter | solution.py:1125
  270.8 8.1 %all-to-all-done.3 = bf16[32,32,192]{2,1,0:T(8,128)(2,1)S(1)} async-done(((bf16[32,32,192]{2,1,0:T(8,128)(2,1)}), bf16[32,32,192]{2,1,0:T(8,128)(2,1)S(1)}, u32[]{:S(2)}, u32[]{:S(2)}) %all-to-all-start.3) | async-done | bytes 393248 | tf_op jit(solution)/shard_map/all_to_all | solution.py:1144
  (174 shorter events, 64.1 us)
Async XLA Ops:
  7.3 109.0 %all-gather.3.cloned.1.call-start = ((), (), s32[]{:S(2)}) async-start(), calls=%async_computation.8 | async-start | bytes 4866048 | tf_op jit(solution)/shard_map/all_gather | solution.py:1059
  11.0 23.9 %collective-permute-start.1 = (bf16[200,768]{1,0:T(8,128)(2,1)S(1)}, bf16[200,768]{1,0:T(8,128)(2,1)S(1)}, u32[]{:S(2)}, u32[]{:S(2)}) collective-permute-start(bf16[200,768]{1,0:T(8,128)(2,1)S(1)} %get-tuple-element.91), channel_id=1, source_target_pairs={{0,8},{4,12},{8,0},{12,4},{16,24},{20,28},{24,16},{28,20},{1,9},{5... | collective-permute-start | bytes 921608 | tf_op jit(solution)/shard_map/ppermute | solution.py:694
  14.0 20.9 %collective-permute-start = (bf16[200,768]{1,0:T(8,128)(2,1)S(1)}, bf16[200,768]{1,0:T(8,128)(2,1)S(1)}, u32[]{:S(2)}, u32[]{:S(2)}) collective-permute-start(bf16[200,768]{1,0:T(8,128)(2,1)S(1)} %get-tuple-element.240), channel_id=1, source_target_pairs={{0,16},{4,20},{8,24},{12,28},{16,0},{20,4},{24,8},{28,12},{1,17},{... | collective-permute-start | bytes 921608 | tf_op jit(solution)/shard_map/ppermute | solution.py:694
  17.3 14.8 %collective-permute-start.2 = (bf16[200,576]{1,0:T(8,128)(2,1)S(1)}, bf16[200,576]{1,0:T(8,128)(2,1)S(1)}, u32[]{:S(2)}, u32[]{:S(2)}) collective-permute-start(bf16[200,576]{1,0:T(8,128)(2,1)S(1)} %maximum_maximum_fusion.refs_2_), channel_id=1, source_target_pairs={{0,1},{1,0},{2,3},{3,2},{4,5},{5,4},{6,7},{7,6},{8,9},{9,8},{10,11... | collective-permute-start | bytes 691208 | tf_op jit(solution)/shard_map/ppermute | solution.py:698
  18.9 16.0 %collective-permute-start.3 = (bf16[200,576]{1,0:T(8,128)(2,1)S(1)}, bf16[200,576]{1,0:T(8,128)(2,1)S(1)}, u32[]{:S(2)}, u32[]{:S(2)}) collective-permute-start(bf16[200,576]{1,0:T(8,128)(2,1)S(1)} %maximum_maximum_fusion.refs_2_), channel_id=1, source_target_pairs={{0,2},{1,3},{2,0},{3,1},{4,6},{5,7},{6,4},{7,5},{8,10},{9,11},{10,... | collective-permute-start | bytes 691208 | tf_op jit(solution)/shard_map/ppermute | solution.py:698
  50.0 22.2 %collective-permute-start.7 = (bf16[240,384]{1,0:T(8,128)(2,1)S(1)}, bf16[240,384]{1,0:T(8,128)(2,1)S(1)}, u32[]{:S(2)}, u32[]{:S(2)}) collective-permute-start(bf16[240,384]{1,0:T(8,128)(2,1)S(1)} %pad_maximum_fusion.6), channel_id=1, source_target_pairs={{0,1},{1,0},{2,3},{3,2},{4,5},{5,4},{6,7},{7,6},{8,9},{9,8},{10,11... | collective-permute-start | bytes 552968 | tf_op jit(solution)/shard_map/ppermute | solution.py:698
  52.6 19.7 %collective-permute-start.8 = (bf16[240,384]{1,0:T(8,128)(2,1)S(1)}, bf16[240,384]{1,0:T(8,128)(2,1)S(1)}, u32[]{:S(2)}, u32[]{:S(2)}) collective-permute-start(bf16[240,384]{1,0:T(8,128)(2,1)S(1)} %pad_maximum_fusion.6), channel_id=1, source_target_pairs={{0,2},{1,3},{2,0},{3,1},{4,6},{5,7},{6,4},{7,5},{8,10},{9,11},{10,... | collective-permute-start | bytes 552968 | tf_op jit(solution)/shard_map/ppermute | solution.py:698
  55.0 17.3 %collective-permute-start.9 = (bf16[240,384]{1,0:T(8,128)(2,1)S(1)}, bf16[240,384]{1,0:T(8,128)(2,1)S(1)}, u32[]{:S(2)}, u32[]{:S(2)}) collective-permute-start(bf16[240,384]{1,0:T(8,128)(2,1)S(1)} %pad_maximum_fusion.6), channel_id=1, source_target_pairs={{0,3},{1,2},{2,1},{3,0},{4,7},{5,6},{6,5},{7,4},{8,11},{9,10},{10,... | collective-permute-start | bytes 552968 | tf_op jit(solution)/shard_map/ppermute | solution.py:698
  84.8 14.1 %collective-permute-start.12 = (bf16[736,384]{1,0:T(8,128)(2,1)S(1)}, bf16[736,384]{1,0:T(8,128)(2,1)S(1)}, u32[]{:S(2)}, u32[]{:S(2)}) collective-permute-start(bf16[736,384]{1,0:T(8,128)(2,1)S(1)} %pad_maximum_fusion.2), channel_id=1, source_target_pairs={{0,16},{4,20},{8,24},{12,28},{16,0},{20,4},{24,8},{28,12},{1,17},{... | collective-permute-start | bytes 1695752 | tf_op jit(solution)/shard_map/ppermute | solution.py:694
  100.1 16.2 %collective-permute-start.14 = (bf16[2880,384]{1,0:T(8,128)(2,1)S(1)}, bf16[2880,384]{1,0:T(8,128)(2,1)}, u32[]{:S(2)}, u32[]{:S(2)}) collective-permute-start(bf16[2880,384]{1,0:T(8,128)(2,1)S(1)} %constant_dynamic-update-slice_fusion.refs_8_), channel_id=1, source_target_pairs={{0,4},{4,0},{8,12},{12,8},{16,20},{20,16},{24,28},{28,24},{1,5},{5... | collective-permute-start | bytes 6635528 | tf_op jit(solution)/shard_map/ppermute | solution.py:694
  100.2 16.1 %all-to-all-start = ((bf16[8,192,192]{2,1,0:T(8,128)(2,1)}), bf16[8,192,192]{2,1,0:T(8,128)(2,1)S(1)}, u32[]{:S(2)}, u32[]{:S(2)}) async-start(bf16[8,192,192]{2,1,0:T(8,128)(2,1)} %get-tuple-element.115), calls=%async_computation | async-start | bytes 1572864 | tf_op jit(solution)/shard_map/all_to_all | solution.py:1092
  103.8 135.1 %reduce-scatter.3.cloned.1.call-start = ((), (), s32[]{:S(2)}) async-start(), calls=%async_computation.6 | async-start | bytes 5308416 | tf_op jit(solution)/shard_map/reduce_scatter | solution.py:1108
  154.5 16.9 %all-to-all-start.1 = ((bf16[8,192,192]{2,1,0:T(8,128)(2,1)}), bf16[8,192,192]{2,1,0:T(8,128)(2,1)}, u32[]{:S(2)}, u32[]{:S(2)}) async-start(bf16[8,192,192]{2,1,0:T(8,128)(2,1)} %get-tuple-element.132), calls=%async_computation.1 | async-start | bytes 1572864 | tf_op jit(solution)/shard_map/all_to_all | solution.py:1107
  173.6 38.7 %collective-permute-start.17 = (bf16[2,96,1920]{2,1,0:T(8,128)(2,1)}, bf16[2,96,1920]{2,1,0:T(8,128)(2,1)}, u32[]{:S(2)}, u32[]{:S(2)}) collective-permute-start(bf16[2,96,1920]{2,1,0:T(8,128)(2,1)} %dynamic-slice_bitcast_fusion.1), channel_id=1, source_target_pairs={{0,16},{4,20},{8,24},{12,28},{16,0},{20,4},{24,8},{28,12},{1,17},{... | collective-permute-start | bytes 2211848 | tf_op jit(solution)/shard_map/ppermute | solution.py:694
  175.1 38.6 %collective-permute-start.16 = (bf16[2,96,2048]{2,1,0:T(8,128)(2,1)}, bf16[2,96,2048]{2,1,0:T(8,128)(2,1)}, u32[]{:S(2)}, u32[]{:S(2)}) collective-permute-start(bf16[2,96,2048]{2,1,0:T(8,128)(2,1)} %dynamic-slice_bitcast_fusion), channel_id=1, source_target_pairs={{0,8},{4,12},{8,0},{12,4},{16,24},{20,28},{24,16},{28,20},{1,9},{5... | collective-permute-start | bytes 2359304 | tf_op jit(solution)/shard_map/ppermute | solution.py:694
  201.1 37.8 %all-to-all-start.2 = ((bf16[32,32,384]{2,1,0:T(8,128)(2,1)}), bf16[32,32,384]{2,1,0:T(8,128)(2,1)}, u32[]{:S(2)}, u32[]{:S(2)}) async-start(bf16[32,32,384]{2,1,0:T(8,128)(2,1)} %get-tuple-element.155), calls=%async_computation.2 | async-start | bytes 1572864 | tf_op jit(solution)/shard_map/all_to_all | solution.py:1117
  212.3 52.0 %reduce-scatter.5.cloned.1.call-start = ((), (), s32[]{:S(2)}) async-start(), calls=%async_computation.7 | async-start | bytes 737280 | tf_op jit(solution)/shard_map/reduce_scatter | solution.py:1125
  215.3 23.3 %collective-permute-start.18 = (bf16[96,2048]{1,0:T(8,128)(2,1)S(1)}, bf16[96,2048]{1,0:T(8,128)(2,1)S(1)}, u32[]{:S(2)}, u32[]{:S(2)}) collective-permute-start(bf16[96,2048]{1,0:T(8,128)(2,1)S(1)} %dynamic-slice_bitcast_fusion.2), channel_id=1, source_target_pairs={{0,16},{4,20},{8,24},{12,28},{16,0},{20,4},{24,8},{28,12},{1,17},{... | collective-permute-start | bytes 1179656 | tf_op jit(solution)/shard_map/ppermute | solution.py:694
  217.1 20.5 %collective-permute-start.19 = (bf16[96,1920]{1,0:T(8,128)(2,1)S(1)}, bf16[96,1920]{1,0:T(8,128)(2,1)S(1)}, u32[]{:S(2)}, u32[]{:S(2)}) collective-permute-start(bf16[96,1920]{1,0:T(8,128)(2,1)S(1)} %dynamic-slice_bitcast_fusion.4), channel_id=1, source_target_pairs={{0,8},{4,12},{8,0},{12,4},{16,24},{20,28},{24,16},{28,20},{1,9},{5... | collective-permute-start | bytes 1105928 | tf_op jit(solution)/shard_map/ppermute | solution.py:694
  239.2 15.0 %collective-permute-start.22 = (bf16[2,24,3968]{2,1,0:T(8,128)(2,1)S(1)}, bf16[2,24,3968]{2,1,0:T(8,128)(2,1)S(1)}, u32[]{:S(2)}, u32[]{:S(2)}) collective-permute-start(bf16[2,24,3968]{2,1,0:T(8,128)(2,1)S(1)} %dynamic-slice_bitcast_fusion.3), channel_id=1, source_target_pairs={{0,1},{1,0},{2,3},{3,2},{4,5},{5,4},{6,7},{7,6},{8,9},{9,8},{10,11... | collective-permute-start | bytes 1142792 | tf_op jit(solution)/shard_map/ppermute | solution.py:698
  244.8 21.1 %collective-permute-start.21 = (bf16[2,192,768]{2,1,0:T(8,128)(2,1)}, bf16[2,192,768]{2,1,0:T(8,128)(2,1)}, u32[]{:S(2)}, u32[]{:S(2)}) collective-permute-start(bf16[2,192,768]{2,1,0:T(8,128)(2,1)} %slice.82), channel_id=1, source_target_pairs={{0,8},{4,12},{8,0},{12,4},{16,24},{20,28},{24,16},{28,20},{1,9},{5... | collective-permute-start | bytes 1769480 | tf_op jit(solution)/shard_map/ppermute | solution.py:694
  254.3 24.6 %all-to-all-start.3 = ((bf16[32,32,192]{2,1,0:T(8,128)(2,1)}), bf16[32,32,192]{2,1,0:T(8,128)(2,1)S(1)}, u32[]{:S(2)}, u32[]{:S(2)}) async-start(bf16[32,32,192]{2,1,0:T(8,128)(2,1)} %get-tuple-element.164), calls=%async_computation.5 | async-start | bytes 1048576 | tf_op jit(solution)/shard_map/all_to_all | solution.py:1144
  267.8 15.9 %collective-permute-start.24 = (bf16[24,3968]{1,0:T(8,128)(2,1)}, bf16[24,3968]{1,0:T(8,128)(2,1)}, u32[]{:S(2)}, u32[]{:S(2)}) collective-permute-start(bf16[24,3968]{1,0:T(8,128)(2,1)} %dynamic-slice_bitcast_fusion.7), channel_id=1, source_target_pairs={{0,2},{1,3},{2,0},{3,1},{4,6},{5,7},{6,4},{7,5},{8,10},{9,11},{10,... | collective-permute-start | bytes 571400 | tf_op jit(solution)/shard_map/ppermute | solution.py:698
  269.3 18.3 %collective-permute-start.23 = (bf16[192,768]{1,0:T(8,128)(2,1)}, bf16[192,768]{1,0:T(8,128)(2,1)}, u32[]{:S(2)}, u32[]{:S(2)}) collective-permute-start(bf16[192,768]{1,0:T(8,128)(2,1)} %fusion.8), channel_id=1, source_target_pairs={{0,16},{4,20},{8,24},{12,28},{16,0},{20,4},{24,8},{28,12},{1,17},{... | collective-permute-start | bytes 884744 | tf_op jit(solution)/shard_map/ppermute | solution.py:694
  (34 other events, 289.5 us)
Sparse Core Ops, SparseCore 0:
  10.9 76.0 all-gather.2
  154.6 83.1 reduce-scatter.2
  240.9 23.3 reduce-scatter.4

commit v2 on v1

--- a/solution.py
+++ b/solution.py
@@ -504,39 +504,43 @@
 def attend_kernel(heads, place, *refs):
     n = len(heads)
     qt_refs, ka_refs, vt_ref = refs[:n], refs[n : 2 * n], refs[2 * n]
-    last = heads[-1] == HEADS_EACH - 1
-    earlier = refs[2 * n + 1 : 3 * n + 1] if not last else refs[2 * n + 1 : 2 * n + 3]
-    refs = refs[2 * n + 1 + (len(earlier) if last else 0) :]
-    out_qt, out_ot = refs[:n], refs[n : 2 * n]
-    o_ref = refs[2 * n] if last else None
-    held = refs[-1]
+    refs = refs[2 * n + 1 :]
+    out_qt, out_ot, o_ref = refs[:n], refs[n : 2 * n], refs[2 * n]
+    held = refs[-n:]
     me = place[0]
     at_row = lax.broadcasted_iota(jnp.int32, (16, TILE), 0)
 
     def one_tile(t, unused):
         here = pl.ds(pl.multiple_of(t * TILE, TILE), TILE)
-        tops = []
+        top = [jnp.full((8, TILE), LOWEST, jnp.float32)] * n
+        total = [jnp.zeros((8, TILE), jnp.float32)] * n
+        out = [jnp.zeros((HEAD, TILE), jnp.float32)] * n
+
+        def score(i, j):
+            span = slice(j * TILE, (j + 1) * TILE)
+            scores = dot(ka_refs[i][span, :], qt_refs[i][:, here])
+            held[i][span, :] = scores
+            top[i] = jnp.maximum(top[i], jnp.max(scores.reshape(TILE // 8, 8, TILE), axis=0))
+
+        def mix(i, j):
+            span = slice(j * TILE, (j + 1) * TILE)
+            h = heads[i]
+            probs = jnp.exp(held[i][span, :] - top[i])
+            total[i] = total[i] + jnp.sum(probs.reshape(TILE // 8, 8, TILE), axis=0)
+            low = probs.astype(jnp.bfloat16)
+            out[i] = out[i] + dot(vt_ref[h * HEAD : (h + 1) * HEAD, span], low)
+
         for i in range(n):
-            q_tile = qt_refs[i][:, here]
-            top = jnp.full((8, TILE), LOWEST, jnp.float32)
             for j in range(TILES):
-                span = slice(j * TILE, (j + 1) * TILE)
-                scores = dot(ka_refs[i][span, :], q_tile)
-                held[i, span, :] = scores
-                top = jnp.maximum(top, jnp.max(scores.reshape(TILE // 8, 8, TILE), axis=0))
-            tops.append(jnp.max(top, axis=0, keepdims=True))
-        for i, h in enumerate(heads):
-            rows = slice(h * HEAD, (h + 1) * HEAD)
-            total = jnp.zeros((8, TILE), jnp.float32)
-            out = jnp.zeros((HEAD, TILE), jnp.float32)
+                score(i, j)
+            top[i] = jnp.max(top[i], axis=0, keepdims=True)
+        for i in range(n):
             for j in range(TILES):
-                span = slice(j * TILE, (j + 1) * TILE)
-                probs = jnp.exp(held[i, span, :] - tops[i])
-                total = total + jnp.sum(probs.reshape(TILE // 8, 8, TILE), axis=0)
-                out = out + dot(vt_ref[rows, span], probs.astype(jnp.bfloat16))
-            total = jnp.sum(total, axis=0, keepdims=True)
-            out_ot[i][:, here] = (out / total).astype(jnp.bfloat16)
-            high, mid, low = split3(tops[i] + jnp.log(total))
+                mix(i, j)
+        for i in range(n):
+            sums = jnp.sum(total[i], axis=0, keepdims=True)
+            out_ot[i][:, here] = (out[i] / sums).astype(jnp.bfloat16)
+            high, mid, low = split3(top[i] + jnp.log(sums))
             side = qt_refs[i][HEAD : HEAD + 16, here].astype(jnp.float32)
             side = jnp.where(at_row == 5, high, side)
             side = jnp.where(at_row == 6, mid, side)
@@ -547,15 +551,11 @@
         return unused
 
     lax.fori_loop(0, TILES, one_tile, 0)
-    if last:
-        for t in range(4):
-            span = slice(t * PAIR, (t + 1) * PAIR)
-            whole = jnp.concatenate(
-                [ref[:, span] for ref in (*earlier, *out_ot)], axis=0
-            )
-            rows = flip(whole)
-            for half in range(2):
-                o_ref[me ^ ARRIVAL[2 * t + half]] = rows[half * GROUP : (half + 1) * GROUP, :]
+    for t in range(4):
+        span = slice(t * PAIR, (t + 1) * PAIR)
+        rows = flip(jnp.concatenate([ref[:, span] for ref in out_ot], axis=0))
+        for half in range(2):
+            o_ref[me ^ ARRIVAL[2 * t + half]] = rows[half * GROUP : (half + 1) * GROUP, :]
 
 
 def attend_back_kernel(heads, place, *refs):
@@ -649,6 +649,23 @@
             back_ref[at + 1] = part[GROUP:]
 
 
+def collect_kernel(first_ref, last_ref, out_ref, bias_ref):
+    for g in range(4):
+        for ref, heads in ((first_ref, (0, 1)), (last_ref, (2,))):
+            total = sum(
+                ref[16 * y + 4 * g + z].astype(jnp.float32) for y in range(2) for z in range(4)
+            )
+            for i, h in enumerate(heads):
+                for part in range(3):
+                    at = i * GROUP + part * HEAD
+                    to = g * GROUP + h * HEAD
+                    piece = total[:, at : at + HEAD]
+                    out_ref[:, part * 4 * GROUP + to : part * 4 * GROUP + to + HEAD] = piece[0:24]
+                    if part != 1:
+                        row = part // 2
+                        bias_ref[row : row + 1, to : to + HEAD] = piece[24:25] + piece[25:26]
+
+
 LOW, WIDE = jnp.bfloat16, jnp.float32
 
 
@@ -668,9 +685,8 @@
 def attend(heads, *ins):
     n = len(heads)
     outs = [((2 * HEAD, SLOTS), LOW)] * n + [((HEAD, SLOTS), LOW)] * n
-    if heads[-1] == HEADS_EACH - 1:
-        outs.append(((8, GROUP, GROUP), LOW))
-    scratch = [pltpu.VMEM((n, SLOTS, TILE), WIDE)]
+    outs.append(((8, GROUP, GROUP), LOW))
+    scratch = [pltpu.VMEM((SLOTS, TILE), WIDE)] * n
     kernel = functools.partial(attend_kernel, heads)
     return call(kernel, f"attend{heads[0]}", ins, outs, scratch)
 
@@ -690,6 +706,11 @@
     return call(kernel, f"attend_back{heads[0]}", ins, outs, scratch, flops=10**10)
 
 
+def collect(*ins):
+    outs = [((24, 12 * GROUP), WIDE), ((2, 4 * GROUP), WIDE)]
+    return call(collect_kernel, "collect", ins, outs, scalars=0, flops=10**6)
+
+
 def from_ctx(value, bits):
     return lax.ppermute(value, "ctx", [(i, i ^ bits) for i in range(8)])
 
@@ -701,9 +722,7 @@
 FF_CUT = 384
 PROJ_ROWS = 48
 DOWN_ROWS = 96
-PIECE = 240
-FIRST = 368
-SECOND = 3 * PIECE - FIRST
+CUT_ROWS = 432
 COLUMNS = 3968
 LEFT = 2048
 
@@ -752,11 +771,10 @@
 
 def dense_kernel(place, *refs):
     a_ref, tok_ref, cot_ref, keep_ref, vec_ref = refs[:5]
-    proj_own, up_own, down_all = refs[5:8]
-    shared = refs[8:10]
-    block_ref, base_ref, ga_ref, rows_ref, keep_cols, give_cols = refs[10:16]
-    up, down, proj, slope, act_ref, att_ref, hid_ref, hid_t, gb_ref = refs[16:25]
-    sums_ref, upb_ref, turned, proj_sem, up_sem, down_sem = refs[25:]
+    proj_own, up_own, down_own, gathered = refs[5:9]
+    block_ref, base_ref, ga_ref, rows_ref, keep_cols, give_cols = refs[9:15]
+    up, down, proj, slope, act_ref, att_ref, hid_ref, hid_t, gb_ref = refs[15:24]
+    sums_ref, upb_ref, turned, ordered, even, odd, branch, proj_sem, up_sem, down_sem = refs[24:]
     me, depth = place[0], place[1]
     width = 4 * GROUP
     proj_copies, up_copies, down_copies = [], [], []
@@ -766,51 +784,38 @@
         made.start()
         into.append(made)
 
-    def spot(k, m, up_row=0):
-        owner = me ^ k
-        return (
-            pl.ds(pl.multiple_of((depth ^ m) * GROUP + up_row, 64), GROUP - up_row),
-            pl.ds(pl.multiple_of(owner * FF_CUT, FF_CUT), FF_CUT),
-        )
-
-    def proj_spot(k, m):
-        owner = me ^ k
-        at = (depth ^ m) * GROUP + (owner >> 1) * PROJ_ROWS
-        return (
-            pl.ds(pl.multiple_of(at, PROJ_ROWS), PROJ_ROWS),
-            pl.ds(pl.multiple_of((owner & 1) * FF_CUT, FF_CUT), FF_CUT),
-        )
-
-    own_rows = pl.ds(pl.multiple_of(depth * GROUP, GROUP), GROUP)
-    starts = []
-    for core in range(2):
-        for i in range(4):
-            starts.append((core, core ^ (0, 2, 4, 6)[i], i * FIRST, core ^ (0, 4, 2, 6)[i], 4 * FIRST + i * SECOND))
-    copy(proj_copies, proj_own, proj.at[own_rows], proj_sem)
-    for core, k_first, first, k_second, second in starts:
-        source = shared[core]
-        for k, m, at in (
-            (k_first, 1, first + GROUP),
-            (k_second, 2, second + 64),
-            (k_second, 3, second + 64 + PROJ_ROWS + GROUP),
-        ):
-            copy(proj_copies, source.at[pl.ds(at, PROJ_ROWS)], proj.at[proj_spot(k, m)], proj_sem)
-    copy(up_copies, up_own, up.at[own_rows], up_sem)
-    for core, k_first, first, k_second, second in starts:
-        source = shared[core]
-        copy(up_copies, source.at[pl.ds(first, GROUP)], up.at[spot(k_first, 1)], up_sem)
-        rows, cols = spot(k_first, 2)
-        rows = pl.ds(pl.multiple_of((depth ^ 2) * GROUP, GROUP), 128)
-        copy(up_copies, source.at[pl.ds(first + PIECE, 128)], up.at[rows, cols], up_sem)
-        copy(up_copies, source.at[pl.ds(second, 64)], up.at[spot(k_second, 2, 128)], up_sem)
-        at = second + 64 + PROJ_ROWS
-        copy(up_copies, source.at[pl.ds(at, GROUP)], up.at[spot(k_second, 3)], up_sem)
-    for i in range(8):
-        for j in range(4):
+    def owner_rows(m, size, at, rows):
+        return pl.ds(pl.multiple_of((depth ^ m) * size + at, PROJ_ROWS), rows)
+
+    every = [(i, m) for i in range(8) for m in (1, 2, 3)]
+    copy(proj_copies, proj_own, proj.at[owner_rows(0, GROUP, 0, GROUP)], proj_sem)
+    for i, m in every:
+        copy(
+            proj_copies,
+            gathered.at[i, m - 1, pl.ds(CUT_ROWS - PROJ_ROWS, PROJ_ROWS)],
+            proj.at[
+                owner_rows(m, GROUP, (i // 2) * PROJ_ROWS, PROJ_ROWS),
+                pl.ds((i % 2) * FF_CUT, FF_CUT),
+            ],
+            proj_sem,
+        )
+    copy(up_copies, up_own, up.at[owner_rows(0, GROUP, 0, GROUP)], up_sem)
+    for i, m in every:
+        copy(
+            up_copies,
+            gathered.at[i, m - 1, pl.ds(0, GROUP)],
+            up.at[owner_rows(m, GROUP, 0, GROUP), pl.ds(i * FF_CUT, FF_CUT)],
+            up_sem,
+        )
+    copy(down_copies, down_own, down.at[owner_rows(0, width, 0, width)], down_sem)
+    for i, m in every:
+        for side in range(2):
             copy(
                 down_copies,
-                down_all.at[i, j],
-                down.at[pl.ds(j * width + i * DOWN_ROWS, DOWN_ROWS)],
+                gathered.at[i, m - 1, pl.ds(GROUP + side * DOWN_ROWS, DOWN_ROWS)],
+                down.at[
+                    owner_rows(m, width, i * DOWN_ROWS, DOWN_ROWS), pl.ds(side * FF_CUT, FF_CUT)
+                ],
                 down_sem,
             )
 
@@ -845,32 +850,52 @@
     hidden = normal1 * gain1 + bias1
     hid_ref[...] = hidden.astype(jnp.bfloat16)
 
-    def by_core(value):
+    def by_owner(value, target):
         for i in range(8):
-            at = 4 * ((i & 1) ^ (me & 1)) + (i >> 1)
-            hid_t[pl.ds(pl.multiple_of(at * 96, 96), 96), :] = value[i * 96 : (i + 1) * 96]
+            away = me ^ i
+            at = (away & 1) * FF_CUT + (away >> 1) * 96
+            for j in range(4):
+                row = pl.multiple_of(at + (depth ^ j) * 24, 8)
+                target[pl.ds(row, 24), :] = value[i * 96 + j * 24 : i * 96 + (j + 1) * 24]
 
     def out_columns(cols, grad):
         keep_cols[:, cols] = dot(hid_t[0:FF_CUT], grad).astype(jnp.bfloat16)
         give_cols[:, cols] = dot(hid_t[FF_CUT:], grad).astype(jnp.bfloat16)
 
-    by_core(flip(hid_ref[...]))
+    by_owner(jnp.transpose(hid_ref[...].astype(jnp.float32)), ordered)
+    hid_t[...] = ordered[...].astype(jnp.bfloat16)
     for made in up_copies:
         made.wait()
     for made in down_copies:
         made.wait()
 
-    def forward(j, branch):
-        cols = pl.ds(pl.multiple_of(j * FF_STEP, FF_STEP), FF_STEP)
-        inner = dot(hid_ref[...], up[:, cols]) + upb_ref[:, cols]
+    def columns(j):
+        return pl.ds(pl.multiple_of(j * FF_STEP, FF_STEP), FF_STEP)
+
+    def rise(j, target):
+        cols = columns(j)
+        target[...] = dot(hid_ref[...], up[:, cols]) + upb_ref[:, cols]
+
+    def fall(j, source):
+        cols = columns(j)
+        inner = source[...]
         share, bell = gelu_parts(inner)
         slope[:, cols] = share + inner * bell * (1.0 / math.sqrt(2.0 * math.pi))
         active = (inner * share).astype(jnp.bfloat16)
         act_ref[:, cols] = active
-        return branch + dot(active, down[cols, :])
-
-    branch = lax.fori_loop(0, 6, forward, jnp.zeros((2 * GROUP, width), jnp.float32))
-    normal2, scale2 = norm(hidden + branch + down_bias)
+        branch[...] += dot(active, down[cols, :])
+
+    def forward(i, unused):
+        rise(2 * i + 1, odd)
+        fall(2 * i, even)
+        rise(jnp.minimum(2 * i + 2, 5), even)
+        fall(2 * i + 1, odd)
+        return unused
+
+    branch[...] = jnp.broadcast_to(down_bias, branch.shape)
+    rise(0, even)
+    lax.fori_loop(0, 3, forward, 0)
+    normal2, scale2 = norm(hidden + branch[...])
     result = normal2 * gain2 + bias2
     block = (keep * result + (1.0 - keep) * tokens).astype(jnp.bfloat16)
     block_ref[0] = block[:GROUP]
@@ -903,7 +928,8 @@
     grad_mixed = norm_back(grad_hidden * gain1, normal1, scale1)
     base_ref[...] = keep * grad_mixed + (1.0 - keep) * cot
     grad_proj = grad_mixed.astype(jnp.bfloat16)
-    by_core(flip(att_ref[...]))
+    by_owner(jnp.transpose(att_ref[...].astype(jnp.float32)), ordered)
+    hid_t[...] = ordered[...].astype(jnp.bfloat16)
     out_columns(slice(4 * width, 5 * width), grad_proj)
     sums_ref[0:1, :] = add_up(grad_proj.astype(jnp.float32))
     sums_ref[6:8, :] = jnp.zeros((2, width), jnp.float32)
@@ -917,13 +943,9 @@
             [column[i * 96 + j * 24 : i * 96 + (j + 1) * 24] for i in range(32)], axis=0
         )
         vectors = jnp.where(lane == 6 + j, part, vectors)
-    for i in range(8):
-        at = 4 * ((i & 1) ^ (me & 1)) + (i >> 1)
-        turned[pl.ds(pl.multiple_of(at * 96, 96), 96), :] = vectors[i * 96 : (i + 1) * 96].astype(
-            jnp.bfloat16
-        )
-    keep_cols[:, 5 * width :] = turned[0:FF_CUT]
-    give_cols[:, 5 * width :] = turned[FF_CUT:]
+    by_owner(vectors, turned)
+    keep_cols[:, 5 * width :] = turned[0:FF_CUT].astype(jnp.bfloat16)
+    give_cols[:, 5 * width :] = turned[FF_CUT:].astype(jnp.bfloat16)
     grad_att = dot_nt(grad_proj, proj[...]).astype(jnp.bfloat16)
     for mb in range(2):
         for j in range(4):
@@ -954,45 +976,43 @@
         pltpu.VMEM((rows, width), LOW),
         pltpu.VMEM((8, width), WIDE),
         pltpu.VMEM((1, hidden), WIDE),
-        pltpu.VMEM((width, 128), LOW),
+        pltpu.VMEM((width, 128), WIDE),
+        pltpu.VMEM((width, rows), WIDE),
+        pltpu.VMEM((rows, FF_STEP), WIDE),
+        pltpu.VMEM((rows, FF_STEP), WIDE),
+        pltpu.VMEM((rows, width), WIDE),
         pltpu.SemaphoreType.DMA((25,)),
-        pltpu.SemaphoreType.DMA((33,)),
-        pltpu.SemaphoreType.DMA((32,)),
+        pltpu.SemaphoreType.DMA((25,)),
+        pltpu.SemaphoreType.DMA((49,)),
     ]
-    return call(dense_kernel, "dense", ins, outs, scratch, any_ins=5, flops=2 * 10**10)
+    return call(dense_kernel, "dense", ins, outs, scratch, any_ins=4, flops=2 * 10**10)
+
+
+def tie(*values):
+    return lax.optimization_barrier(values)
 
 
 def take(value, at, axis):
     return lax.dynamic_index_in_dim(value, at, axis, keepdims=False)
 
 
-def halve(value, at, axis, send):
-    kept = take(value, at, axis).astype(jnp.float32)
-    return (kept + send(take(value, 1 - at, axis)).astype(jnp.float32)).astype(jnp.bfloat16)
-
-
-def scatter_plane(value, me):
-    across, along = (me >> 1) & 1, me >> 2
+def join(kept, given, send):
+    return (kept.astype(jnp.float32) + send(given).astype(jnp.float32)).astype(jnp.bfloat16)
+
+
+def over(bits):
+    return lambda value: from_ctx(value, bits)
+
+
+def scatter_plane(value):
     value = value.reshape(2, 2, 96, COLUMNS)
-    left = halve(value[..., :LEFT], across, 1, lambda v: from_ctx(v, 2))
-    right = halve(value[..., LEFT:], along, 0, lambda v: from_ctx(v, 4))
-    return left, right
-
-
-def scatter_plane_end(left, right, me):
-    across, along = (me >> 1) & 1, me >> 2
-    left = halve(left, along, 0, lambda v: from_ctx(v, 4))
-    right = halve(right, across, 0, lambda v: from_ctx(v, 2))
-    return jnp.concatenate([left, right], axis=1)
-
-
-def scatter_depth(value, depth):
-    return halve(value.reshape(2, 2, 24, value.shape[1]), depth & 1, 1, lambda v: from_fsdp(v, 1))
-
-
-def scatter_depth_end(value, depth):
-    kept = take(value, depth >> 1, 0).astype(jnp.float32)
-    return kept + from_fsdp(take(value, 1 - (depth >> 1), 0), 2).astype(jnp.float32)
+    left, right = value[..., :LEFT], value[..., LEFT:]
+    return join(left[:, 0], left[:, 1], over(2)), join(right[0], right[1], over(4))
+
+
+def scatter_plane_end(left, right):
+    left, right = join(left[0], left[1], over(4)), join(right[0], right[1], over(2))
+    return jnp.concatenate([left, right], axis=1).reshape(2, 2, 24, COLUMNS)
 
 
 def fast_on_device(
@@ -1046,51 +1066,36 @@
         ]
     ).reshape(4, 3 * GROUP)
     columns = jnp.concatenate([columns, vectors, jnp.zeros((4, 3 * GROUP), low)], axis=0)
+    up_cut = lax.dynamic_slice_in_dim(up_weight, me * FF_CUT, FF_CUT, 1)
+    down_cut = lax.dynamic_slice_in_dim(down_weight, me * DOWN_ROWS, DOWN_ROWS, 0)
+    proj_cut = lax.dynamic_slice(
+        proj_weight, ((me >> 1) * PROJ_ROWS, (me & 1) * FF_CUT), (PROJ_ROWS, FF_CUT)
+    )
+    cut = jnp.concatenate([up_cut, down_cut[:, :FF_CUT], down_cut[:, FF_CUT:], proj_cut], axis=0)
     came = from_ctx(take(marked, 1 - height, 0), 4)
     across = from_ctx(own, 2)
-    near, mid = from_fsdp(columns, 1), from_fsdp(columns, 2)
-    own, came, across, near, mid = lax.optimization_barrier((own, came, across, near, mid))
-    far = from_fsdp(columns, 3)
-    four = jnp.stack([own, came, across, from_ctx(came, 2)])
-    four, far = lax.optimization_barrier((four, far))
+    cuts = [from_fsdp(cut, m) for m in (1, 2, 3)]
+    corner = from_ctx(came, 2)
+    own, came, across, corner, columns, *cuts = tie(own, came, across, corner, columns, *cuts)
+    gathered = lax.all_gather(jnp.stack(cuts), "ctx", axis=0)
+    near, mid, far = [from_fsdp(columns, m) for m in (1, 2, 3)]
+    four = jnp.stack([own, came, across, corner])
     eight = from_ctx(four, 1)
-
-    down_cut = lax.dynamic_slice_in_dim(down_weight, me * DOWN_ROWS, DOWN_ROWS, 0)
-    down_all = lax.all_gather(down_cut, ("ctx", "fsdp"), axis=0).reshape(8, 4, DOWN_ROWS, features)
-    up_cut = lax.dynamic_slice_in_dim(up_weight, me * FF_CUT, FF_CUT, 1)
-    proj_cut = lax.dynamic_slice(
-        proj_weight, ((me >> 1) * PROJ_ROWS, (me & 1) * FF_CUT), (PROJ_ROWS, FF_CUT)
-    )
-    cut = jnp.concatenate([up_cut, proj_cut], axis=0)
 
     documents = jnp.arange(NDOC, dtype=jnp.int32)
     keep_rows = jnp.sum(
         jnp.where(ids[:, :, None] == documents, keep_mask[:, 0][:, None, :], 0), axis=2
     ).astype(jnp.float32).reshape(2 * GROUP, 1)
 
-    cut, four = lax.optimization_barrier((cut, four))
-    cuts = [from_fsdp(cut, m) for m in (1, 2, 3)]
     made = project(place, four, eight, columns, near, mid, far)
     qt, ka = list(made[:3]), made[3:6]
     vt, qkv_mine, vec = made[6:]
-    ot = [None] * 3
-    turned = qt
-    qt = [None] * 3
-    qt[0], qt[1], ot[0], ot[1] = attend((0, 1), place, *turned[:2], *ka[:2], vt)
-    last, ot[1], *cuts = lax.optimization_barrier((turned[2], ot[1], *cuts))
-    cuts = jnp.concatenate(cuts, axis=0)
-    first, second = cuts[:FIRST], cuts[FIRST:]
-    both = [first, from_ctx(first, 2), second, from_ctx(second, 4)]
-    qt[2], ot[2], o = attend((2,), place, last, ka[2], vt, ot[0], ot[1])
-    o, *both = lax.optimization_barrier((o, *both))
-    first = jnp.concatenate(both[:2], axis=0)
-    second = jnp.concatenate(both[2:], axis=0)
-    first_far, second_far = from_ctx(first, 4), from_ctx(second, 2)
-    held = jnp.concatenate([first, first_far, second, second_far], axis=0)
-    held_too = from_ctx(held, 1)
-    xt, qn, kt, *va, by_head = turn(four, eight, *turned[:2], last, *ka, vt, qkv_mine)
+    turned = list(qt)
+    *made, o = attend((0, 1, 2), place, *turned, *ka, vt)
+    qt, ot = made[:3], made[3:]
     heads = lax.all_to_all(o, "ctx", 0, 0, tiled=True)
-    heads, xt, qn, kt, *va, by_head = lax.optimization_barrier((heads, xt, qn, kt, *va, by_head))
+    xt, qn, kt, *va, by_head = turn(four, eight, *turned, *ka, vt, qkv_mine)
+    heads, xt = tie(heads, xt)
     block_rows, base, grad_heads, grad_down, kept, given = dense(
         place,
         heads,
@@ -1100,41 +1105,43 @@
         vec,
         proj_weight,
         up_weight,
-        down_all,
-        held,
-        held_too,
+        down_weight,
+        gathered,
     )
     grad_o = lax.all_to_all(grad_heads, "ctx", 0, 0, tiled=True)
     down_part = lax.psum_scatter(grad_down, "ctx", scatter_dimension=0, tiled=True)
     each = features // 32
-    both = (kept.astype(jnp.float32) + from_ctx(given, 1).astype(jnp.float32)).astype(low)
-    grad_o, both = lax.optimization_barrier((grad_o, both))
-    left, right = scatter_plane(both, me)
+    both = join(kept, given, over(1))
+    grad_o, both = tie(grad_o, both)
+    left, right = scatter_plane(both)
     shared = (place, grad_o, kt, qn, xt)
     sent, grads = attend_back((0, 1), *shared, *ot[:2], *qt[:2], *ka[:2], *va[:2])
-    last, left, right, grads = lax.optimization_barrier((qt[2], left, right, grads))
-    both = scatter_plane_end(left, right, me)
+    last, left, right, grads = tie(qt[2], left, right, grads)
+    both = scatter_plane_end(left, right)
     came_first = lax.all_to_all(sent, ("ctx", "fsdp"), 0, 0, tiled=True)
     sent, kept, given, _ = attend_back(
         (2,), *shared, ot[2], last, ka[2], va[2], grads, by_head
     )
-    given, both, came_first, down_part = lax.optimization_barrier(
-        (given, both, came_first, down_part)
-    )
-    both = scatter_depth(both, depth)
-    out_down = lax.psum_scatter(down_part, "fsdp", scatter_dimension=0, tiled=True).astype(
-        jnp.float32
-    )
-
-    half = (kept.astype(jnp.float32) + from_ctx(given, 1).astype(jnp.float32)).astype(low)
-    half, sent = lax.optimization_barrier((half, sent))
+    given, came_first, down_part, both = tie(given, came_first, down_part, both)
+    out_down = lax.psum_scatter(down_part, "fsdp", scatter_dimension=0, tiled=True)
+
+    half = join(kept, given, over(1))
+    sent, half = tie(sent, half)
+    near = from_fsdp(both[:, 1], 1)
     quarter = half[:2].astype(jnp.float32) + from_ctx(half[2:], 2).astype(jnp.float32)
-    quarter, both, out_down = lax.optimization_barrier((quarter, both, out_down))
-    both = scatter_depth_end(both, depth)
-    out_up, out_proj = both[:, : 4 * features], both[:, 4 * features : 5 * features]
-    vectors = both[:, 5 * features :]
+    quarter, near = tie(quarter, near)
+    both = join(both[:, 0], near, lambda value: value)
+    mid = from_fsdp(both[1], 2)
+
+    def columns_of(start, stop):
+        return both[0, :, start:stop].astype(jnp.float32) + mid[:, start:stop].astype(jnp.float32)
+
+    out_up, out_proj = columns_of(0, 4 * features), columns_of(4 * features, 5 * features)
+    vectors = columns_of(5 * features, 5 * features + 10).T
     mine = quarter[0]
     swapped = from_ctx(quarter[1].astype(low), 4).astype(jnp.float32)
+    swapped, out_down = tie(swapped, out_down)
+    out_down = out_down.astype(jnp.float32)
     first = height == 0
     back = jnp.concatenate(
         [jnp.where(first, mine, swapped), jnp.where(first, swapped, mine)], axis=0
@@ -1142,17 +1149,9 @@
     grad_tokens = base + keep_rows * back
 
     came_last = lax.all_to_all(sent, ("ctx", "fsdp"), 0, 0, tiled=True)
-    came = []
-    for value in (came_first, came_last):
-        value = value.reshape(2, 4, 4, 32, -1).astype(jnp.float32)
-        came.append(jnp.sum(value, axis=(0, 2)))
-    came = jnp.concatenate(came, axis=2)
-    out_qkv = came[:, :each].reshape(4, each, HEADS_EACH, 3, HEAD).transpose(1, 3, 0, 2, 4)
-    out_qkv = out_qkv.reshape(each, 3 * features)
-    head_bias = (came[:, each] + came[:, each + 1]).reshape(4, HEADS_EACH, 3, HEAD)
+    out_qkv, out_bias = collect(came_first, came_last)
     at = (4 * me + depth) * each
-    out_query_bias = lax.dynamic_slice_in_dim(head_bias[:, :, 0].reshape(features), at, each)
-    out_value_bias = lax.dynamic_slice_in_dim(head_bias[:, :, 2].reshape(features), at, each)
+    out_query_bias, out_value_bias = lax.dynamic_slice_in_dim(out_bias, at, each, 1)
 
     return (
         block_rows.reshape(2, 1, GROUP, features),
@@ -1161,15 +1160,15 @@
         out_query_bias,
         out_value_bias,
         out_proj,
-        vectors[:, 0],
-        vectors[:, 1],
-        vectors[:, 2],
+        vectors[0],
+        vectors[1],
+        vectors[2],
         out_up,
-        vectors[:, 6:10].T.reshape(4 * each),
+        vectors[6:10].reshape(4 * each),
         out_down,
-        vectors[:, 3],
-        vectors[:, 4],
-        vectors[:, 5],
+        vectors[3],
+        vectors[4],
+        vectors[5],
     )
 
 

time: 298 us -> 281 us (0.943)
  starting transfers between devices: 61.1 us -> 40.6 us
  waiting for transfers between devices: 69 us -> 82.5 us
  local copies, waits for them, and re-layouts: 20 us -> 15.9 us
  Pallas kernels: 114 us -> 111 us
    ppermute x8, waiting for transfers between devices: 29.3 us -> 44.1 us  [from_fsdp(): return lax.ppermute(value, 'fsdp', [(i, i ^ bits) for i in range(4)])]
    all_to_all x1, starting transfers between devices: 11.2 us -> 3.37 us  [fast_on_device(): came_first = lax.all_to_all(sent, ('ctx', 'fsdp'), 0, 0, tiled=True)]
    ppermute x17 -> x12, waiting for transfers between devices: 15.9 us -> 22.6 us  [from_ctx(): return lax.ppermute(value, 'ctx', [(i, i ^ bits) for i in range(8)])]
    ppermute x17 -> x12, starting transfers between devices: 17.1 us -> 10.9 us  [from_ctx(): return lax.ppermute(value, 'ctx', [(i, i ^ bits) for i in range(8)])]
    reduce_scatter x1, waiting for transfers between devices: 3.8 us -> 0.02 us  [fast_on_device(): lax.psum_scatter(down_part, 'fsdp', scatter_dimension=0, tiled=True)]
    ppermute x8, starting transfers between devices: 18.4 us -> 14.8 us  [from_fsdp(): return lax.ppermute(value, 'fsdp', [(i, i ^ bits) for i in range(4)])]
    pallas_call x7, Pallas kernels: 114 us -> 111 us  [call(): pl.pallas_call(kernel, name=name, out_shape=[jax.ShapeDtypeStruct(shape,...]
    convert_element_type x8 -> x9, other arithmetic: 10.1 us -> 9.12 us  [the longest x7 7.44 us: join(): (kept.astype(jnp.float32) + send(given).astype(jnp.float32)).astype(jnp.b...]
  transfers between devices with their start and end apart: 32 -> 27, of which waited for: 15 -> 15; matrix products, arithmetic and copies ran while one was open for 11% -> 8% of each run, Pallas kernels for 26% -> 27%
where the time goes in v2:
time: 281 us; the launch traced here: 280 us
  Pallas kernels  111 us (40%)
  waiting for transfers between devices  82.5 us (29%)
  starting transfers between devices  40.6 us (14%)
  other arithmetic  16.4 us (6%)
  local copies, waits for them, and re-layouts  15.9 us (6%)
  between operations  14.2 us (5%)
    pallas_call x7, Pallas kernels, call(): pl.pallas_call(kernel, name=name, out_shape=[jax.ShapeDtypeStruct(shape,...  111 us
    ppermute x8, waiting for transfers between devices, from_fsdp(): return lax.ppermute(value, 'fsdp', [(i, i ^ bits) for i in range(4)])  44.1 us
    ppermute x12, waiting for transfers between devices, from_ctx(): return lax.ppermute(value, 'ctx', [(i, i ^ bits) for i in range(8)])  22.6 us
    ppermute x8, starting transfers between devices, from_fsdp(): return lax.ppermute(value, 'fsdp', [(i, i ^ bits) for i in range(4)])  14.8 us
    ppermute x12, starting transfers between devices, from_ctx(): return lax.ppermute(value, 'ctx', [(i, i ^ bits) for i in range(8)])  10.9 us
    convert_element_type x7, other arithmetic, join(): (kept.astype(jnp.float32) + send(given).astype(jnp.float32)).astype(jnp.b...  7.44 us
    all_to_all x1, waiting for transfers between devices, fast_on_device(): came_last = lax.all_to_all(sent, ('ctx', 'fsdp'), 0, 0, tiled=True)  5.72 us
  transfers between devices with their start and end apart: 27, of which 15 were waited for; matrix products, arithmetic and copies ran while one was open for 8% of the time, Pallas kernels for 27%

profile of v2, /device:TPU:0, one launch (start us, length us, event | category | flops | bytes accessed | tf_op | source)
XLA Modules:
  0.0 280.4 jit_solution(7385653368002073879)
XLA Ops:
  9.2 3.1 %collective-permute-start = (bf16[200,768]{1,0:T(8,128)(2,1)S(1)}, bf16[200,768]{1,0:T(8,128)(2,1)S(1)}, u32[]{:S(2)}, u32[]{:S(2)}) collective-permute-start(bf16[200,768]{1,0:T(8,128)(2,1)S(1)} %get-tuple-element.212), channel_id=1, source_target_pairs={{0,16},{4,20},{8,24},{12,28},{16,0},{20,4},{24,8},{28,12},{1,17},{... | collective-permute-start | bytes 921608 | tf_op jit(solution)/shard_map/ppermute | solution.py:715
  14.9 3.7 %collective-permute-start.5 = (bf16[432,384]{1,0:T(8,128)(2,1)S(1)}, bf16[432,384]{1,0:T(8,128)(2,1)S(1)}, u32[]{:S(2)}, u32[]{:S(2)}) collective-permute-start(bf16[432,384]{1,0:T(8,128)(2,1)S(1)} %pad_maximum_fusion.3), channel_id=1, source_target_pairs={{0,3},{1,2},{2,1},{3,0},{4,7},{5,6},{6,5},{7,4},{8,11},{9,10},{10,... | collective-permute-start | bytes 995336 | tf_op jit(solution)/shard_map/ppermute | solution.py:719
  23.1 6.5 %collective-permute-done.1 = bf16[200,768]{1,0:T(8,128)(2,1)S(1)} collective-permute-done((bf16[200,768]{1,0:T(8,128)(2,1)S(1)}, bf16[200,768]{1,0:T(8,128)(2,1)S(1)}, u32[]{:S(2)}, u32[]{:S(2)}) %collective-permute-start.1) | collective-permute-done | bytes 307232 | tf_op jit(solution)/shard_map/ppermute | solution.py:715
  29.6 17.0 %collective-permute-done.4 = bf16[432,384]{1,0:T(8,128)(2,1)S(1)} collective-permute-done((bf16[432,384]{1,0:T(8,128)(2,1)S(1)}, bf16[432,384]{1,0:T(8,128)(2,1)S(1)}, u32[]{:S(2)}, u32[]{:S(2)}) %collective-permute-start.4) | collective-permute-done | bytes 331808 | tf_op jit(solution)/shard_map/ppermute | solution.py:719
  53.1 5.9 %collective-permute-done.9.refs_5_ = bf16[200,576]{1,0:T(8,128)(2,1)S(1)} collective-permute-done((bf16[200,576]{1,0:T(8,128)(2,1)S(1)}, bf16[200,576]{1,0:T(8,128)(2,1)S(1)}, u32[]{:S(2)}, u32[]{:S(2)}) %collective-permute-start.9) | collective-permute-done | bytes 230432 | tf_op jit(solution)/shard_map/ppermute | solution.py:719
  59.0 13.2 %collective-permute-done.8.refs_4_ = bf16[200,576]{1,0:T(8,128)(2,1)S(1)} collective-permute-done((bf16[200,576]{1,0:T(8,128)(2,1)S(1)}, bf16[200,576]{1,0:T(8,128)(2,1)S(1)}, u32[]{:S(2)}, u32[]{:S(2)}) %collective-permute-start.8) | collective-permute-done | bytes 230432 | tf_op jit(solution)/shard_map/ppermute | solution.py:719
  72.9 7.1 %project.1 = (bf16[128,1536]{1,0:T(8,128)(2,1)}, bf16[128,1536]{1,0:T(8,128)(2,1)}, bf16[128,1536]{1,0:T(8,128)(2,1)}, bf16[1536,128]{1,0:T(8,128)(2,1)}, bf16[1...) custom-call(s32[10]{0:T(128)} %stack.38.place, ...), custom_call_target="tpu_custom_call" | custom-call | flops 5000000000 | bytes 10000000 | tf_op jit(solution)/shard_map/project/pallas_call | solution.py:416
  80.0 15.1 %attend0.1 = (bf16[128,1536]{1,0:T(8,128)(2,1)}, bf16[128,1536]{1,0:T(8,128)(2,1)}, bf16[128,1536]{1,0:T(8,128)(2,1)}, bf16[64,1536]{1,0:T(8,128)(2,1)}, bf16[64...) custom-call(s32[10]{0:T(128)} %stack.38.place, ...), custom_call_target="tpu_custom_call" | custom-call | flops 5000000000 | bytes 10000000 | tf_op jit(solution)/shard_map/attend0/pallas_call | solution.py:416
  95.2 3.7 %all-to-all-start = ((bf16[8,192,192]{2,1,0:T(8,128)(2,1)}), bf16[8,192,192]{2,1,0:T(8,128)(2,1)S(1)}, u32[]{:S(2)}, u32[]{:S(2)}) async-start(bf16[8,192,192]{2,1,0:T(8,128)(2,1)} %get-tuple-element.89), calls=%async_computation | async-start | bytes 1572864 | tf_op jit(solution)/shard_map/all_to_all | solution.py:1096
  99.9 6.9 %turn.1 = (bf16[768,1536]{1,0:T(8,128)(2,1)}, bf16[1536,192]{1,0:T(8,128)(2,1)}, bf16[192,1536]{1,0:T(8,128)(2,1)}, bf16[1536,128]{1,0:T(8,128)(2,1)}, bf16[1536...) custom-call(bf16[4,200,768]{2,1,0:T(8,128)(2,1)} %copy-done.1, ...), custom_call_target="tpu_custom_call" | custom-call | flops 5000000000 | bytes 10000000 | tf_op jit(solution)/shard_map/turn/pallas_call | solution.py:416
  106.8 4.6 %all-to-all-done.refs_0_ = bf16[8,192,192]{2,1,0:T(8,128)(2,1)S(1)} async-done(((bf16[8,192,192]{2,1,0:T(8,128)(2,1)}), bf16[8,192,192]{2,1,0:T(8,128)(2,1)S(1)}, u32[]{:S(2)}, u32[]{:S(2)}) %all-to-all-start) | async-done | bytes 589856 | tf_op jit(solution)/shard_map/all_to_all | solution.py:1096
  112.3 36.0 %dense.1 = (bf16[2,192,768]{2,1,0:T(8,128)(2,1)}, f32[384,768]{1,0:T(8,128)}, bf16[8,192,192]{2,1,0:T(8,128)(2,1)}, bf16[3072,768]{1,0:T(8,128)(2,1)}, bf16[384,...) custom-call(s32[10]{0:T(128)} %stack.38.place, bf16[8,192,192]{2,1,0:T(8,128)(2,1)} %copy-done.4, ...), custom_call_target="tpu_custom_call" | custom-call | flops 20000000000 | bytes 10000000 | tf_op jit(solution)/shard_map/dense/pallas_call | solution.py:416
  148.4 4.5 %all-to-all-start.1 = ((bf16[8,192,192]{2,1,0:T(8,128)(2,1)}), bf16[8,192,192]{2,1,0:T(8,128)(2,1)}, u32[]{:S(2)}, u32[]{:S(2)}) async-start(bf16[8,192,192]{2,1,0:T(8,128)(2,1)} %get-tuple-element.99), calls=%async_computation.1 | async-start | bytes 1572864 | tf_op jit(solution)/shard_map/all_to_all | solution.py:1111
  155.7 4.2 %add_convert_fusion = bf16[384,3968]{1,0:T(8,128)(2,1)S(1)} fusion(bf16[384,3968]{1,0:T(8,128)(2,1)} %copy-done, bf16[384,3968]{1,0:T(8,128)(2,1)} %get-tuple-element.100), kind=kLoop, calls=%fused_computation | loop fusion | flops 6094848 | bytes 9142272 | tf_op jit(solution)/shard_map/convert_element_type | solution.py:1000
  159.9 5.4 %all-to-all-done.1.refs_0_ = bf16[8,192,192]{2,1,0:T(8,128)(2,1)} async-done(((bf16[8,192,192]{2,1,0:T(8,128)(2,1)}), bf16[8,192,192]{2,1,0:T(8,128)(2,1)}, u32[]{:S(2)}, u32[]{:S(2)}) %all-to-all-start.1) | async-done | bytes 589856 | tf_op jit(solution)/shard_map/all_to_all | solution.py:1111
  168.3 25.3 %attend_back0.1 = (bf16[32,32,384]{2,1,0:T(8,128)(2,1)}, bf16[1536,384]{1,0:T(8,128)(2,1)}) custom-call(s32[10]{0:T(128)} %stack.38.place, bf16[8,192,192]{2,1,0:T(8,128)(2,1)} %all-to-all-done.1.refs_0_, bf16[192,1536]{1,0:T(8,128)(2,1)} %get-tuple-element.103.refs_1_, bf16[1536,192]{1,0:T(8,128)(2,1)} %get-tuple-element.104.refs_2_, ...), custom_call_target="tpu_custom_call" | custom-call | flops 10000000000 | bytes 10000000 | tf_op jit(solution)/shard_map/attend_back0/pallas_call | solution.py:416
  193.6 3.4 %all-to-all-start.2 = ((bf16[32,32,384]{2,1,0:T(8,128)(2,1)}), bf16[32,32,384]{2,1,0:T(8,128)(2,1)}, u32[]{:S(2)}, u32[]{:S(2)}) async-start(bf16[32,32,384]{2,1,0:T(8,128)(2,1)} %get-tuple-element.123), calls=%async_computation.2 | async-start | bytes 1572864 | tf_op jit(solution)/shard_map/all_to_all | solution.py:1121
  203.0 18.1 %attend_back2.1 = (bf16[32,32,192]{2,1,0:T(8,128)(2,1)}, bf16[4,192,768]{2,1,0:T(8,128)(2,1)}, bf16[4,192,768]{2,1,0:T(8,128)(2,1)}, bf16[1536,192]{1,0:T(8,128)(2,1)}) custom-call(s32[10]{0:T(128)} %stack.38.place, bf16[8,192,192]{2,1,0:T(8,128)(2,1)} %all-to-all-done.1.refs_0_, bf16[192,1536]{1,0:T(8,128)(2,1)} %get-tuple-element.103.refs_1_, ...), custom_call_target="tpu_custom_call" | custom-call | flops 10000000000 | bytes 10000000 | tf_op jit(solution)/shard_map/attend_back2/pallas_call | solution.py:416
  223.8 2.9 %collective-permute-done.15 = bf16[4,192,768]{2,1,0:T(8,128)(2,1)S(1)} collective-permute-done((bf16[4,192,768]{2,1,0:T(8,128)(2,1)}, bf16[4,192,768]{2,1,0:T(8,128)(2,1)S(1)}, u32[]{:S(2)}, u32[]{:S(2)}) %collective-permute-start.15) | collective-permute-done | bytes 1179680 | tf_op jit(solution)/shard_map/ppermute | solution.py:715
  230.9 3.3 %all-to-all-start.3 = ((bf16[32,32,192]{2,1,0:T(8,128)(2,1)}), bf16[32,32,192]{2,1,0:T(8,128)(2,1)}, u32[]{:S(2)}, u32[]{:S(2)}) async-start(bf16[32,32,192]{2,1,0:T(8,128)(2,1)} %get-tuple-element.134), calls=%async_computation.5 | async-start | bytes 1048576 | tf_op jit(solution)/shard_map/all_to_all | solution.py:1151
  234.3 9.6 %collective-permute-done.16 = bf16[2,192,768]{2,1,0:T(8,128)(2,1)} collective-permute-done((bf16[2,192,768]{2,1,0:T(8,128)(2,1)S(1)}, bf16[2,192,768]{2,1,0:T(8,128)(2,1)}, u32[]{:S(2)}, u32[]{:S(2)}) %collective-permute-start.16) | collective-permute-done | bytes 589856 | tf_op jit(solution)/shard_map/ppermute | solution.py:715
  245.1 5.8 %collective-permute-done.17 = bf16[2,24,3968]{2,1,0:T(8,128)(2,1)S(1)} collective-permute-done((bf16[2,24,3968]{2,1,0:T(8,128)(2,1)}, bf16[2,24,3968]{2,1,0:T(8,128)(2,1)S(1)}, u32[]{:S(2)}, u32[]{:S(2)}) %collective-permute-start.17) | collective-permute-done | bytes 380960 | tf_op jit(solution)/shard_map/ppermute | solution.py:719
  251.1 4.2 %collective-permute-start.19 = (bf16[24,3968]{1,0:T(8,128)(2,1)S(1)}, bf16[24,3968]{1,0:T(8,128)(2,1)S(1)}, u32[]{:S(2)}, u32[]{:S(2)}) collective-permute-start(bf16[24,3968]{1,0:T(8,128)(2,1)S(1)} %slice_bitcast_fusion.7), channel_id=1, source_target_pairs={{0,2},{1,3},{2,0},{3,1},{4,6},{5,7},{6,4},{7,5},{8,10},{9,11},{10,... | collective-permute-start | bytes 571400 | tf_op jit(solution)/shard_map/ppermute | solution.py:719
  255.3 5.7 %all-to-all-done.3.last_ref = bf16[32,32,192]{2,1,0:T(8,128)(2,1)} async-done(((bf16[32,32,192]{2,1,0:T(8,128)(2,1)}), bf16[32,32,192]{2,1,0:T(8,128)(2,1)}, u32[]{:S(2)}, u32[]{:S(2)}) %all-to-all-start.3) | async-done | bytes 393248 | tf_op jit(solution)/shard_map/all_to_all | solution.py:1151
  (131 shorter events, 51.0 us)
Async XLA Ops:
  7.2 104.2 %all-gather.3.cloned.1.call-start = ((), (), s32[]{:S(2)}) async-start(), calls=%async_computation.8 | async-start | bytes 8957952 | tf_op jit(solution)/shard_map/all_gather | solution.py:1080
  9.2 12.0 %collective-permute-start = (bf16[200,768]{1,0:T(8,128)(2,1)S(1)}, bf16[200,768]{1,0:T(8,128)(2,1)S(1)}, u32[]{:S(2)}, u32[]{:S(2)}) collective-permute-start(bf16[200,768]{1,0:T(8,128)(2,1)S(1)} %get-tuple-element.212), channel_id=1, source_target_pairs={{0,16},{4,20},{8,24},{12,28},{16,0},{20,4},{24,8},{28,12},{1,17},{... | collective-permute-start | bytes 921608 | tf_op jit(solution)/shard_map/ppermute | solution.py:715
  14.9 14.7 %collective-permute-start.5 = (bf16[432,384]{1,0:T(8,128)(2,1)S(1)}, bf16[432,384]{1,0:T(8,128)(2,1)S(1)}, u32[]{:S(2)}, u32[]{:S(2)}) collective-permute-start(bf16[432,384]{1,0:T(8,128)(2,1)S(1)} %pad_maximum_fusion.3), channel_id=1, source_target_pairs={{0,3},{1,2},{2,1},{3,0},{4,7},{5,6},{6,5},{7,4},{8,11},{9,10},{10,... | collective-permute-start | bytes 995336 | tf_op jit(solution)/shard_map/ppermute | solution.py:719
  18.6 28.0 %collective-permute-start.4 = (bf16[432,384]{1,0:T(8,128)(2,1)S(1)}, bf16[432,384]{1,0:T(8,128)(2,1)S(1)}, u32[]{:S(2)}, u32[]{:S(2)}) collective-permute-start(bf16[432,384]{1,0:T(8,128)(2,1)S(1)} %pad_maximum_fusion.3), channel_id=1, source_target_pairs={{0,2},{1,3},{2,0},{3,1},{4,6},{5,7},{6,4},{7,5},{8,10},{9,11},{10,... | collective-permute-start | bytes 995336 | tf_op jit(solution)/shard_map/ppermute | solution.py:719
  18.6 28.0 %collective-permute-start.3 = (bf16[432,384]{1,0:T(8,128)(2,1)S(1)}, bf16[432,384]{1,0:T(8,128)(2,1)S(1)}, u32[]{:S(2)}, u32[]{:S(2)}) collective-permute-start(bf16[432,384]{1,0:T(8,128)(2,1)S(1)} %pad_maximum_fusion.3), channel_id=1, source_target_pairs={{0,1},{1,0},{2,3},{3,2},{4,5},{5,4},{6,7},{7,6},{8,9},{9,8},{10,11... | collective-permute-start | bytes 995336 | tf_op jit(solution)/shard_map/ppermute | solution.py:719
  21.2 25.4 %collective-permute-start.2 = (bf16[200,768]{1,0:T(8,128)(2,1)S(1)}, bf16[200,768]{1,0:T(8,128)(2,1)S(1)}, u32[]{:S(2)}, u32[]{:S(2)}) collective-permute-start(bf16[200,768]{1,0:T(8,128)(2,1)S(1)} %collective-permute-done), channel_id=1, source_target_pairs={{0,8},{4,12},{8,0},{12,4},{16,24},{20,28},{24,16},{28,20},{1,9},{5... | collective-permute-start | bytes 921608 | tf_op jit(solution)/shard_map/ppermute | solution.py:715
  47.9 24.2 %collective-permute-start.6 = (bf16[4,200,768]{2,1,0:T(8,128)(2,1)S(1)}, bf16[4,200,768]{2,1,0:T(8,128)(2,1)}, u32[]{:S(2)}, u32[]{:S(2)}) collective-permute-start(bf16[4,200,768]{2,1,0:T(8,128)(2,1)S(1)} %pad_maximum_fusion.refs_0_), channel_id=1, source_target_pairs={{0,4},{4,0},{8,12},{12,8},{16,20},{20,16},{24,28},{28,24},{1,5},{5... | collective-permute-start | bytes 3686408 | tf_op jit(solution)/shard_map/ppermute | solution.py:715
  48.0 11.0 %collective-permute-start.9 = (bf16[200,576]{1,0:T(8,128)(2,1)S(1)}, bf16[200,576]{1,0:T(8,128)(2,1)S(1)}, u32[]{:S(2)}, u32[]{:S(2)}) collective-permute-start(bf16[200,576]{1,0:T(8,128)(2,1)S(1)} %maximum_maximum_fusion.refs_2_), channel_id=1, source_target_pairs={{0,3},{1,2},{2,1},{3,0},{4,7},{5,6},{6,5},{7,4},{8,11},{9,10},{10,... | collective-permute-start | bytes 691208 | tf_op jit(solution)/shard_map/ppermute | solution.py:719
  50.5 21.6 %collective-permute-start.8 = (bf16[200,576]{1,0:T(8,128)(2,1)S(1)}, bf16[200,576]{1,0:T(8,128)(2,1)S(1)}, u32[]{:S(2)}, u32[]{:S(2)}) collective-permute-start(bf16[200,576]{1,0:T(8,128)(2,1)S(1)} %maximum_maximum_fusion.refs_2_), channel_id=1, source_target_pairs={{0,2},{1,3},{2,0},{3,1},{4,6},{5,7},{6,4},{7,5},{8,10},{9,11},{10,... | collective-permute-start | bytes 691208 | tf_op jit(solution)/shard_map/ppermute | solution.py:719
  50.5 21.6 %collective-permute-start.7 = (bf16[200,576]{1,0:T(8,128)(2,1)S(1)}, bf16[200,576]{1,0:T(8,128)(2,1)S(1)}, u32[]{:S(2)}, u32[]{:S(2)}) collective-permute-start(bf16[200,576]{1,0:T(8,128)(2,1)S(1)} %maximum_maximum_fusion.refs_2_), channel_id=1, source_target_pairs={{0,1},{1,0},{2,3},{3,2},{4,5},{5,4},{6,7},{7,6},{8,9},{9,8},{10,11... | collective-permute-start | bytes 691208 | tf_op jit(solution)/shard_map/ppermute | solution.py:719
  95.2 16.2 %all-to-all-start = ((bf16[8,192,192]{2,1,0:T(8,128)(2,1)}), bf16[8,192,192]{2,1,0:T(8,128)(2,1)S(1)}, u32[]{:S(2)}, u32[]{:S(2)}) async-start(bf16[8,192,192]{2,1,0:T(8,128)(2,1)} %get-tuple-element.89), calls=%async_computation | async-start | bytes 1572864 | tf_op jit(solution)/shard_map/all_to_all | solution.py:1096
  98.9 124.7 %reduce-scatter.3.cloned.1.call-start = ((), (), s32[]{:S(2)}) async-start(), calls=%async_computation.6 | async-start | bytes 5308416 | tf_op jit(solution)/shard_map/reduce_scatter | solution.py:1112
  148.4 16.9 %all-to-all-start.1 = ((bf16[8,192,192]{2,1,0:T(8,128)(2,1)}), bf16[8,192,192]{2,1,0:T(8,128)(2,1)}, u32[]{:S(2)}, u32[]{:S(2)}) async-start(bf16[8,192,192]{2,1,0:T(8,128)(2,1)} %get-tuple-element.99), calls=%async_computation.1 | async-start | bytes 1572864 | tf_op jit(solution)/shard_map/all_to_all | solution.py:1111
  166.2 30.8 %collective-permute-start.12 = (bf16[2,96,1920]{2,1,0:T(8,128)(2,1)}, bf16[2,96,1920]{2,1,0:T(8,128)(2,1)}, u32[]{:S(2)}, u32[]{:S(2)}) collective-permute-start(bf16[2,96,1920]{2,1,0:T(8,128)(2,1)} %slice_bitcast_fusion.2), channel_id=1, source_target_pairs={{0,16},{4,20},{8,24},{12,28},{16,0},{20,4},{24,8},{28,12},{1,17},{... | collective-permute-start | bytes 2211848 | tf_op jit(solution)/shard_map/ppermute | solution.py:715
  167.7 30.9 %collective-permute-start.11 = (bf16[2,96,2048]{2,1,0:T(8,128)(2,1)}, bf16[2,96,2048]{2,1,0:T(8,128)(2,1)}, u32[]{:S(2)}, u32[]{:S(2)}) collective-permute-start(bf16[2,96,2048]{2,1,0:T(8,128)(2,1)} %slice_bitcast_fusion), channel_id=1, source_target_pairs={{0,8},{4,12},{8,0},{12,4},{16,24},{20,28},{24,16},{28,20},{1,9},{5... | collective-permute-start | bytes 2359304 | tf_op jit(solution)/shard_map/ppermute | solution.py:715
  193.6 30.0 %all-to-all-start.2 = ((bf16[32,32,384]{2,1,0:T(8,128)(2,1)}), bf16[32,32,384]{2,1,0:T(8,128)(2,1)}, u32[]{:S(2)}, u32[]{:S(2)}) async-start(bf16[32,32,384]{2,1,0:T(8,128)(2,1)} %get-tuple-element.123), calls=%async_computation.2 | async-start | bytes 1572864 | tf_op jit(solution)/shard_map/all_to_all | solution.py:1121
  197.0 72.8 %reduce-scatter.5.cloned.1.call-start = ((), (), s32[]{:S(2)}) async-start(), calls=%async_computation.7 | async-start | bytes 737280 | tf_op jit(solution)/shard_map/reduce_scatter | solution.py:1126
  200.0 22.4 %collective-permute-start.14 = (bf16[96,1920]{1,0:T(8,128)(2,1)S(1)}, bf16[96,1920]{1,0:T(8,128)(2,1)S(1)}, u32[]{:S(2)}, u32[]{:S(2)}) collective-permute-start(bf16[96,1920]{1,0:T(8,128)(2,1)S(1)} %slice_bitcast_fusion.6), channel_id=1, source_target_pairs={{0,8},{4,12},{8,0},{12,4},{16,24},{20,28},{24,16},{28,20},{1,9},{5... | collective-permute-start | bytes 1105928 | tf_op jit(solution)/shard_map/ppermute | solution.py:715
  201.5 21.9 %collective-permute-start.13 = (bf16[96,2048]{1,0:T(8,128)(2,1)S(1)}, bf16[96,2048]{1,0:T(8,128)(2,1)S(1)}, u32[]{:S(2)}, u32[]{:S(2)}) collective-permute-start(bf16[96,2048]{1,0:T(8,128)(2,1)S(1)} %slice_bitcast_fusion.4), channel_id=1, source_target_pairs={{0,16},{4,20},{8,24},{12,28},{16,0},{20,4},{24,8},{28,12},{1,17},{... | collective-permute-start | bytes 1179656 | tf_op jit(solution)/shard_map/ppermute | solution.py:715
  227.1 16.8 %collective-permute-start.16 = (bf16[2,192,768]{2,1,0:T(8,128)(2,1)S(1)}, bf16[2,192,768]{2,1,0:T(8,128)(2,1)}, u32[]{:S(2)}, u32[]{:S(2)}) collective-permute-start(bf16[2,192,768]{2,1,0:T(8,128)(2,1)S(1)} %slice.108), channel_id=1, source_target_pairs={{0,8},{4,12},{8,0},{12,4},{16,24},{20,28},{24,16},{28,20},{1,9},{5... | collective-permute-start | bytes 1769480 | tf_op jit(solution)/shard_map/ppermute | solution.py:715
  229.1 21.9 %collective-permute-start.17 = (bf16[2,24,3968]{2,1,0:T(8,128)(2,1)}, bf16[2,24,3968]{2,1,0:T(8,128)(2,1)S(1)}, u32[]{:S(2)}, u32[]{:S(2)}) collective-permute-start(bf16[2,24,3968]{2,1,0:T(8,128)(2,1)} %slice_bitcast_fusion.5), channel_id=1, source_target_pairs={{0,1},{1,0},{2,3},{3,2},{4,5},{5,4},{6,7},{7,6},{8,9},{9,8},{10,11... | collective-permute-start | bytes 1142792 | tf_op jit(solution)/shard_map/ppermute | solution.py:719
  230.9 30.1 %all-to-all-start.3 = ((bf16[32,32,192]{2,1,0:T(8,128)(2,1)}), bf16[32,32,192]{2,1,0:T(8,128)(2,1)}, u32[]{:S(2)}, u32[]{:S(2)}) async-start(bf16[32,32,192]{2,1,0:T(8,128)(2,1)} %get-tuple-element.134), calls=%async_computation.5 | async-start | bytes 1048576 | tf_op jit(solution)/shard_map/all_to_all | solution.py:1151
  251.1 15.7 %collective-permute-start.19 = (bf16[24,3968]{1,0:T(8,128)(2,1)S(1)}, bf16[24,3968]{1,0:T(8,128)(2,1)S(1)}, u32[]{:S(2)}, u32[]{:S(2)}) collective-permute-start(bf16[24,3968]{1,0:T(8,128)(2,1)S(1)} %slice_bitcast_fusion.7), channel_id=1, source_target_pairs={{0,2},{1,3},{2,0},{3,1},{4,6},{5,7},{6,4},{7,5},{8,10},{9,11},{10,... | collective-permute-start | bytes 571400 | tf_op jit(solution)/shard_map/ppermute | solution.py:719
  255.3 14.4 %collective-permute-start.18 = (bf16[192,768]{1,0:T(8,128)(2,1)S(1)}, bf16[192,768]{1,0:T(8,128)(2,1)S(1)}, u32[]{:S(2)}, u32[]{:S(2)}) collective-permute-start(bf16[192,768]{1,0:T(8,128)(2,1)S(1)} %fusion.8), channel_id=1, source_target_pairs={{0,16},{4,20},{8,24},{12,28},{16,0},{20,4},{24,8},{28,12},{1,17},{... | collective-permute-start | bytes 884744 | tf_op jit(solution)/shard_map/ppermute | solution.py:715
  (23 other events, 208.5 us)
Sparse Core Ops, SparseCore 0:
  47.8 51.7 all-gather.2
  148.5 74.0 reduce-scatter.2
  231.0 27.4 reduce-scatter.4

commit v3 on v2

--- a/solution.py
+++ b/solution.py
@@ -595,24 +595,40 @@
 
     def keys(j, unused):
         here = pl.ds(pl.multiple_of(j * TILE, TILE), TILE)
-        for i, h in enumerate(heads):
-            rows = slice(h * HEAD, (h + 1) * HEAD)
-            key = ka_refs[i][here, :]
-            val = va_refs[i][here, :]
-            key_t = kt_ref[rows, here]
-            dk = jnp.zeros((TILE, HEAD), jnp.float32)
-            dv = jnp.zeros((TILE, HEAD), jnp.float32)
-            for t in range(TILES):
-                span = slice(t * TILE, (t + 1) * TILE)
-                probs = jnp.exp(dot(key, qt_refs[i][:, span]))
-                grad_probs = dot(val, dot_t[i, :, span])
-                grad_scores = (probs * grad_probs).astype(jnp.bfloat16)
-                dv = dv + dot(probs.astype(jnp.bfloat16), don[i, span, :])
-                dk = dk + dot(grad_scores, qn_ref[span, rows])
-                dqt[i, :, span] = dqt[i, :, span] + dot(key_t, grad_scores)
+        steps = [(i, t) for i in range(n) for t in range(TILES)]
+        keys_of = [ka_refs[i][here, :] for i in range(n)]
+        vals_of = [va_refs[i][here, :] for i in range(n)]
+        turned = [kt_ref[h * HEAD : (h + 1) * HEAD, here] for h in heads]
+        dk = [jnp.zeros((HEAD, TILE), jnp.float32) for i in range(n)]
+        dv = [jnp.zeros((HEAD, TILE), jnp.float32) for i in range(n)]
+
+        def ahead(step):
+            i, t = step
+            span = slice(t * TILE, (t + 1) * TILE)
+            return dot(keys_of[i], qt_refs[i][:, span]), dot(vals_of[i], dot_t[i, :, span])
+
+        def behind(step, probs, grad_scores):
+            i, t = step
+            span = slice(t * TILE, (t + 1) * TILE)
+            dv[i] = dv[i] + dot_nt(dot_t[i, 0:HEAD, span], probs)
+            dk[i] = dk[i] + dot_nt(qt_refs[i][0:HEAD, span], grad_scores)
+            dqt[i, :, span] = dqt[i, :, span] + dot(turned[i], grad_scores)
+
+        ready, done = ahead(steps[0]), None
+        for at, step in enumerate(steps):
+            scores, grad_probs = ready
+            if at + 1 < len(steps):
+                ready = ahead(steps[at + 1])
+            probs = jnp.exp(scores)
+            grad_scores = (probs * grad_probs).astype(jnp.bfloat16)
+            if done is not None:
+                behind(*done)
+            done = step, probs.astype(jnp.bfloat16), grad_scores
+        behind(*done)
+        for i in range(n):
             at = i * GROUP
-            g_ref[here, at + HEAD : at + 2 * HEAD] = dk.astype(jnp.bfloat16)
-            g_ref[here, at + 2 * HEAD : at + GROUP] = dv.astype(jnp.bfloat16)
+            both = jnp.transpose(jnp.concatenate([dk[i], dv[i]], axis=0)).astype(jnp.bfloat16)
+            g_ref[here, at + HEAD : at + GROUP] = both
         return unused
 
     lax.fori_loop(0, TILES, keys, 0)
@@ -647,6 +663,36 @@
             part = (part + dot_nt(g_ref[here, :], w_ref[:, split:])).astype(jnp.bfloat16)
             back_ref[at] = part[:GROUP]
             back_ref[at + 1] = part[GROUP:]
+
+
+def assemble_kernel(*refs):
+    stay, near, mid, deep, deep_far, deep_next, deep_last = refs[:7]
+    up_ref, proj_ref, down_ref, vec_ref = refs[7:]
+    terms = (deep[0], deep_far[0], deep_next[0], deep_last[...])
+    deep_sum = sum(value.astype(jnp.float32) for value in terms)
+
+    def columns(start, stop):
+        parts = (stay[0, :, start:stop], near[0, :, start:stop], mid[:, start:stop])
+        return sum(value.astype(jnp.float32) for value in parts)
+
+    width = 4 * GROUP
+    up_ref[...] = columns(0, 4 * width)
+    proj_ref[...] = columns(4 * width, 5 * width)
+    vec_ref[...] = jnp.transpose(columns(5 * width, DOWN_AT))[0:16]
+    for k in range(4):
+        at, end = DOWN_AT + k * width, DOWN_AT + (k + 1) * width
+        parts = []
+        if at < RIGHT:
+            parts.append(columns(at, min(end, RIGHT)))
+        if end > RIGHT:
+            parts.append(deep_sum[:, max(at, RIGHT) - RIGHT : end - RIGHT])
+        down_ref[24 * k : 24 * (k + 1), :] = jnp.concatenate(parts, axis=1)
+
+
+def pack_kernel(*refs):
+    for m in range(3):
+        refs[3][m * PART[0] : (m + 1) * PART[0], :] = refs[m][: PART[0], :]
+        refs[4][m * PART[1] : (m + 1) * PART[1], :] = refs[m][PART[0] :, :]
 
 
 def collect_kernel(first_ref, last_ref, out_ref, bias_ref):
@@ -706,6 +752,18 @@
     return call(kernel, f"attend_back{heads[0]}", ins, outs, scratch, flops=10**10)
 
 
+def assemble(*ins):
+    width = 4 * GROUP
+    shapes = ((24, 4 * width), (24, width), (96, width), (16, 24))
+    outs = [(shape, WIDE) for shape in shapes]
+    return call(assemble_kernel, "assemble", ins, outs, scalars=0, flops=10**6)
+
+
+def pack(*ins):
+    outs = [((3 * rows, 384), LOW) for rows in PART]
+    return call(pack_kernel, "pack", ins, outs, scalars=0, flops=10**6)
+
+
 def collect(*ins):
     outs = [((24, 12 * GROUP), WIDE), ((2, 4 * GROUP), WIDE)]
     return call(collect_kernel, "collect", ins, outs, scalars=0, flops=10**6)
@@ -722,9 +780,12 @@
 FF_CUT = 384
 PROJ_ROWS = 48
 DOWN_ROWS = 96
-CUT_ROWS = 432
-COLUMNS = 3968
-LEFT = 2048
+PART = (240, 192)
+DOWN_AT = 3968
+COLUMNS = 7040
+LEFT = 2816
+RIGHT = 5632
+BACK_STEP = 768
 
 
 def norm(value):
@@ -771,10 +832,11 @@
 
 def dense_kernel(place, *refs):
     a_ref, tok_ref, cot_ref, keep_ref, vec_ref = refs[:5]
-    proj_own, up_own, down_own, gathered = refs[5:9]
-    block_ref, base_ref, ga_ref, rows_ref, keep_cols, give_cols = refs[9:15]
-    up, down, proj, slope, act_ref, att_ref, hid_ref, hid_t, gb_ref = refs[15:24]
-    sums_ref, upb_ref, turned, ordered, even, odd, branch, proj_sem, up_sem, down_sem = refs[24:]
+    proj_own, up_own, down_own = refs[5:8]
+    shared = refs[8:16]
+    block_ref, base_ref, ga_ref, keep_cols, give_cols = refs[16:21]
+    up, down, proj, slope, act_ref, att_ref, hid_ref, hid_t, gb_ref = refs[21:30]
+    sums_ref, upb_ref, turned, ordered, even, odd, branch, proj_sem, up_sem, down_sem = refs[30:]
     me, depth = place[0], place[1]
     width = 4 * GROUP
     proj_copies, up_copies, down_copies = [], [], []
@@ -787,34 +849,44 @@
     def owner_rows(m, size, at, rows):
         return pl.ds(pl.multiple_of((depth ^ m) * size + at, PROJ_ROWS), rows)
 
-    every = [(i, m) for i in range(8) for m in (1, 2, 3)]
+    def pieces(first, ways, rows):
+        for source, pair in zip(shared[first : first + 4], ways):
+            for i, k in enumerate(pair):
+                for m in (1, 2, 3):
+                    yield source, me ^ k, m, (3 * i + m - 1) * rows
+
+    ways = ((0, 2), (4, 6), (1, 3), (5, 7))
     copy(proj_copies, proj_own, proj.at[owner_rows(0, GROUP, 0, GROUP)], proj_sem)
-    for i, m in every:
+    for source, owner, m, at in pieces(0, ways, PART[0]):
         copy(
             proj_copies,
-            gathered.at[i, m - 1, pl.ds(CUT_ROWS - PROJ_ROWS, PROJ_ROWS)],
+            source.at[pl.ds(at + GROUP, PROJ_ROWS)],
             proj.at[
-                owner_rows(m, GROUP, (i // 2) * PROJ_ROWS, PROJ_ROWS),
-                pl.ds((i % 2) * FF_CUT, FF_CUT),
+                owner_rows(m, GROUP, (owner >> 1) * PROJ_ROWS, PROJ_ROWS),
+                pl.ds(pl.multiple_of((owner & 1) * FF_CUT, FF_CUT), FF_CUT),
             ],
             proj_sem,
         )
     copy(up_copies, up_own, up.at[owner_rows(0, GROUP, 0, GROUP)], up_sem)
-    for i, m in every:
+    for source, owner, m, at in pieces(0, ways, PART[0]):
         copy(
             up_copies,
-            gathered.at[i, m - 1, pl.ds(0, GROUP)],
-            up.at[owner_rows(m, GROUP, 0, GROUP), pl.ds(i * FF_CUT, FF_CUT)],
+            source.at[pl.ds(at, GROUP)],
+            up.at[
+                owner_rows(m, GROUP, 0, GROUP),
+                pl.ds(pl.multiple_of(owner * FF_CUT, FF_CUT), FF_CUT),
+            ],
             up_sem,
         )
     copy(down_copies, down_own, down.at[owner_rows(0, width, 0, width)], down_sem)
-    for i, m in every:
+    for source, owner, m, at in pieces(4, ((0, 4), (2, 6), (1, 5), (3, 7)), PART[1]):
         for side in range(2):
             copy(
                 down_copies,
-                gathered.at[i, m - 1, pl.ds(GROUP + side * DOWN_ROWS, DOWN_ROWS)],
+                source.at[pl.ds(at + side * DOWN_ROWS, DOWN_ROWS)],
                 down.at[
-                    owner_rows(m, width, i * DOWN_ROWS, DOWN_ROWS), pl.ds(side * FF_CUT, FF_CUT)
+                    owner_rows(m, width, owner * DOWN_ROWS, DOWN_ROWS),
+                    pl.ds(side * FF_CUT, FF_CUT),
                 ],
                 down_sem,
             )
@@ -913,16 +985,25 @@
     sums_ref[5:6, :] = add_up(grad)
 
     def backward(j, total):
-        cols = pl.ds(pl.multiple_of(j * FF_STEP, FF_STEP), FF_STEP)
+        cols = pl.ds(pl.multiple_of(j * BACK_STEP, BACK_STEP), BACK_STEP)
         grad_inner = (dot_nt(gb_ref[...], down[cols, :]) * slope[:, cols]).astype(jnp.bfloat16)
         out_columns(cols, grad_inner)
-        rows_ref[cols, :] = dot(flip(act_ref[:, cols]), gb_ref[...]).astype(
-            jnp.bfloat16
-        )
+        active = jnp.transpose(act_ref[:, cols].astype(jnp.float32))
+        for i in range(8):
+            for k in range(4):
+                away = ((i >> 2) ^ (me & 1)) * FF_CUT + k * 96 + ((i & 3) ^ depth) * 24
+                at = i * 96 + k * 24
+                ordered[pl.ds(pl.multiple_of(away, 8), 24), :] = active[at : at + 24]
+        part = dot(ordered[...].astype(jnp.bfloat16), gb_ref[...]).astype(jnp.bfloat16)
+        rows = pl.ds(pl.multiple_of((j ^ (me >> 1)) * 96, 96), 96)
+        for k in range(4):
+            lanes = slice(DOWN_AT + k * width, DOWN_AT + (k + 1) * width)
+            keep_cols[rows, lanes] = part[k * 96 : (k + 1) * 96]
+            give_cols[rows, lanes] = part[FF_CUT + k * 96 : FF_CUT + (k + 1) * 96]
         upb_ref[:, cols] = add_up(grad_inner.astype(jnp.float32))
         return total + dot_nt(grad_inner, up[:, cols])
 
-    grad_hidden = lax.fori_loop(0, 6, backward, grad_sum)
+    grad_hidden = lax.fori_loop(0, 4, backward, grad_sum)
     sums_ref[1:2, :] = add_up(grad_hidden * normal1)
     sums_ref[2:3, :] = add_up(grad_hidden)
     grad_mixed = norm_back(grad_hidden * gain1, normal1, scale1)
@@ -944,8 +1025,8 @@
         )
         vectors = jnp.where(lane == 6 + j, part, vectors)
     by_owner(vectors, turned)
-    keep_cols[:, 5 * width :] = turned[0:FF_CUT].astype(jnp.bfloat16)
-    give_cols[:, 5 * width :] = turned[FF_CUT:].astype(jnp.bfloat16)
+    keep_cols[:, 5 * width : DOWN_AT] = turned[0:FF_CUT].astype(jnp.bfloat16)
+    give_cols[:, 5 * width : DOWN_AT] = turned[FF_CUT:].astype(jnp.bfloat16)
     grad_att = dot_nt(grad_proj, proj[...]).astype(jnp.bfloat16)
     for mb in range(2):
         for j in range(4):
@@ -960,7 +1041,6 @@
         ((2, GROUP, width), LOW),
         ((rows, width), WIDE),
         ((8, GROUP, GROUP), LOW),
-        ((hidden, width), LOW),
         ((FF_CUT, COLUMNS), LOW),
         ((FF_CUT, COLUMNS), LOW),
     ]
@@ -985,7 +1065,7 @@
         pltpu.SemaphoreType.DMA((25,)),
         pltpu.SemaphoreType.DMA((49,)),
     ]
-    return call(dense_kernel, "dense", ins, outs, scratch, any_ins=4, flops=2 * 10**10)
+    return call(dense_kernel, "dense", ins, outs, scratch, any_ins=11, flops=2 * 10**10)
 
 
 def tie(*values):
@@ -996,23 +1076,38 @@
     return lax.dynamic_index_in_dim(value, at, axis, keepdims=False)
 
 
-def join(kept, given, send):
-    return (kept.astype(jnp.float32) + send(given).astype(jnp.float32)).astype(jnp.bfloat16)
-
-
-def over(bits):
-    return lambda value: from_ctx(value, bits)
-
-
-def scatter_plane(value):
-    value = value.reshape(2, 2, 96, COLUMNS)
-    left, right = value[..., :LEFT], value[..., LEFT:]
-    return join(left[:, 0], left[:, 1], over(2)), join(right[0], right[1], over(4))
-
-
-def scatter_plane_end(left, right):
-    left, right = join(left[0], left[1], over(4)), join(right[0], right[1], over(2))
-    return jnp.concatenate([left, right], axis=1).reshape(2, 2, 24, COLUMNS)
+def add(kept, came):
+    return (kept.astype(jnp.float32) + came.astype(jnp.float32)).astype(jnp.bfloat16)
+
+
+def split_plane(kept, came):
+    kept, came = [value.reshape(2, 2, 96, COLUMNS) for value in (kept, came)]
+    left, right = slice(0, LEFT), slice(LEFT, RIGHT)
+    deep = [value[..., RIGHT:].reshape(4, 2, 2, 24, -1) for value in (kept, came)]
+    return [
+        add(kept[:, 0, :, left], came[:, 0, :, left]),
+        add(kept[:, 1, :, left], came[:, 1, :, left]),
+        add(kept[0, :, :, right], came[0, :, :, right]),
+        add(kept[1, :, :, right], came[1, :, :, right]),
+        add(deep[0][:, :, 0], deep[1][:, :, 0]),
+        add(deep[0][:, :, 1], deep[1][:, :, 1]),
+    ]
+
+
+def end_plane(left, left_in, right, right_in):
+    pairs = [
+        (add(left[0], left_in[0]), from_ctx(add(left[1], left_in[1]), 4)),
+        (add(right[0], right_in[0]), from_ctx(add(right[1], right_in[1]), 2)),
+    ]
+
+    def part(at):
+        parts = []
+        for values in pairs:
+            kept, came = [value.reshape(2, 2, 24, -1)[:, at] for value in values]
+            parts.append(add(kept, came))
+        return jnp.concatenate(parts, axis=2)
+
+    return part
 
 
 def fast_on_device(
@@ -1071,16 +1166,26 @@
     proj_cut = lax.dynamic_slice(
         proj_weight, ((me >> 1) * PROJ_ROWS, (me & 1) * FF_CUT), (PROJ_ROWS, FF_CUT)
     )
-    cut = jnp.concatenate([up_cut, down_cut[:, :FF_CUT], down_cut[:, FF_CUT:], proj_cut], axis=0)
+    cut = jnp.concatenate([up_cut, proj_cut, down_cut[:, :FF_CUT], down_cut[:, FF_CUT:]], axis=0)
     came = from_ctx(take(marked, 1 - height, 0), 4)
     across = from_ctx(own, 2)
     cuts = [from_fsdp(cut, m) for m in (1, 2, 3)]
+    came, columns = tie(came, columns)
     corner = from_ctx(came, 2)
-    own, came, across, corner, columns, *cuts = tie(own, came, across, corner, columns, *cuts)
-    gathered = lax.all_gather(jnp.stack(cuts), "ctx", axis=0)
-    near, mid, far = [from_fsdp(columns, m) for m in (1, 2, 3)]
+    near = from_fsdp(columns, 1)
+    own, came, across, corner, near, columns, *cuts = tie(
+        own, came, across, corner, near, columns, *cuts
+    )
+    mid, far = [from_fsdp(columns, m) for m in (2, 3)]
     four = jnp.stack([own, came, across, corner])
     eight = from_ctx(four, 1)
+    some, rest = pack(*cuts)
+    some_too, rest_too = from_ctx(some, 2), from_ctx(rest, 4)
+    eight, some_too, rest_too = tie(eight, some_too, rest_too)
+    some = jnp.concatenate([some, some_too], axis=0)
+    rest = jnp.concatenate([rest, rest_too], axis=0)
+    shared = [some, from_ctx(some, 4), from_ctx(some, 1), None]
+    shared += [rest, from_ctx(rest, 2), from_ctx(rest, 1), None]
 
     documents = jnp.arange(NDOC, dtype=jnp.int32)
     keep_rows = jnp.sum(
@@ -1093,10 +1198,12 @@
     turned = list(qt)
     *made, o = attend((0, 1, 2), place, *turned, *ka, vt)
     qt, ot = made[:3], made[3:]
+    o, shared[1], shared[5] = tie(o, shared[1], shared[5])
+    shared[3], shared[7] = from_ctx(shared[1], 1), from_ctx(shared[5], 1)
     heads = lax.all_to_all(o, "ctx", 0, 0, tiled=True)
     xt, qn, kt, *va, by_head = turn(four, eight, *turned, *ka, vt, qkv_mine)
     heads, xt = tie(heads, xt)
-    block_rows, base, grad_heads, grad_down, kept, given = dense(
+    block_rows, base, grad_heads, kept, given = dense(
         place,
         heads,
         rows,
@@ -1106,42 +1213,57 @@
         proj_weight,
         up_weight,
         down_weight,
-        gathered,
+        *shared,
     )
     grad_o = lax.all_to_all(grad_heads, "ctx", 0, 0, tiled=True)
-    down_part = lax.psum_scatter(grad_down, "ctx", scatter_dimension=0, tiled=True)
     each = features // 32
-    both = join(kept, given, over(1))
-    grad_o, both = tie(grad_o, both)
-    left, right = scatter_plane(both)
+    came = from_ctx(given, 1)
+    grad_o, left, left_out, right, right_out, deep, deep_out = tie(
+        grad_o, *split_plane(kept, came)
+    )
+    left_in, right_in = from_ctx(left_out, 2), from_ctx(right_out, 4)
+    deep_in = from_fsdp(deep_out, 1)
     shared = (place, grad_o, kt, qn, xt)
     sent, grads = attend_back((0, 1), *shared, *ot[:2], *qt[:2], *ka[:2], *va[:2])
-    last, left, right, grads = tie(qt[2], left, right, grads)
-    both = scatter_plane_end(left, right)
+    last, left, left_in, right, right_in, deep, deep_in, grads = tie(
+        qt[2], left, left_in, right, right_in, deep, deep_in, grads
+    )
+    deep_far = from_fsdp(add(deep[:, 1], deep_in[:, 1]), 2)
+    deep = add(deep[:, 0], deep_in[:, 0])
+    part = end_plane(left, left_in, right, right_in)
     came_first = lax.all_to_all(sent, ("ctx", "fsdp"), 0, 0, tiled=True)
     sent, kept, given, _ = attend_back(
         (2,), *shared, ot[2], last, ka[2], va[2], grads, by_head
     )
-    given, came_first, down_part, both = tie(given, came_first, down_part, both)
-    out_down = lax.psum_scatter(down_part, "fsdp", scatter_dimension=0, tiled=True)
-
-    half = join(kept, given, over(1))
-    sent, half = tie(sent, half)
-    near = from_fsdp(both[:, 1], 1)
-    quarter = half[:2].astype(jnp.float32) + from_ctx(half[2:], 2).astype(jnp.float32)
-    quarter, near = tie(quarter, near)
-    both = join(both[:, 0], near, lambda value: value)
-    mid = from_fsdp(both[1], 2)
-
-    def columns_of(start, stop):
-        return both[0, :, start:stop].astype(jnp.float32) + mid[:, start:stop].astype(jnp.float32)
-
-    out_up, out_proj = columns_of(0, 4 * features), columns_of(4 * features, 5 * features)
-    vectors = columns_of(5 * features, 5 * features + 10).T
+    given, came_first = tie(given, came_first)
+
+    came = from_ctx(given, 1)
+    half_out = add(kept[2:], came[2:])
+    sent, half_out = tie(sent, half_out)
+    near = from_fsdp(part(1), 1)
+    half_in = from_ctx(half_out, 2)
+    deep_far, _ = tie(deep_far, half_out)
+    deep, deep_far = [value.reshape(2, 2, 24, -1) for value in (deep, deep_far)]
+    deep_next = from_ctx(add(deep[:, 1], deep_far[:, 1]), 2)
+    half_in, near = tie(half_in, near)
+    quarter = sum(value.astype(jnp.float32) for value in (kept[:2], came[:2], half_in))
+    stay = part(0)
+    mid = from_fsdp(add(stay[1], near[1]), 2)
+    deep_sum = [deep[:, 0], deep_far[:, 0], deep_next]
+    deep_out = sum(value[1].astype(jnp.float32) for value in deep_sum).astype(low)
+    deep_last = from_ctx(deep_out, 4)
+
+    out_up, out_proj, out_down, vectors = assemble(
+        stay,
+        near,
+        mid,
+        deep.reshape(4, 24, -1),
+        deep_far.reshape(4, 24, -1),
+        deep_next,
+        deep_last,
+    )
     mine = quarter[0]
     swapped = from_ctx(quarter[1].astype(low), 4).astype(jnp.float32)
-    swapped, out_down = tie(swapped, out_down)
-    out_down = out_down.astype(jnp.float32)
     first = height == 0
     back = jnp.concatenate(
         [jnp.where(first, mine, swapped), jnp.where(first, swapped, mine)], axis=0

time: 281 us -> 266 us (0.947)
  waiting for transfers between devices: 82.5 us -> 67.9 us
  between operations: 14.2 us -> 1.25 us
  starting transfers between devices: 40.6 us -> 48.7 us
  Pallas kernels: 111 us -> 104 us
  other arithmetic: 16.4 us -> 22.2 us
  local copies, waits for them, and re-layouts: 15.9 us -> 20.1 us
    ppermute x8 -> x10, waiting for transfers between devices: 44.1 us -> 30.5 us  [from_fsdp(): return lax.ppermute(value, 'fsdp', [(i, i ^ bits) for i in range(4)])]
    ppermute x12 -> x22, waiting for transfers between devices: 22.6 us -> 32.9 us  [from_ctx(): return lax.ppermute(value, 'ctx', [(i, i ^ bits) for i in range(8)])]
    ppermute x12 -> x22, starting transfers between devices: 10.9 us -> 19.9 us  [from_ctx(): return lax.ppermute(value, 'ctx', [(i, i ^ bits) for i in range(8)])]
    convert_element_type x9 -> x13, other arithmetic: 9.12 us -> 17.5 us  [the longest x12 15.9 us: add(): (kept.astype(jnp.float32) + came.astype(jnp.float32)).astype(jnp.bfloat16)]
    pallas_call x7 -> x9, Pallas kernels: 111 us -> 104 us  [call(): pl.pallas_call(kernel, name=name, out_shape=[jax.ShapeDtypeStruct(shape,...]
    all_to_all x1, waiting for transfers between devices: 5.72 us -> 0.01 us  [fast_on_device(): came_last = lax.all_to_all(sent, ('ctx', 'fsdp'), 0, 0, tiled=True)]
    all_to_all x1, waiting for transfers between devices: 5.36 us -> 0.01 us  [fast_on_device(): grad_o = lax.all_to_all(grad_heads, 'ctx', 0, 0, tiled=True)]
    ppermute x8 -> x10, starting transfers between devices: 14.8 us -> 12.8 us  [from_fsdp(): return lax.ppermute(value, 'fsdp', [(i, i ^ bits) for i in range(4)])]
  transfers between devices with their start and end apart: 27 -> 36, of which waited for: 15 -> 11; matrix products, arithmetic and copies ran while one was open for 8% -> 13% of each run, Pallas kernels for 27% -> 26%
where the time goes in v3:
time: 266 us; the launch traced here: 265 us
  Pallas kernels  104 us (39%)
  waiting for transfers between devices  67.9 us (26%)
  starting transfers between devices  48.7 us (18%)
  other arithmetic  22.2 us (8%)
  local copies, waits for them, and re-layouts  20.1 us (8%)
    pallas_call x9, Pallas kernels, call(): pl.pallas_call(kernel, name=name, out_shape=[jax.ShapeDtypeStruct(shape,...  104 us
    ppermute x22, waiting for transfers between devices, from_ctx(): return lax.ppermute(value, 'ctx', [(i, i ^ bits) for i in range(8)])  32.9 us
    ppermute x10, waiting for transfers between devices, from_fsdp(): return lax.ppermute(value, 'fsdp', [(i, i ^ bits) for i in range(4)])  30.5 us
    ppermute x22, starting transfers between devices, from_ctx(): return lax.ppermute(value, 'ctx', [(i, i ^ bits) for i in range(8)])  19.9 us
    convert_element_type x12, other arithmetic, add(): (kept.astype(jnp.float32) + came.astype(jnp.float32)).astype(jnp.bfloat16)  15.9 us
    ppermute x10, starting transfers between devices, from_fsdp(): return lax.ppermute(value, 'fsdp', [(i, i ^ bits) for i in range(4)])  12.8 us
    unnamed x73, local copies, waits for them, and re-layouts  5.6 us
  transfers between devices with their start and end apart: 36, of which 11 were waited for; matrix products, arithmetic and copies ran while one was open for 13% of the time, Pallas kernels for 26%

profile of v3, /device:TPU:0, one launch (start us, length us, event | category | flops | bytes accessed | tf_op | source)
XLA Modules:
  0.0 264.6 jit_solution(2679791854732465320)
XLA Ops:
  3.4 5.1 %collective-permute-start.6 = (bf16[432,384]{1,0:T(8,128)(2,1)S(1)}, bf16[432,384]{1,0:T(8,128)(2,1)S(1)}, u32[]{:S(2)}, u32[]{:S(2)}) collective-permute-start(bf16[432,384]{1,0:T(8,128)(2,1)S(1)} %pad_maximum_fusion.3), channel_id=1, source_target_pairs={{0,3},{1,2},{2,1},{3,0},{4,7},{5,6},{6,5},{7,4},{8,11},{9,10},{10,... | collective-permute-start | bytes 995336 | tf_op jit(solution)/shard_map/ppermute | solution.py:777
  14.4 3.6 %collective-permute-done = bf16[200,768]{1,0:T(8,128)(2,1)S(1)} collective-permute-done((bf16[200,768]{1,0:T(8,128)(2,1)S(1)}, bf16[200,768]{1,0:T(8,128)(2,1)S(1)}, u32[]{:S(2)}, u32[]{:S(2)}) %collective-permute-start) | collective-permute-done | bytes 307232 | tf_op jit(solution)/shard_map/ppermute | solution.py:773
  20.8 16.0 %collective-permute-done.5.refs_1_ = bf16[432,384]{1,0:T(8,128)(2,1)S(1)} collective-permute-done((bf16[432,384]{1,0:T(8,128)(2,1)S(1)}, bf16[432,384]{1,0:T(8,128)(2,1)S(1)}, u32[]{:S(2)}, u32[]{:S(2)}) %collective-permute-start.5) | collective-permute-done | bytes 331808 | tf_op jit(solution)/shard_map/ppermute | solution.py:777
  37.9 2.6 pack.1
  44.0 2.6 collective-permute-start.11
  48.6 5.5 %collective-permute-done.9 = bf16[576,384]{1,0:T(8,128)(2,1)S(1)} collective-permute-done((bf16[576,384]{1,0:T(8,128)(2,1)}, bf16[576,384]{1,0:T(8,128)(2,1)S(1)}, u32[]{:S(2)}, u32[]{:S(2)}) %collective-permute-start.9) | collective-permute-done | bytes 442400 | tf_op jit(solution)/shard_map/ppermute | solution.py:773
  59.4 8.9 %collective-permute-done.10.refs_4_ = bf16[200,576]{1,0:T(8,128)(2,1)S(1)} collective-permute-done((bf16[200,576]{1,0:T(8,128)(2,1)S(1)}, bf16[200,576]{1,0:T(8,128)(2,1)S(1)}, u32[]{:S(2)}, u32[]{:S(2)}) %collective-permute-start.10) | collective-permute-done | bytes 230432 | tf_op jit(solution)/shard_map/ppermute | solution.py:777
  69.0 6.1 %project.1 = (bf16[128,1536]{1,0:T(8,128)(2,1)}, bf16[128,1536]{1,0:T(8,128)(2,1)}, bf16[128,1536]{1,0:T(8,128)(2,1)}, bf16[1536,128]{1,0:T(8,128)(2,1)}, bf16[1...) custom-call(s32[10]{0:T(128)} %stack.26.place, ...), custom_call_target="tpu_custom_call" | custom-call | flops 5000000000 | bytes 10000000 | tf_op jit(solution)/shard_map/project/pallas_call | solution.py:416
  75.1 15.1 %attend0.1 = (bf16[128,1536]{1,0:T(8,128)(2,1)}, bf16[128,1536]{1,0:T(8,128)(2,1)}, bf16[128,1536]{1,0:T(8,128)(2,1)}, bf16[64,1536]{1,0:T(8,128)(2,1)}, bf16[64...) custom-call(s32[10]{0:T(128)} %stack.26.place, ...), custom_call_target="tpu_custom_call" | custom-call | flops 5000000000 | bytes 10000000 | tf_op jit(solution)/shard_map/attend0/pallas_call | solution.py:416
  90.9 3.7 %all-to-all-start = ((bf16[8,192,192]{2,1,0:T(8,128)(2,1)}), bf16[8,192,192]{2,1,0:T(8,128)(2,1)S(1)}, u32[]{:S(2)}, u32[]{:S(2)}) async-start(bf16[8,192,192]{2,1,0:T(8,128)(2,1)} %get-tuple-element.121), calls=%async_computation | async-start | bytes 1572864 | tf_op jit(solution)/shard_map/all_to_all | solution.py:1203
  95.7 6.9 %turn.1 = (bf16[768,1536]{1,0:T(8,128)(2,1)}, bf16[1536,192]{1,0:T(8,128)(2,1)}, bf16[192,1536]{1,0:T(8,128)(2,1)}, bf16[1536,128]{1,0:T(8,128)(2,1)}, bf16[1536...) custom-call(bf16[4,200,768]{2,1,0:T(8,128)(2,1)} %copy-done.2, ...), custom_call_target="tpu_custom_call" | custom-call | flops 5000000000 | bytes 10000000 | tf_op jit(solution)/shard_map/turn/pallas_call | solution.py:416
  102.5 4.5 %all-to-all-done.refs_0_ = bf16[8,192,192]{2,1,0:T(8,128)(2,1)S(1)} async-done(((bf16[8,192,192]{2,1,0:T(8,128)(2,1)}), bf16[8,192,192]{2,1,0:T(8,128)(2,1)S(1)}, u32[]{:S(2)}, u32[]{:S(2)}) %all-to-all-start) | async-done | bytes 589856 | tf_op jit(solution)/shard_map/all_to_all | solution.py:1203
  108.2 35.4 %dense.1 = (bf16[2,192,768]{2,1,0:T(8,128)(2,1)}, f32[384,768]{1,0:T(8,128)}, bf16[8,192,192]{2,1,0:T(8,128)(2,1)}, bf16[384,7040]{1,0:T(8,128)(2,1)}, bf16[384,7040]{1,0:T(8,128)(2,1)}) custom-call(s32[10]{0:T(128)} %stack.26.place, bf16[8,192,192]{2,1,0:T(8,128)(2,1)} %copy-done.10, bf16[2,192,768]{2,1,0:T(8,128)(2,1)} %bitcast.157, ...), custom_call_target="tpu_custom_call" | custom-call | flops 20000000000 | bytes 10000000 | tf_op jit(solution)/shard_map/dense/pallas_call | solution.py:416
  143.7 4.2 %all-to-all-start.1 = ((bf16[8,192,192]{2,1,0:T(8,128)(2,1)}), bf16[8,192,192]{2,1,0:T(8,128)(2,1)}, u32[]{:S(2)}, u32[]{:S(2)}) async-start(bf16[8,192,192]{2,1,0:T(8,128)(2,1)} %get-tuple-element.130), calls=%async_computation.1 | async-start | bytes 1572864 | tf_op jit(solution)/shard_map/all_to_all | solution.py:1218
  149.5 3.4 %collective-permute-done.18 = bf16[384,7040]{1,0:T(8,128)(2,1)} collective-permute-done((bf16[384,7040]{1,0:T(8,128)(2,1)}, bf16[384,7040]{1,0:T(8,128)(2,1)}, u32[]{:S(2)}, u32[]{:S(2)}) %collective-permute-start.18) | collective-permute-done | bytes 5406752 | tf_op jit(solution)/shard_map/ppermute | solution.py:773
  154.3 2.5 fusion.3
  158.3 3.2 %fusion.5 = (bf16[2,96,2816]{2,1,0:T(8,128)(2,1)}, bf16[2,96,2816]{2,1,0:T(8,128)(2,1)S(1)}) fusion(bf16[2,2,96,7040]{3,2,1,0:T(8,128)(2,1)} %bitcast.14, bf16[2,2,96,7040]{3,2,1,0:T(8,128)(2,1)S(1)} %bitcast.145), kind=kLoop, calls=%fused_computation.14 | loop fusion | flops 4325376 | bytes 6488064 | tf_op jit(solution)/shard_map/convert_element_type | solution.py:1080
  163.1 18.3 %attend_back0.1 = (bf16[32,32,384]{2,1,0:T(8,128)(2,1)}, bf16[1536,384]{1,0:T(8,128)(2,1)}) custom-call(s32[10]{0:T(128)} %stack.26.place, bf16[8,192,192]{2,1,0:T(8,128)(2,1)} %all-to-all-done.1.refs_0_, bf16[192,1536]{1,0:T(8,128)(2,1)} %get-tuple-element.134.refs_1_, bf16[1536,192]{1,0:T(8,128)(2,1)} %get-tuple-element.135.refs_2_, ...), custom_call_target="tpu_custom_call" | custom-call | flops 10000000000 | bytes 10000000 | tf_op jit(solution)/shard_map/attend_back0/pallas_call | solution.py:416
  181.4 4.6 %all-to-all-start.2 = ((bf16[32,32,384]{2,1,0:T(8,128)(2,1)}), bf16[32,32,384]{2,1,0:T(8,128)(2,1)}, u32[]{:S(2)}, u32[]{:S(2)}) async-start(bf16[32,32,384]{2,1,0:T(8,128)(2,1)} %get-tuple-element.158), calls=%async_computation.2 | async-start | bytes 1572864 | tf_op jit(solution)/shard_map/all_to_all | solution.py:1234
  196.4 15.5 %attend_back2.1 = (bf16[32,32,192]{2,1,0:T(8,128)(2,1)}, bf16[4,192,768]{2,1,0:T(8,128)(2,1)}, bf16[4,192,768]{2,1,0:T(8,128)(2,1)}, bf16[1536,192]{1,0:T(8,128)(2,1)}) custom-call(s32[10]{0:T(128)} %stack.26.place, bf16[8,192,192]{2,1,0:T(8,128)(2,1)} %all-to-all-done.1.refs_0_, bf16[192,1536]{1,0:T(8,128)(2,1)} %get-tuple-element.134.refs_1_, ...), custom_call_target="tpu_custom_call" | custom-call | flops 10000000000 | bytes 10000000 | tf_op jit(solution)/shard_map/attend_back2/pallas_call | solution.py:416
  221.4 3.5 %all-to-all-start.3 = ((bf16[32,32,192]{2,1,0:T(8,128)(2,1)}), bf16[32,32,192]{2,1,0:T(8,128)(2,1)}, u32[]{:S(2)}, u32[]{:S(2)}) async-start(bf16[32,32,192]{2,1,0:T(8,128)(2,1)} %get-tuple-element.168), calls=%async_computation.3 | async-start | bytes 1048576 | tf_op jit(solution)/shard_map/all_to_all | solution.py:1273
  224.9 16.8 %collective-permute-done.30.refs_5_ = bf16[2,24,1408]{2,1,0:T(8,128)(2,1)S(1)} collective-permute-done((bf16[2,24,1408]{2,1,0:T(8,128)(2,1)S(1)}, bf16[2,24,1408]{2,1,0:T(8,128)(2,1)S(1)}, u32[]{:S(2)}, u32[]{:S(2)}) %collective-permute-start.30) | collective-permute-done | bytes 135200 | tf_op jit(solution)/shard_map/ppermute | solution.py:773
  252.4 5.6 %collective-permute-done.28.refs_2_ = bf16[24,5632]{1,0:T(8,128)(2,1)} collective-permute-done((bf16[24,5632]{1,0:T(8,128)(2,1)}, bf16[24,5632]{1,0:T(8,128)(2,1)}, u32[]{:S(2)}, u32[]{:S(2)}) %collective-permute-start.28) | collective-permute-done | bytes 270368 | tf_op jit(solution)/shard_map/ppermute | solution.py:777
  258.0 2.4 assemble.1
  (179 shorter events, 67.5 us)
Async XLA Ops:
  3.4 17.4 %collective-permute-start.6 = (bf16[432,384]{1,0:T(8,128)(2,1)S(1)}, bf16[432,384]{1,0:T(8,128)(2,1)S(1)}, u32[]{:S(2)}, u32[]{:S(2)}) collective-permute-start(bf16[432,384]{1,0:T(8,128)(2,1)S(1)} %pad_maximum_fusion.3), channel_id=1, source_target_pairs={{0,3},{1,2},{2,1},{3,0},{4,7},{5,6},{6,5},{7,4},{8,11},{9,10},{10,... | collective-permute-start | bytes 995336 | tf_op jit(solution)/shard_map/ppermute | solution.py:777
  8.5 28.3 %collective-permute-start.5 = (bf16[432,384]{1,0:T(8,128)(2,1)S(1)}, bf16[432,384]{1,0:T(8,128)(2,1)S(1)}, u32[]{:S(2)}, u32[]{:S(2)}) collective-permute-start(bf16[432,384]{1,0:T(8,128)(2,1)S(1)} %pad_maximum_fusion.3), channel_id=1, source_target_pairs={{0,2},{1,3},{2,0},{3,1},{4,6},{5,7},{6,4},{7,5},{8,10},{9,11},{10,... | collective-permute-start | bytes 995336 | tf_op jit(solution)/shard_map/ppermute | solution.py:777
  8.6 28.3 %collective-permute-start.4 = (bf16[432,384]{1,0:T(8,128)(2,1)S(1)}, bf16[432,384]{1,0:T(8,128)(2,1)S(1)}, u32[]{:S(2)}, u32[]{:S(2)}) collective-permute-start(bf16[432,384]{1,0:T(8,128)(2,1)S(1)} %pad_maximum_fusion.3), channel_id=1, source_target_pairs={{0,1},{1,0},{2,3},{3,2},{4,5},{5,4},{6,7},{7,6},{8,9},{9,8},{10,11... | collective-permute-start | bytes 995336 | tf_op jit(solution)/shard_map/ppermute | solution.py:777
  17.9 18.9 %collective-permute-start.2 = (bf16[200,768]{1,0:T(8,128)(2,1)S(1)}, bf16[200,768]{1,0:T(8,128)(2,1)S(1)}, u32[]{:S(2)}, u32[]{:S(2)}) collective-permute-start(bf16[200,768]{1,0:T(8,128)(2,1)S(1)} %collective-permute-done), channel_id=1, source_target_pairs={{0,8},{4,12},{8,0},{12,4},{16,24},{20,28},{24,16},{28,20},{1,9},{5... | collective-permute-start | bytes 921608 | tf_op jit(solution)/shard_map/ppermute | solution.py:773
  19.5 17.4 %collective-permute-start.3 = (bf16[200,576]{1,0:T(8,128)(2,1)S(1)}, bf16[200,576]{1,0:T(8,128)(2,1)S(1)}, u32[]{:S(2)}, u32[]{:S(2)}) collective-permute-start(bf16[200,576]{1,0:T(8,128)(2,1)S(1)} %maximum_maximum_fusion.refs_2_), channel_id=1, source_target_pairs={{0,1},{1,0},{2,3},{3,2},{4,5},{5,4},{6,7},{7,6},{8,9},{9,8},{10,11... | collective-permute-start | bytes 691208 | tf_op jit(solution)/shard_map/ppermute | solution.py:777
  37.8 17.4 %collective-permute-start.7 = (bf16[4,200,768]{2,1,0:T(8,128)(2,1)S(1)}, bf16[4,200,768]{2,1,0:T(8,128)(2,1)}, u32[]{:S(2)}, u32[]{:S(2)}) collective-permute-start(bf16[4,200,768]{2,1,0:T(8,128)(2,1)S(1)} %pad_maximum_fusion.refs_0_), channel_id=1, source_target_pairs={{0,4},{4,0},{8,12},{12,8},{16,20},{20,16},{24,28},{28,24},{1,5},{5... | collective-permute-start | bytes 3686408 | tf_op jit(solution)/shard_map/ppermute | solution.py:773
  46.7 21.7 %collective-permute-start.10 = (bf16[200,576]{1,0:T(8,128)(2,1)S(1)}, bf16[200,576]{1,0:T(8,128)(2,1)S(1)}, u32[]{:S(2)}, u32[]{:S(2)}) collective-permute-start(bf16[200,576]{1,0:T(8,128)(2,1)S(1)} %maximum_maximum_fusion.refs_2_), channel_id=1, source_target_pairs={{0,2},{1,3},{2,0},{3,1},{4,6},{5,7},{6,4},{7,5},{8,10},{9,11},{10,... | collective-permute-start | bytes 691208 | tf_op jit(solution)/shard_map/ppermute | solution.py:777
  56.1 34.2 %collective-permute-start.12 = (bf16[1440,384]{1,0:T(8,128)(2,1)}, bf16[1440,384]{1,0:T(8,128)(2,1)}, u32[]{:S(2)}, u32[]{:S(2)}) collective-permute-start(bf16[1440,384]{1,0:T(8,128)(2,1)} %constant_dynamic-update-slice_fusion.refs_8_), channel_id=1, source_target_pairs={{0,16},{4,20},{8,24},{12,28},{16,0},{20,4},{24,8},{28,12},{1,17},{... | collective-permute-start | bytes 3317768 | tf_op jit(solution)/shard_map/ppermute | solution.py:773
  57.7 49.4 %collective-permute-start.14 = (bf16[1440,384]{1,0:T(8,128)(2,1)}, bf16[1440,384]{1,0:T(8,128)(2,1)}, u32[]{:S(2)}, u32[]{:S(2)}) collective-permute-start(bf16[1440,384]{1,0:T(8,128)(2,1)} %constant_dynamic-update-slice_fusion.refs_8_), channel_id=1, source_target_pairs={{0,4},{4,0},{8,12},{12,8},{16,20},{20,16},{24,28},{28,24},{1,5},{5... | collective-permute-start | bytes 3317768 | tf_op jit(solution)/shard_map/ppermute | solution.py:773
  57.8 32.4 %collective-permute-start.13 = (bf16[1152,384]{1,0:T(8,128)(2,1)S(1)}, bf16[1152,384]{1,0:T(8,128)(2,1)}, u32[]{:S(2)}, u32[]{:S(2)}) collective-permute-start(bf16[1152,384]{1,0:T(8,128)(2,1)S(1)} %constant_dynamic-update-slice_fusion.2.refs_12_), channel_id=1, source_target_pairs={{0,8},{4,12},{8,0},{12,4},{16,24},{20,28},{24,16},{28,20},{1,9},{5... | collective-permute-start | bytes 2654216 | tf_op jit(solution)/shard_map/ppermute | solution.py:773
  90.3 16.8 %collective-permute-start.15 = (bf16[1440,384]{1,0:T(8,128)(2,1)}, bf16[1440,384]{1,0:T(8,128)(2,1)S(1)}, u32[]{:S(2)}, u32[]{:S(2)}) collective-permute-start(bf16[1440,384]{1,0:T(8,128)(2,1)} %collective-permute-done.12.refs_9_), channel_id=1, source_target_pairs={{0,4},{4,0},{8,12},{12,8},{16,20},{20,16},{24,28},{28,24},{1,5},{5... | collective-permute-start | bytes 3317768 | tf_op jit(solution)/shard_map/ppermute | solution.py:773
  90.3 16.7 %collective-permute-start.16 = (bf16[1152,384]{1,0:T(8,128)(2,1)S(1)}, bf16[1152,384]{1,0:T(8,128)(2,1)}, u32[]{:S(2)}, u32[]{:S(2)}) collective-permute-start(bf16[1152,384]{1,0:T(8,128)(2,1)S(1)} %constant_dynamic-update-slice_fusion.2.refs_12_), channel_id=1, source_target_pairs={{0,4},{4,0},{8,12},{12,8},{16,20},{20,16},{24,28},{28,24},{1,5},{5... | collective-permute-start | bytes 2654216 | tf_op jit(solution)/shard_map/ppermute | solution.py:773
  143.7 18.1 %all-to-all-start.1 = ((bf16[8,192,192]{2,1,0:T(8,128)(2,1)}), bf16[8,192,192]{2,1,0:T(8,128)(2,1)}, u32[]{:S(2)}, u32[]{:S(2)}) async-start(bf16[8,192,192]{2,1,0:T(8,128)(2,1)} %get-tuple-element.130), calls=%async_computation.1 | async-start | bytes 1572864 | tf_op jit(solution)/shard_map/all_to_all | solution.py:1218
  161.9 26.3 %collective-permute-start.19 = (bf16[2,96,2816]{2,1,0:T(8,128)(2,1)}, bf16[2,96,2816]{2,1,0:T(8,128)(2,1)}, u32[]{:S(2)}, u32[]{:S(2)}) collective-permute-start(bf16[2,96,2816]{2,1,0:T(8,128)(2,1)} %fusion.3), channel_id=1, source_target_pairs={{0,8},{4,12},{8,0},{12,4},{16,24},{20,28},{24,16},{28,20},{1,9},{5... | collective-permute-start | bytes 3244040 | tf_op jit(solution)/shard_map/ppermute | solution.py:773
  162.4 25.9 %collective-permute-start.20 = (bf16[2,96,2816]{2,1,0:T(8,128)(2,1)}, bf16[2,96,2816]{2,1,0:T(8,128)(2,1)}, u32[]{:S(2)}, u32[]{:S(2)}) collective-permute-start(bf16[2,96,2816]{2,1,0:T(8,128)(2,1)} %get-tuple-element.142), channel_id=1, source_target_pairs={{0,16},{4,20},{8,24},{12,28},{16,0},{20,4},{24,8},{28,12},{1,17},{... | collective-permute-start | bytes 3244040 | tf_op jit(solution)/shard_map/ppermute | solution.py:773
  163.1 22.9 %collective-permute-start.21 = (bf16[4,2,24,1408]{3,2,0,1:T(8,128)(2,1)S(1)}, bf16[4,2,24,1408]{3,2,0,1:T(8,128)(2,1)}, u32[]{:S(2)}, u32[]{:S(2)}) collective-permute-start(bf16[4,2,24,1408]{3,2,0,1:T(8,128)(2,1)S(1)} %get-tuple-element.144), channel_id=1, source_target_pairs={{0,1},{1,0},{2,3},{3,2},{4,5},{5,4},{6,7},{7,6},{8,9},{9,8},{10,11... | collective-permute-start | bytes 1622024 | tf_op jit(solution)/shard_map/ppermute | solution.py:777
  181.4 30.5 %all-to-all-start.2 = ((bf16[32,32,384]{2,1,0:T(8,128)(2,1)}), bf16[32,32,384]{2,1,0:T(8,128)(2,1)}, u32[]{:S(2)}, u32[]{:S(2)}) async-start(bf16[32,32,384]{2,1,0:T(8,128)(2,1)} %get-tuple-element.158), calls=%async_computation.2 | async-start | bytes 1572864 | tf_op jit(solution)/shard_map/all_to_all | solution.py:1234
  189.6 29.3 %collective-permute-start.29 = (bf16[4,24,1408]{2,1,0:T(8,128)(2,1)S(1)}, bf16[4,24,1408]{2,1,0:T(8,128)(2,1)S(1)}, u32[]{:S(2)}, u32[]{:S(2)}) collective-permute-start(bf16[4,24,1408]{2,1,0:T(8,128)(2,1)S(1)} %get-tuple-element.234), channel_id=1, source_target_pairs={{0,2},{1,3},{2,0},{3,1},{4,6},{5,7},{6,4},{7,5},{8,10},{9,11},{10,... | collective-permute-start | bytes 811016 | tf_op jit(solution)/shard_map/ppermute | solution.py:777
  192.0 20.9 %collective-permute-start.24 = (bf16[96,2816]{1,0:T(8,128)(2,1)}, bf16[96,2816]{1,0:T(8,128)(2,1)}, u32[]{:S(2)}, u32[]{:S(2)}) collective-permute-start(bf16[96,2816]{1,0:T(8,128)(2,1)} %get-tuple-element.227), channel_id=1, source_target_pairs={{0,16},{4,20},{8,24},{12,28},{16,0},{20,4},{24,8},{28,12},{1,17},{... | collective-permute-start | bytes 1622024 | tf_op jit(solution)/shard_map/ppermute | solution.py:773
  194.9 19.1 %collective-permute-start.25 = (bf16[96,2816]{1,0:T(8,128)(2,1)S(1)}, bf16[96,2816]{1,0:T(8,128)(2,1)}, u32[]{:S(2)}, u32[]{:S(2)}) collective-permute-start(bf16[96,2816]{1,0:T(8,128)(2,1)S(1)} %get-tuple-element.229), channel_id=1, source_target_pairs={{0,8},{4,12},{8,0},{12,4},{16,24},{20,28},{24,16},{28,20},{1,9},{5... | collective-permute-start | bytes 1622024 | tf_op jit(solution)/shard_map/ppermute | solution.py:773
  216.2 27.7 %collective-permute-start.26 = (bf16[2,24,5632]{2,1,0:T(8,128)(2,1)}, bf16[2,24,5632]{2,1,0:T(8,128)(2,1)S(1)}, u32[]{:S(2)}, u32[]{:S(2)}) collective-permute-start(bf16[2,24,5632]{2,1,0:T(8,128)(2,1)} %pad_maximum_fusion.2), channel_id=1, source_target_pairs={{0,1},{1,0},{2,3},{3,2},{4,5},{5,4},{6,7},{7,6},{8,9},{9,8},{10,11... | collective-permute-start | bytes 1622024 | tf_op jit(solution)/shard_map/ppermute | solution.py:777
  218.4 25.4 %collective-permute-start.23 = (bf16[2,192,768]{2,1,0:T(8,128)(2,1)S(1)}, bf16[2,192,768]{2,1,0:T(8,128)(2,1)}, u32[]{:S(2)}, u32[]{:S(2)}) collective-permute-start(bf16[2,192,768]{2,1,0:T(8,128)(2,1)S(1)} %add_convert_fusion.4), channel_id=1, source_target_pairs={{0,8},{4,12},{8,0},{12,4},{16,24},{20,28},{24,16},{28,20},{1,9},{5... | collective-permute-start | bytes 1769480 | tf_op jit(solution)/shard_map/ppermute | solution.py:773
  218.9 22.8 %collective-permute-start.30 = (bf16[2,24,1408]{2,1,0:T(8,128)(2,1)S(1)}, bf16[2,24,1408]{2,1,0:T(8,128)(2,1)S(1)}, u32[]{:S(2)}, u32[]{:S(2)}) collective-permute-start(bf16[2,24,1408]{2,1,0:T(8,128)(2,1)S(1)} %fusion.19), channel_id=1, source_target_pairs={{0,8},{4,12},{8,0},{12,4},{16,24},{20,28},{24,16},{28,20},{1,9},{5... | collective-permute-start | bytes 405512 | tf_op jit(solution)/shard_map/ppermute | solution.py:773
  221.4 27.6 %all-to-all-start.3 = ((bf16[32,32,192]{2,1,0:T(8,128)(2,1)}), bf16[32,32,192]{2,1,0:T(8,128)(2,1)}, u32[]{:S(2)}, u32[]{:S(2)}) async-start(bf16[32,32,192]{2,1,0:T(8,128)(2,1)} %get-tuple-element.168), calls=%async_computation.3 | async-start | bytes 1048576 | tf_op jit(solution)/shard_map/all_to_all | solution.py:1273
  (47 other events, 446.4 us)
